TPU v7x, 32 devices: a whole 2x2x4 slice. The times are simulated.
32 devices in a mesh: win: 8 (over y, x, core), seq: 4 (over z).
Axes of the slice: x: 2, y: 2, z: 4, core: 2. Of those that a mesh axis runs over, the one named last changes fastest.
Arguments:
- tokens: bfloat16 [16, 512, 768], P('win', 'seq'), may hold values from -50 to 50, as said below
- cotangent: bfloat16 [16, 512, 768], P('win', 'seq'), may hold values from -6 to 6
- noise_times: float32 [16], P('win'), may hold values from 0 to 1
- cath_ids: int32 [16], P('win'), may hold values from 0 to 3
- chain_start: int32 [16], P('win'), may hold values from 128 to 512
- distance_bins: int32 [16, 512, 512], P('win', 'seq'), may hold values from 0 to 63
- class_table: bfloat16 [4, 768], replicated, may hold values from -6 to 6
- ada_weight: bfloat16 [768, 4608], replicated, may hold values from -0.21875 to 0.21875
- qkv_weight: bfloat16 [768, 2304], replicated, may hold values from -0.21875 to 0.21875
- out_weight: bfloat16 [768, 768], replicated, may hold values from -0.875 to 0.875
- pair_table: bfloat16 [128, 256], replicated, may hold values from -6 to 6
- pair_weight: bfloat16 [256, 12], replicated, may hold values from -0.375 to 0.375
- gate_weight: bfloat16 [768, 3072], replicated, may hold values from -0.21875 to 0.21875
- up_weight: bfloat16 [768, 3072], replicated, may hold values from -0.21875 to 0.21875
- down_weight: bfloat16 [3072, 768], replicated, may hold values from -0.21875 to 0.21875
Outputs:
- layer_out: bfloat16 [16, 512, 768], P('win', 'seq')
- grad_tokens: bfloat16 [16, 512, 768], P('win', 'seq')
- grad_class: float32 [3072], P(('win', 'seq'))
- grad_ada: float32 [3538944], P(('win', 'seq'))
- grad_qkv: float32 [1769472], P(('win', 'seq'))
- grad_out: float32 [589824], P(('win', 'seq'))
- grad_pair_table: float32 [32768], P(('win', 'seq'))
- grad_pair_weight: float32 [3072], P(('win', 'seq'))
- grad_gate: float32 [2359296], P(('win', 'seq'))
- grad_up: float32 [2359296], P(('win', 'seq'))
- grad_down: float32 [2359296], P(('win', 'seq'))
Inputs may be any that keep to these rules, and one draw needn't show every extreme that they name: tokens: activations with row and feature scales. `chain_start`: the value 512 means the window holds a single chain.
All inputs are finite; a program needn't handle non-finite values.
Results may differ from a plain program's by a relative error of at most 0.019.
Values may be sent and summed in bfloat16 or wider, within the bound.
A program may use at most 384 MiB of HBM per device.

v0:
```python
import math

import jax
import jax.numpy as jnp
from jax import lax
from jax.sharding import PartitionSpec as P

highest = lax.Precision.HIGHEST
norm_eps = 1e-06


def layer_norm_parts(values):
    centered = values - jnp.mean(values, axis=-1, keepdims=True)
    variance = jnp.mean(centered * centered, axis=-1, keepdims=True)
    inv_std = lax.rsqrt(variance + norm_eps)
    return (centered * inv_std, inv_std)


def norm_back(grad_normed, normed, inv_std):
    first_mean = jnp.mean(grad_normed, axis=-1, keepdims=True)
    second_mean = jnp.mean(grad_normed * normed, axis=-1, keepdims=True)
    return (grad_normed - first_mean - normed * second_mean) * inv_std


def time_embed(noise_times, model_width):
    half_width = model_width // 2
    frequency = jnp.exp(
        -math.log(10000.0) * jnp.arange(half_width).astype(jnp.float32) / half_width
    )
    angles = 1000.0 * noise_times[:, None] * frequency[None, :]
    return jnp.concatenate([jnp.sin(angles), jnp.cos(angles)], axis=-1)


def per_device(
    tokens,
    cotangent,
    noise_times,
    cath_ids,
    chain_start,
    distance_bins,
    class_table,
    ada_weight,
    qkv_weight,
    out_weight,
    pair_table,
    pair_weight,
    gate_weight,
    up_weight,
    down_weight,
):
    windows, row_count, model_width = tokens.shape
    length = distance_bins.shape[2]
    head_count = pair_weight.shape[1]
    head_size = model_width // head_count
    head_scale = 1.0 / math.sqrt(head_size)
    table_rows = pair_table.shape[0]
    bin_count = table_rows // 2
    classes = class_table.shape[0]
    total_rows = windows * row_count
    group_size = math.gcd(windows, max(1, 512 // row_count))
    groups = windows // group_size
    class_onehot = (cath_ids[:, None] == jnp.arange(classes, dtype=jnp.int32)[None, :]).astype(
        jnp.float32
    )
    pre_cond = jnp.dot(
        class_onehot, class_table.astype(jnp.float32), precision=highest
    ) + time_embed(noise_times, model_width)
    cond_sig = jax.nn.sigmoid(pre_cond)
    condition = pre_cond * cond_sig
    ada_float = ada_weight.astype(jnp.float32)
    modulation = jnp.dot(condition, ada_float, precision=highest).reshape(windows, 6, model_width)
    shift_attn = modulation[:, 0][:, None, :]
    scale_attn = modulation[:, 1][:, None, :]
    gate_attn = modulation[:, 2][:, None, :]
    shift_ffn = modulation[:, 3][:, None, :]
    scale_ffn = modulation[:, 4][:, None, :]
    gate_ffn = modulation[:, 5][:, None, :]
    table_bias = jnp.dot(pair_table, pair_weight, preferred_element_type=jnp.float32).astype(
        jnp.bfloat16
    )
    row_pos = lax.axis_index("seq") * row_count + jnp.arange(row_count, dtype=jnp.int32)
    key_pos = jnp.arange(length, dtype=jnp.int32)
    row_first = row_pos[None, :] < chain_start[:, None]
    key_first = key_pos[None, :] < chain_start[:, None]
    pair_index = distance_bins + bin_count * (
        row_first[:, :, None] == key_first[:, None, :]
    ).astype(jnp.int32)
    tokens_float = tokens.astype(jnp.float32)
    normed_x, inv_x = layer_norm_parts(tokens_float)
    attn_in = (
        (normed_x * (1.0 + scale_attn) + shift_attn)
        .astype(jnp.bfloat16)
        .reshape(total_rows, model_width)
    )
    qkv_values = jnp.dot(attn_in, qkv_weight, preferred_element_type=jnp.float32).astype(
        jnp.bfloat16
    )
    qkv_values = qkv_values.reshape(windows, row_count, 3 * model_width)
    queries = qkv_values[:, :, :model_width]
    keys_here = qkv_values[:, :, model_width : 2 * model_width]
    values_here = qkv_values[:, :, 2 * model_width :]
    keys_all, values_all = (
        lax.all_gather(keys_here, "seq", axis=1, tiled=True),
        lax.all_gather(values_here, "seq", axis=1, tiled=True),
    )

    def split_groups(array):
        return array.reshape((groups, group_size) + array.shape[1:])

    def head_split(array):
        return array.reshape(array.shape[:-1] + (head_count, head_size))

    def block_scores(query_block, key_block, index_block):
        pair_onehot = (
            index_block[:, None, :, :]
            == jnp.arange(table_rows, dtype=jnp.int32)[None, :, None, None]
        ).astype(jnp.bfloat16)
        raw_scores = jnp.einsum(
            "grhe,glhe->ghrl", query_block, key_block, preferred_element_type=jnp.float32
        )
        pair_bias = jnp.einsum(
            "kh,gkrl->ghrl", table_bias, pair_onehot, preferred_element_type=jnp.float32
        )
        return (raw_scores * head_scale + pair_bias, pair_onehot)

    def attend(block_items):
        query_block, key_block, value_block, index_block = block_items
        scores, _ = block_scores(query_block, key_block, index_block)
        row_max = jnp.max(scores, axis=-1, keepdims=True)
        exp_scores = jnp.exp(scores - row_max)
        exp_total = jnp.sum(exp_scores, axis=-1, keepdims=True)
        probs_low = (exp_scores / exp_total).astype(jnp.bfloat16)
        attn_mixed = jnp.einsum(
            "ghrl,glhe->grhe", probs_low, value_block, preferred_element_type=jnp.float32
        )
        return (attn_mixed.astype(jnp.bfloat16), (row_max + jnp.log(exp_total))[..., 0])

    query_groups = split_groups(head_split(queries))
    index_groups = split_groups(pair_index)
    attn_mixed, log_totals = lax.map(
        attend,
        (
            query_groups,
            split_groups(head_split(keys_all)),
            split_groups(head_split(values_all)),
            index_groups,
        ),
    )
    attn_mixed = attn_mixed.reshape(total_rows, model_width)
    attn_out = jnp.dot(attn_mixed, out_weight, preferred_element_type=jnp.float32).reshape(
        windows, row_count, model_width
    )
    gate_attn_sig = jax.nn.sigmoid(gate_attn)
    hidden_state = tokens_float + gate_attn_sig * attn_out
    normed_h, inv_h = layer_norm_parts(hidden_state)
    ffn_in = (
        (normed_h * (1.0 + scale_ffn) + shift_ffn)
        .astype(jnp.bfloat16)
        .reshape(total_rows, model_width)
    )
    gate_val = jnp.dot(ffn_in, gate_weight, preferred_element_type=jnp.float32)
    up_val = jnp.dot(ffn_in, up_weight, preferred_element_type=jnp.float32)
    gate_sig = jax.nn.sigmoid(gate_val)
    silu_gate = gate_val * gate_sig
    ffn_hidden = (silu_gate * up_val).astype(jnp.bfloat16)
    ffn_out = jnp.dot(ffn_hidden, down_weight, preferred_element_type=jnp.float32).reshape(
        windows, row_count, model_width
    )
    gate_ffn_sig = jax.nn.sigmoid(gate_ffn)
    layer_out = (hidden_state + gate_ffn_sig * ffn_out).astype(jnp.bfloat16)
    grad_layer = cotangent.astype(jnp.float32)
    grad_ffn = (gate_ffn_sig * grad_layer).astype(jnp.bfloat16).reshape(total_rows, model_width)
    grad_gate_ffn = jnp.sum(grad_layer * ffn_out * gate_ffn_sig * (1.0 - gate_ffn_sig), axis=1)
    grad_down = jnp.einsum("tf,td->fd", ffn_hidden, grad_ffn, preferred_element_type=jnp.float32)
    grad_hidden_ffn = jnp.einsum(
        "td,fd->tf", grad_ffn, down_weight, preferred_element_type=jnp.float32
    )
    grad_up_val = (grad_hidden_ffn * silu_gate).astype(jnp.bfloat16)
    grad_gate_val = (
        grad_hidden_ffn * up_val * gate_sig * (1.0 + gate_val * (1.0 - gate_sig))
    ).astype(jnp.bfloat16)
    grad_gate = jnp.einsum("td,tf->df", ffn_in, grad_gate_val, preferred_element_type=jnp.float32)
    grad_up = jnp.einsum("td,tf->df", ffn_in, grad_up_val, preferred_element_type=jnp.float32)
    grad_ffn_in = jnp.einsum(
        "tf,df->td", grad_gate_val, gate_weight, preferred_element_type=jnp.float32
    )
    grad_ffn_in = grad_ffn_in + jnp.einsum(
        "tf,df->td", grad_up_val, up_weight, preferred_element_type=jnp.float32
    )
    grad_ffn_in = grad_ffn_in.reshape(windows, row_count, model_width)
    grad_scale_ffn = jnp.sum(grad_ffn_in * normed_h, axis=1)
    grad_shift_ffn = jnp.sum(grad_ffn_in, axis=1)
    grad_hidden = grad_layer + norm_back(grad_ffn_in * (1.0 + scale_ffn), normed_h, inv_h)
    grad_attn_out = (
        (gate_attn_sig * grad_hidden).astype(jnp.bfloat16).reshape(total_rows, model_width)
    )
    grad_gate_attn = jnp.sum(grad_hidden * attn_out * gate_attn_sig * (1.0 - gate_attn_sig), axis=1)
    grad_out = jnp.einsum(
        "td,te->de", attn_mixed, grad_attn_out, preferred_element_type=jnp.float32
    )
    grad_mixed = jnp.einsum(
        "te,de->td", grad_attn_out, out_weight, preferred_element_type=jnp.float32
    ).astype(jnp.bfloat16)
    grad_mixed = grad_mixed.reshape(windows, row_count, model_width)
    keys_back, values_back = (
        lax.all_gather(keys_here, "seq", axis=1, tiled=True),
        lax.all_gather(values_here, "seq", axis=1, tiled=True),
    )

    def attend_back(block_items):
        query_block, key_block, value_block, index_block, log_block, grad_block = block_items
        scores, pair_onehot = block_scores(query_block, key_block, index_block)
        soft_probs = jnp.exp(scores - log_block[..., None])
        probs_low = soft_probs.astype(jnp.bfloat16)
        grad_probs = jnp.einsum(
            "grhe,glhe->ghrl", grad_block, value_block, preferred_element_type=jnp.float32
        )
        grad_scores = (
            soft_probs * (grad_probs - jnp.sum(soft_probs * grad_probs, axis=-1, keepdims=True))
        ).astype(jnp.bfloat16)
        grad_query = (
            jnp.einsum(
                "ghrl,glhe->grhe", grad_scores, key_block, preferred_element_type=jnp.float32
            )
            * head_scale
        )
        grad_key = (
            jnp.einsum(
                "ghrl,grhe->glhe", grad_scores, query_block, preferred_element_type=jnp.float32
            )
            * head_scale
        )
        grad_value = jnp.einsum(
            "ghrl,grhe->glhe", probs_low, grad_block, preferred_element_type=jnp.float32
        )
        grad_table = jnp.einsum(
            "ghrl,gkrl->kh", grad_scores, pair_onehot, preferred_element_type=jnp.float32
        )
        return (grad_query.astype(jnp.bfloat16), grad_key, grad_value, grad_table)

    grad_query, grad_key, grad_value, grad_table = lax.map(
        attend_back,
        (
            query_groups,
            split_groups(head_split(keys_back)),
            split_groups(head_split(values_back)),
            index_groups,
            log_totals,
            split_groups(head_split(grad_mixed)),
        ),
    )
    grad_table = jnp.sum(grad_table, axis=0)
    grad_key = grad_key.reshape(windows, length, model_width)
    grad_value = grad_value.reshape(windows, length, model_width)
    grad_keys, grad_values = (
        lax.psum_scatter(
            grad_key.astype(jnp.bfloat16), "seq", scatter_dimension=1, tiled=True
        ).astype(jnp.float32),
        lax.psum_scatter(
            grad_value.astype(jnp.bfloat16), "seq", scatter_dimension=1, tiled=True
        ).astype(jnp.float32),
    )
    grad_qkv_val = jnp.concatenate(
        [
            grad_query.reshape(windows, row_count, model_width),
            grad_keys.astype(jnp.bfloat16),
            grad_values.astype(jnp.bfloat16),
        ],
        axis=-1,
    )
    grad_qkv_val = grad_qkv_val.reshape(total_rows, 3 * model_width)
    grad_qkv = jnp.einsum("td,te->de", attn_in, grad_qkv_val, preferred_element_type=jnp.float32)
    grad_attn_in = jnp.einsum(
        "te,de->td", grad_qkv_val, qkv_weight, preferred_element_type=jnp.float32
    )
    grad_attn_in = grad_attn_in.reshape(windows, row_count, model_width)
    grad_scale_attn = jnp.sum(grad_attn_in * normed_x, axis=1)
    grad_shift_attn = jnp.sum(grad_attn_in, axis=1)
    grad_tokens = (
        grad_hidden + norm_back(grad_attn_in * (1.0 + scale_attn), normed_x, inv_x)
    ).astype(jnp.bfloat16)
    grad_mod = jnp.stack(
        [
            grad_shift_attn,
            grad_scale_attn,
            grad_gate_attn,
            grad_shift_ffn,
            grad_scale_ffn,
            grad_gate_ffn,
        ],
        axis=1,
    )
    grad_mod = grad_mod.reshape(windows, 6 * model_width)
    grad_cond = jnp.dot(grad_mod, ada_float.T, precision=highest)
    grad_pre = grad_cond * cond_sig * (1.0 + pre_cond * (1.0 - cond_sig))
    grad_class = jnp.dot(class_onehot.T, grad_pre, precision=highest)
    grad_pair_weight = jnp.dot(pair_table.astype(jnp.float32).T, grad_table, precision=highest)
    grad_pair_table = jnp.dot(grad_table, pair_weight.astype(jnp.float32).T, precision=highest)
    grad_ada = jnp.dot(condition.T, grad_mod, precision=highest)
    win_count = lax.axis_size("win")
    seq_count = lax.axis_size("seq")
    flats = [
        grad_class.reshape(-1),
        grad_ada.reshape(-1),
        grad_qkv.reshape(-1),
        grad_out.reshape(-1),
        grad_pair_table.reshape(-1),
        grad_pair_weight.reshape(-1),
        grad_gate.reshape(-1),
        grad_up.reshape(-1),
        grad_down.reshape(-1),
    ]
    shares = [flat.shape[0] // (win_count * seq_count) for flat in flats]
    packed = jnp.concatenate([flat.reshape(win_count, seq_count, -1) for flat in flats], axis=-1)
    all_terms = lax.all_to_all(
        lax.all_to_all(packed.astype(jnp.bfloat16), "win", split_axis=0, concat_axis=0, tiled=True),
        "seq",
        split_axis=1,
        concat_axis=1,
        tiled=True,
    ).astype(packed.dtype)
    owned = jnp.sum(all_terms, axis=(0, 1))
    pieces = []
    offset = 0
    for share in shares:
        pieces.append(owned[offset : offset + share])
        offset = offset + share
    return (
        layer_out,
        grad_tokens,
        pieces[0],
        pieces[1],
        pieces[2],
        pieces[3],
        pieces[4],
        pieces[5],
        pieces[6],
        pieces[7],
        pieces[8],
    )


def solution(mesh):
    placed = (
        P("win", "seq", None),
        P("win", "seq", None),
        P("win"),
        P("win"),
        P("win"),
        P("win", "seq", None),
        P(),
        P(),
        P(),
        P(),
        P(),
        P(),
        P(),
        P(),
        P(),
    )
    return jax.shard_map(
        per_device,
        mesh=mesh,
        in_specs=placed,
        out_specs=(
            P("win", "seq", None),
            P("win", "seq", None),
            P(("win", "seq")),
            P(("win", "seq")),
            P(("win", "seq")),
            P(("win", "seq")),
            P(("win", "seq")),
            P(("win", "seq")),
            P(("win", "seq")),
            P(("win", "seq")),
            P(("win", "seq")),
        ),
        check_vma=False,
    )
```

profile of v0, /device:TPU:0, one launch (start us, length us, event | category | flops | bytes accessed | tf_op | source)
XLA Modules:
  0.0 1485.0 jit_solution(1629381651813120850)
XLA Ops:
  9.8 6.5 fusion.62
  17.6 1.7 broadcast_subtract_fusion
  29.2 2.0 select_add_fusion
  31.2 2.0 copy.85
  33.3 14.8 fusion.1
  48.0 9.3 copy.86
  57.3 1.9 copy.83
  61.8 1.8 fusion.39
  63.6 2.2 all-gather.5.cloned.1.call-done
  65.8 2.6 copy.84
  68.4 4.5 fusion.70
  73.0 2.6 copy-done.2
  75.6 1.5 fusion.4
  77.7 26.2 %all-gather.3.cloned.1.call-done = bf16[2,512,768]{2,1,0:T(8,128)(2,1)} async-done(((bf16[2,128,768]{2,1,0:T(8,128)(2,1)}), bf16[2,512,768]{2,1,0:T(8,128)(2,1)}) %all-gather.3.cloned.1.call-update) | async-done | bytes 1572880 | tf_op jit(solution)/shard_map/all_gather | solution.py:104
  103.8 2.6 copy.82
  106.5 5.1 fusion.17
  112.7 3.1 fusion.71
  115.9 3.1 fusion.72
  119.0 4.6 multiply_convert_fusion.2
  125.3 1.5 fusion.43
  127.8 1.5 fusion.73
  129.3 2.0 multiply_reduce_fusion.1
  134.2 1.9 copy.88
  136.1 1.8 squeeze.37
  138.0 5.4 fusion.13
  143.3 2.6 copy.92
  146.0 5.5 multiply_reduce_fusion
  151.5 3.8 multiply_convert_fusion
  155.3 1.6 copy-done.3
  157.0 1.7 multiply_convert_fusion.1
  158.7 2.6 copy.90
  161.3 7.7 copy.96
  169.0 4.3 fusion.16
  173.3 1.9 copy.93
  176.6 2.5 convolution_convert_fusion.5
  179.1 2.8 reshape_reshape.44
  181.9 11.5 fusion.21
  194.4 1.5 reshape_reshape.45
  197.6 1.6 reshape_reshape.46
  199.2 5.2 convolution_convert_fusion.3
  204.4 8.2 reshape_reshape.47
  212.6 5.2 convolution_convert_fusion.2
  217.8 8.3 reshape_reshape.48
  226.1 5.2 convolution_convert_fusion.1
  231.3 8.6 reshape_reshape.49
  240.0 4.0 fusion.37
  244.1 7.8 fusion.22
  251.9 13.2 convolution_convert_fusion
  265.5 10.3 reshape_reshape.42
  275.7 2.9 bitcast_convert_fusion
  278.7 5.8 reshape_reshape.43
  285.9 69.4 %dynamic-update-slice.1 = bf16[8,4,406720]{2,1,0:T(4,128)(2,1)} dynamic-update-slice(bf16[8,4,406720]{2,1,0:T(4,128)(2,1)} %dynamic-update-slice, bf16[8,4,110592]{2,1,0:T(4,128)(2,1)} %reshape_reshape.42, s32[]{} %constant.92, s32[]{} %constant.92, s32[]{} %constant.93) | dynamic-update-slice | bytes 14155780
  355.3 33.3 %dynamic-update-slice.2 = bf16[8,4,406720]{2,1,0:T(4,128)(2,1)} dynamic-update-slice(bf16[8,4,406720]{2,1,0:T(4,128)(2,1)} %dynamic-update-slice.1, bf16[8,4,55296]{2,1,0:T(4,128)(2,1)S(1)} %reshape_reshape.43, s32[]{} %constant.92, s32[]{} %constant.92, s32[]{} %constant.94) | dynamic-update-slice | bytes 7077892
  388.7 15.5 %dynamic-update-slice.3 = bf16[8,4,406720]{2,1,0:T(4,128)(2,1)} dynamic-update-slice(bf16[8,4,406720]{2,1,0:T(4,128)(2,1)} %dynamic-update-slice.2, bf16[8,4,18432]{2,1,0:T(4,128)(2,1)} %reshape_reshape.44, s32[]{} %constant.92, s32[]{} %constant.92, s32[]{} %constant.95) | dynamic-update-slice | bytes 2359300
  404.1 2.9 dynamic-update-slice.4
  407.1 2.5 dynamic-update-slice.5
  409.6 49.8 %dynamic-update-slice.6 = bf16[8,4,406720]{2,1,0:T(4,128)(2,1)} dynamic-update-slice(bf16[8,4,406720]{2,1,0:T(4,128)(2,1)} %dynamic-update-slice.5, bf16[8,4,73728]{2,1,0:T(4,128)(2,1)} %reshape_reshape.47, s32[]{} %constant.92, s32[]{} %constant.92, s32[]{} %constant.98) | dynamic-update-slice | bytes 9437188
  459.3 49.8 %dynamic-update-slice.7 = bf16[8,4,406720]{2,1,0:T(4,128)(2,1)} dynamic-update-slice(bf16[8,4,406720]{2,1,0:T(4,128)(2,1)} %dynamic-update-slice.6, bf16[8,4,73728]{2,1,0:T(4,128)(2,1)} %reshape_reshape.48, s32[]{} %constant.92, s32[]{} %constant.92, s32[]{} %constant.99) | dynamic-update-slice | bytes 9437188
  509.1 49.5 %dynamic-update-slice.8 = bf16[8,4,406720]{2,1,0:T(4,128)(2,1)} dynamic-update-slice(bf16[8,4,406720]{2,1,0:T(4,128)(2,1)} %dynamic-update-slice.7, bf16[8,4,73728]{2,1,0:T(4,128)(2,1)} %reshape_reshape.49, s32[]{} %constant.92, s32[]{} %constant.92, s32[]{} %constant.100) | dynamic-update-slice | bytes 9437188 | tf_op jit(solution)/shard_map/concatenate | solution.py:314
  558.6 292.9 %all_to_all.10 = bf16[8,4,406720]{2,1,0:T(4,128)(2,1)} all-to-all(bf16[8,4,406720]{2,1,0:T(4,128)(2,1)} %dynamic-update-slice.8), channel_id=1, replica_groups=mesh['win'=8,'seq'=4] {'win'}, dimensions={0} | all-to-all | bytes 52060160 | tf_op jit(solution)/shard_map/all_to_all | solution.py:316
  851.5 18.1 %copy.98 = bf16[8,4,406720]{2,0,1:T(8,128)(2,1)} copy(bf16[8,4,406720]{2,1,0:T(4,128)(2,1)} %all_to_all.10) | data formatting | bytes 52060160 | tf_op jit(solution)/shard_map/all_to_all | solution.py:316
  869.6 8.7 all-to-all-start.1
  879.5 560.2 %all-to-all-done.1 = bf16[8,4,406720]{2,0,1:T(8,128)(2,1)} async-done(((bf16[8,4,406720]{2,0,1:T(8,128)(2,1)}), bf16[8,4,406720]{2,0,1:T(8,128)(2,1)}, u32[]{:S(2)}, u32[]{:S(2)}) %all-to-all-start.1) | async-done | bytes 26030112 | tf_op jit(solution)/shard_map/all_to_all | solution.py:315
  1439.7 33.6 %convert_reduce_fusion = f32[406720]{0:T(1024)S(1)} fusion(bf16[8,4,406720]{2,0,1:T(8,128)(2,1)} %all-to-all-done.1), kind=kLoop, calls=%fused_computation.3 | loop fusion | flops 25623360 | bytes 27656960 | tf_op jit(solution)/shard_map/reduce_sum | solution.py:322
  (177 shorter events, 35.6 us)
Async XLA Ops:
  7.2 16.5 %copy-start = (bf16[768,2304]{1,0:T(8,128)(2,1)S(1)}, bf16[768,2304]{1,0:T(8,128)(2,1)}, u32[]{:S(2)}) copy-start(bf16[768,2304]{1,0:T(8,128)(2,1)} %param.23) | copy-start | bytes 10616836
  7.2 58.6 %all-gather.5.cloned.1.call-start = ((), (), s32[]{:S(2)}) async-start(), calls=%async_computation.5 | async-start | bytes 1966080 | tf_op jit(solution)/shard_map/all_gather | solution.py:103
  9.2 0.6 copy-start.26
  20.5 3.2 copy-start.40
  21.8 1.9 copy-start.42
  22.4 1.3 copy-start.30
  22.4 39.4 %copy-start.28 = (f32[2,768]{1,0:T(2,128)}, f32[2,768]{1,0:T(2,128)S(1)}, u32[]{:S(2)}) copy-start(f32[2,768]{1,0:T(2,128)S(1)} %get-tuple-element.119) | copy-start | bytes 18436
  23.7 2.2 copy-start.19
  25.9 78.0 %all-gather.3.cloned.1.call-start = ((), (), s32[]{:S(2)}) async-start(), calls=%async_computation.4 | async-start | bytes 1966080 | tf_op jit(solution)/shard_map/all_gather | solution.py:104
  26.6 213.3 %reduce-scatter.5.cloned.1.call-start = ((), (), s32[]{:S(2)}) async-start(), calls=%async_computation.7 | async-start | bytes 1966080 | tf_op jit(solution)/shard_map/reduce_scatter | solution.py:259
  72.9 2.6 copy-start.2
  72.9 4.1 copy-start.23
  77.0 0.6 copy-start.25
  106.4 6.2 slice-start.2
  106.4 5.1 copy-start.4
  106.4 5.1 copy-start.10
  106.4 5.1 copy-start.24
  106.4 6.2 slice-start.3
  111.5 4.3 copy-start.17
  111.5 0.9 copy-start.22
  111.5 0.9 copy-start.37
  112.2 3.7 slice-start
  112.7 3.2 copy-start.9
  112.7 3.1 slice-start.1
  112.7 6.3 slice-start.4
  115.9 3.2 copy-start.14
  115.9 3.2 slice-start.5
  123.7 1.5 copy-start.15
  123.7 1.6 copy-start.8
  123.7 4.0 copy-start.11
  127.7 1.5 copy-start.16
  127.7 1.5 copy-start.29
  127.7 1.5 copy-start.35
  127.7 1.5 copy-start.36
  131.2 0.9 copy-start.6
  132.2 0.8 copy-start.13
  145.9 94.0 %reduce-scatter.3.cloned.1.call-start = ((), (), s32[]{:S(2)}) async-start(), calls=%async_computation.6 | async-start | bytes 1966080 | tf_op jit(solution)/shard_map/reduce_scatter | solution.py:256
  151.5 5.5 copy-start.12
  155.3 1.6 copy-start.3
  181.9 11.5 copy-start.44
  231.3 8.7 copy-start.31
  239.9 4.2 copy-start.27
  239.9 4.1 copy-start.34
  239.9 4.1 copy-start.39
  239.9 4.1 copy-start.38
  240.0 4.1 copy-start.33
  251.9 13.2 copy-start.49
  265.4 10.3 copy-start.20
  265.4 10.3 copy-start.21
  265.4 10.3 copy-start.47
  265.5 10.3 copy-start.48
  355.3 51.7 %copy-start.32 = (bf16[8,4,96]{2,1,0:T(4,128)(2,1)S(1)}, bf16[8,4,96]{2,1,0:T(4,128)(2,1)}, u32[]{:S(2)}) copy-start(bf16[8,4,96]{2,1,0:T(4,128)(2,1)} %reshape_reshape.46) | copy-start | bytes 18436
  869.6 8.8 copy-start.46
  869.6 8.8 copy-start.45
  869.6 8.8 copy-start.5
  869.6 8.8 copy-start.7
  869.6 8.8 copy-start.18
  869.6 8.8 copy-start.41
  869.6 8.8 copy-start.43
  869.6 570.0 %all-to-all-start.1 = ((bf16[8,4,406720]{2,0,1:T(8,128)(2,1)}), bf16[8,4,406720]{2,0,1:T(8,128)(2,1)}, u32[]{:S(2)}, u32[]{:S(2)}) async-start(bf16[8,4,406720]{2,0,1:T(8,128)(2,1)} %copy.98), calls=%async_computation.3 | async-start | bytes 52068352 | tf_op jit(solution)/shard_map/all_to_all | solution.py:315
  1439.7 38.6 %copy-start.1 = (bf16[768,2304]{1,0:T(8,128)(2,1)S(1)}, bf16[768,2304]{1,0:T(8,128)(2,1)}, u32[]{:S(2)}) copy-start(bf16[768,2304]{1,0:T(8,128)(2,1)} %param.23) | copy-start | bytes 10616836
Sparse Core Ops, SparseCore 0:
  26.0 39.7 all-gather.4
  67.9 35.8 all-gather.2
  146.0 34.2 reduce-scatter.4
  182.5 34.2 reduce-scatter.2
where the time goes:
time: 1510 us; the launch traced here: 1480 us
  waiting for transfers between devices  589 us (39%)
  local copies, waits for them, and re-layouts  397 us (26%)
  blocking collectives  293 us (19%)
  matrix products  127 us (8%)
  other arithmetic  55.5 us (4%)
    all_to_all x1, waiting for transfers between devices, per_device(): lax.all_to_all(lax.all_to_all(packed.astype(jnp.bfloat16), 'win', split_a...  560 us
    all_to_all x1, blocking collectives, per_device(): lax.all_to_all(packed.astype(jnp.bfloat16), 'win', split_axis=0, concat_a...  293 us
    unnamed x129, local copies, waits for them, and re-layouts  235 us
    concatenate x1, local copies, waits for them, and re-layouts, per_device(): jnp.concatenate([flat.reshape(win_count, seq_count, -1) for flat in flats...  49.5 us
    another operation x9, local copies, waits for them, and re-layouts, per_device(): flat.reshape(win_count, seq_count, -1)  47.2 us
    reduce_sum x1, other arithmetic, per_device(): owned = jnp.sum(all_terms, axis=(0, 1))  33.6 us
  transfers between devices with their start and end apart: 5, of which 3 were waited for; matrix products, arithmetic and copies ran while one was open for 9% of the time, Pallas kernels for 0%

commit v1 on v0

v1 whole, which is shorter than its diff:
```python
import math

import jax
import jax.numpy as jnp
from jax import lax
from jax.sharding import PartitionSpec as P

highest = lax.Precision.HIGHEST
norm_eps = 1e-06
f32 = jnp.float32
bf16 = jnp.bfloat16


def layer_norm_parts(values):
    centered = values - jnp.mean(values, axis=-1, keepdims=True)
    variance = jnp.mean(centered * centered, axis=-1, keepdims=True)
    inv_std = lax.rsqrt(variance + norm_eps)
    return (centered * inv_std, inv_std)


def norm_back(grad_normed, normed, inv_std):
    first_mean = jnp.mean(grad_normed, axis=-1, keepdims=True)
    second_mean = jnp.mean(grad_normed * normed, axis=-1, keepdims=True)
    return (grad_normed - first_mean - normed * second_mean) * inv_std


def time_embed(noise_times, model_width):
    half_width = model_width // 2
    frequency = jnp.exp(
        -math.log(10000.0) * jnp.arange(half_width).astype(f32) / half_width
    )
    angles = 1000.0 * noise_times[:, None] * frequency[None, :]
    return jnp.concatenate([jnp.sin(angles), jnp.cos(angles)], axis=-1)


def dot(a, b):
    return jnp.dot(a, b, preferred_element_type=f32)


def dot_nt(a, b):
    return lax.dot_general(a, b, (((1,), (1,)), ((), ())), preferred_element_type=f32)


def dot_tn(a, b):
    return lax.dot_general(a, b, (((0,), (0,)), ((), ())), preferred_element_type=f32)


def halving_steps(flip):
    win_bits = int(math.log2(lax.axis_size("win")))
    seq_bits = int(math.log2(lax.axis_size("seq")))
    far = list(range(1, win_bits))
    if flip:
        far = far[::-1]
    return [("win", bit) for bit in [0] + far] + [("seq", bit) for bit in range(seq_bits)]


def exchange(values, axis, bit):
    size = lax.axis_size(axis)
    return lax.ppermute(values, axis, [(i, i ^ (1 << bit)) for i in range(size)])


def reduce_owned(grad, flip):
    win_bits = int(math.log2(lax.axis_size("win")))
    seq_bits = int(math.log2(lax.axis_size("seq")))
    columns = grad.shape[1]
    names = [("win", bit) for bit in range(win_bits)[::-1]] + [("seq", bit) for bit in range(seq_bits)[::-1]]
    current = grad
    for step in halving_steps(flip):
        at = names.index(step)
        before = 2**at
        rows = current.shape[0]
        view = current.reshape(before, 2, rows // (2 * before), columns)
        mine = (lax.axis_index(step[0]) >> step[1]) & 1
        send = lax.dynamic_index_in_dim(view, 1 - mine, 1, keepdims=False).astype(bf16)
        got = exchange(send.reshape(rows // 2, columns), *step)
        keep = lax.dynamic_index_in_dim(view, mine, 1, keepdims=False).reshape(rows // 2, columns)
        current = keep.astype(f32) + got.astype(f32)
        names.remove(step)
        if names:
            current = current.astype(bf16)
    return current


def per_device(
    tokens,
    cotangent,
    noise_times,
    cath_ids,
    chain_start,
    distance_bins,
    class_table,
    ada_weight,
    qkv_weight,
    out_weight,
    pair_table,
    pair_weight,
    gate_weight,
    up_weight,
    down_weight,
):
    windows, row_count, width = tokens.shape
    length = distance_bins.shape[2]
    head_count = pair_weight.shape[1]
    head_size = width // head_count
    head_scale = 1.0 / math.sqrt(head_size)
    table_rows = pair_table.shape[0]
    bin_count = table_rows // 2
    classes = class_table.shape[0]
    total_rows = windows * row_count
    win_count = lax.axis_size("win")
    seq_count = lax.axis_size("seq")
    devices = win_count * seq_count
    owner = lax.axis_index("win") * seq_count + lax.axis_index("seq")
    tokens_all = lax.all_gather(tokens, "seq", axis=1, tiled=True)
    class_onehot = (cath_ids[:, None] == jnp.arange(classes, dtype=jnp.int32)[None, :]).astype(f32)
    pre_cond = jnp.dot(
        class_onehot, class_table.astype(f32), precision=highest
    ) + time_embed(noise_times, width)
    cond_sig = jax.nn.sigmoid(pre_cond)
    condition = pre_cond * cond_sig
    window_facts = lax.all_gather(
        jnp.concatenate([pre_cond, class_onehot], axis=-1), "win", axis=0, tiled=True
    )
    ada_float = ada_weight.astype(f32)
    modulation = jnp.dot(condition, ada_float, precision=highest).reshape(windows, 6, width)
    shift_attn = modulation[:, 0][:, None, :]
    scale_attn = modulation[:, 1][:, None, :]
    gate_attn = modulation[:, 2][:, None, :]
    shift_ffn = modulation[:, 3][:, None, :]
    scale_ffn = modulation[:, 4][:, None, :]
    gate_ffn = modulation[:, 5][:, None, :]
    table_bias = dot(pair_table, pair_weight).astype(bf16)
    row_pos = lax.axis_index("seq") * row_count + jnp.arange(row_count, dtype=jnp.int32)
    key_pos = jnp.arange(length, dtype=jnp.int32)
    row_first = row_pos[None, :] < chain_start[:, None]
    key_first = key_pos[None, :] < chain_start[:, None]
    pair_index = distance_bins + bin_count * (
        row_first[:, :, None] == key_first[:, None, :]
    ).astype(jnp.int32)
    tokens_float = tokens.astype(f32)
    normed_x, inv_x = layer_norm_parts(tokens_float)
    attn_in = (normed_x * (1.0 + scale_attn) + shift_attn).astype(bf16).reshape(total_rows, width)
    normed_all, _ = layer_norm_parts(tokens_all.astype(f32))
    attn_in_all = (
        (normed_all * (1.0 + scale_attn) + shift_attn).astype(bf16).reshape(windows * length, width)
    )
    queries = dot(attn_in, qkv_weight[:, :width]).astype(bf16)
    keys_values = dot(attn_in_all, qkv_weight[:, width:]).astype(bf16)
    keys_all = keys_values[:, :width]
    values_all = keys_values[:, width:]

    def head_split(array, rows):
        return array.reshape(windows, rows, head_count, head_size)

    query_heads = head_split(queries, row_count)
    key_heads = head_split(keys_all, length)
    value_heads = head_split(values_all, length)
    pair_onehot = (
        pair_index[:, None, :, :] == jnp.arange(table_rows, dtype=jnp.int32)[None, :, None, None]
    ).astype(bf16)
    raw_scores = jnp.einsum("grhe,glhe->ghrl", query_heads, key_heads, preferred_element_type=f32)
    pair_bias = jnp.einsum("kh,gkrl->ghrl", table_bias, pair_onehot, preferred_element_type=f32)
    scores = raw_scores * head_scale + pair_bias
    row_max = jnp.max(scores, axis=-1, keepdims=True)
    exp_scores = jnp.exp(scores - row_max)
    exp_total = jnp.sum(exp_scores, axis=-1, keepdims=True)
    soft_probs = exp_scores / exp_total
    probs_low = soft_probs.astype(bf16)
    attn_mixed = jnp.einsum("ghrl,glhe->grhe", probs_low, value_heads, preferred_element_type=f32)
    attn_mixed = attn_mixed.astype(bf16).reshape(total_rows, width)

    attn_out = dot(attn_mixed, out_weight).reshape(windows, row_count, width)
    gate_attn_sig = jax.nn.sigmoid(gate_attn)
    hidden_state = tokens_float + gate_attn_sig * attn_out
    normed_h, inv_h = layer_norm_parts(hidden_state)
    ffn_in = (normed_h * (1.0 + scale_ffn) + shift_ffn).astype(bf16).reshape(total_rows, width)
    gate_val = dot(ffn_in, gate_weight)
    up_val = dot(ffn_in, up_weight)
    gate_sig = jax.nn.sigmoid(gate_val)
    silu_gate = gate_val * gate_sig
    ffn_hidden = (silu_gate * up_val).astype(bf16)
    gate_ffn_sig = jax.nn.sigmoid(gate_ffn)
    grad_layer = cotangent.astype(f32)
    grad_ffn = (gate_ffn_sig * grad_layer).astype(bf16).reshape(total_rows, width)
    owned_down = reduce_owned(dot_tn(ffn_hidden, grad_ffn).astype(bf16), False)
    ffn_out = dot(ffn_hidden, down_weight).reshape(windows, row_count, width)
    layer_out = (hidden_state + gate_ffn_sig * ffn_out).astype(bf16)
    grad_gate_ffn = jnp.sum(grad_layer * ffn_out * gate_ffn_sig * (1.0 - gate_ffn_sig), axis=1)
    grad_hidden_ffn = dot_nt(grad_ffn, down_weight)
    grad_up_val = (grad_hidden_ffn * silu_gate).astype(bf16)
    grad_gate_val = (
        grad_hidden_ffn * up_val * gate_sig * (1.0 + gate_val * (1.0 - gate_sig))
    ).astype(bf16)
    owned_gate = reduce_owned(dot_tn(ffn_in, grad_gate_val).astype(bf16), True)
    owned_up = reduce_owned(dot_tn(ffn_in, grad_up_val).astype(bf16), False)
    grad_ffn_in = dot_nt(grad_gate_val, gate_weight) + dot_nt(grad_up_val, up_weight)
    grad_ffn_in = grad_ffn_in.reshape(windows, row_count, width)
    grad_scale_ffn = jnp.sum(grad_ffn_in * normed_h, axis=1)
    grad_shift_ffn = jnp.sum(grad_ffn_in, axis=1)
    grad_hidden = grad_layer + norm_back(grad_ffn_in * (1.0 + scale_ffn), normed_h, inv_h)
    grad_attn_out = (gate_attn_sig * grad_hidden).astype(bf16).reshape(total_rows, width)
    grad_gate_attn = jnp.sum(grad_hidden * attn_out * gate_attn_sig * (1.0 - gate_attn_sig), axis=1)
    grad_out = dot_tn(attn_mixed, grad_attn_out).astype(bf16)
    grad_mixed = dot_nt(grad_attn_out, out_weight).astype(bf16)

    grad_heads = head_split(grad_mixed, row_count)
    grad_probs = jnp.einsum("grhe,glhe->ghrl", grad_heads, value_heads, preferred_element_type=f32)
    grad_scores = (
        soft_probs * (grad_probs - jnp.sum(soft_probs * grad_probs, axis=-1, keepdims=True))
    ).astype(bf16)
    grad_query = (
        jnp.einsum("ghrl,glhe->grhe", grad_scores, key_heads, preferred_element_type=f32) * head_scale
    )
    grad_key = (
        jnp.einsum("ghrl,grhe->glhe", grad_scores, query_heads, preferred_element_type=f32)
        * head_scale
    )
    grad_value = jnp.einsum("ghrl,grhe->glhe", probs_low, grad_heads, preferred_element_type=f32)
    grad_table = jnp.einsum("ghrl,gkrl->kh", grad_scores, pair_onehot, preferred_element_type=f32)
    grad_query = grad_query.astype(bf16).reshape(total_rows, width)
    grad_kv = jnp.concatenate(
        [
            grad_key.astype(bf16).reshape(windows * length, width),
            grad_value.astype(bf16).reshape(windows * length, width),
        ],
        axis=-1,
    )
    grad_in_part = dot_nt(grad_kv, qkv_weight[:, width:]).astype(bf16)
    grad_in_far = lax.psum_scatter(
        grad_in_part.reshape(windows, length, width), "seq", scatter_dimension=1, tiled=True
    )
    grad_qkv = jnp.concatenate(
        [
            dot_tn(attn_in, grad_query).astype(bf16),
            dot_tn(attn_in_all, grad_kv).astype(bf16),
            grad_out,
        ],
        axis=-1,
    )
    owned_qkv_out = reduce_owned(grad_qkv, True)
    grad_attn_in = dot_nt(grad_query, qkv_weight[:, :width]).reshape(
        windows, row_count, width
    ) + grad_in_far.astype(f32)
    grad_scale_attn = jnp.sum(grad_attn_in * normed_x, axis=1)
    grad_shift_attn = jnp.sum(grad_attn_in, axis=1)
    grad_tokens = (
        grad_hidden + norm_back(grad_attn_in * (1.0 + scale_attn), normed_x, inv_x)
    ).astype(bf16)
    grad_mod = jnp.concatenate(
        [
            grad_shift_attn,
            grad_scale_attn,
            grad_gate_attn,
            grad_shift_ffn,
            grad_scale_ffn,
            grad_gate_ffn,
        ],
        axis=1,
    )
    parts = jnp.concatenate([grad_mod.reshape(-1), grad_table.reshape(-1)])
    parts_all = lax.all_gather(parts, ("win", "seq"), axis=0)
    mod_size = windows * 6 * width
    mod_all = jnp.sum(
        parts_all[:, :mod_size].reshape(win_count, seq_count, windows, 6 * width), axis=1
    ).reshape(win_count * windows, 6 * width)
    table_all = jnp.sum(parts_all[:, mod_size:], axis=0).reshape(table_rows, head_count)
    pre_all = window_facts[:, :width]
    onehot_all = window_facts[:, width:]
    ada_rows = width // devices
    sig_all = jax.nn.sigmoid(pre_all)
    condition_rows = lax.dynamic_slice_in_dim(pre_all * sig_all, owner * ada_rows, ada_rows, 1)
    owned_ada = lax.dot_general(
        condition_rows, mod_all, (((0,), (0,)), ((), ())), precision=highest
    )
    class_share = classes * width // devices
    per_class = width // class_share
    column_at = (owner % per_class) * class_share
    pre_cols = lax.dynamic_slice_in_dim(pre_all, column_at, class_share, 1)
    sig_cols = lax.dynamic_slice_in_dim(sig_all, column_at, class_share, 1)
    ada_cols = lax.dynamic_slice_in_dim(ada_weight, column_at, class_share, 0).astype(f32)
    grad_cond = lax.dot_general(mod_all, ada_cols, (((1,), (1,)), ((), ())), precision=highest)
    grad_pre = grad_cond * sig_cols * (1.0 + pre_cols * (1.0 - sig_cols))
    onehot_mine = lax.dynamic_slice_in_dim(onehot_all, owner // per_class, 1, 1)
    owned_class = jnp.sum(grad_pre * onehot_mine, axis=0)
    grad_pair_table = jnp.dot(table_all, pair_weight.astype(f32).T, precision=highest).reshape(-1)
    grad_pair_weight = jnp.dot(pair_table.astype(f32).T, table_all, precision=highest).reshape(-1)
    table_size = grad_pair_table.shape[0] // devices
    weight_size = grad_pair_weight.shape[0] // devices
    owned_pair_table = lax.dynamic_slice_in_dim(grad_pair_table, owner * table_size, table_size)
    owned_pair_weight = lax.dynamic_slice_in_dim(grad_pair_weight, owner * weight_size, weight_size)
    return (
        layer_out,
        grad_tokens,
        owned_class,
        owned_ada.reshape(-1),
        owned_qkv_out[:, : 3 * width].reshape(-1),
        owned_qkv_out[:, 3 * width :].reshape(-1),
        owned_pair_table,
        owned_pair_weight,
        owned_gate.reshape(-1),
        owned_up.reshape(-1),
        owned_down.reshape(-1),
    )


def solution(mesh):
    rows = P("win", "seq", None)
    flat = P(("win", "seq"))
    placed = (rows, rows, P("win"), P("win"), P("win"), rows) + (P(),) * 9
    return jax.shard_map(
        per_device, mesh=mesh, in_specs=placed, out_specs=(rows, rows) + (flat,) * 9, check_vma=False
    )
```

time: 1510 us -> 376 us (0.25); the launches traced: 1480 us -> 371 us
  waiting for transfers between devices: 589 us -> 77.6 us
  local copies, waits for them, and re-layouts: 397 us -> 89.3 us
  blocking collectives: 293 us -> 10.7 us
    all_to_all x1 -> x0, waiting for transfers between devices: 560 us -> none  [per_device(): lax.all_to_all(lax.all_to_all(packed.astype(jnp.bfloat16), 'win', split_a...]
    all_to_all x1 -> x0, blocking collectives: 293 us -> none  [per_device(): lax.all_to_all(packed.astype(jnp.bfloat16), 'win', split_axis=0, concat_a...]
    unnamed x129 -> x152, local copies, waits for them, and re-layouts: 235 us -> 24 us
    ppermute x0 -> x20, waiting for transfers between devices: none -> 67.7 us  [exchange(): return lax.ppermute(values, axis, [(i, i ^ 1 << bit) for i in range(size)])]
    concatenate x2, local copies, waits for them, and re-layouts: 51.4 us -> 1.4 us  [the longest x1 1.28 us: per_device(): jnp.concatenate([grad_shift_attn, grad_scale_attn, grad_gate_attn, grad_s...]
    another operation x10 -> x0, local copies, waits for them, and re-layouts: 47.2 us -> none  [the longest x9 47.2 us: per_device(): flat.reshape(win_count, seq_count, -1)]
    reduce_sum x2, other arithmetic: 35.1 us -> 0.67 us  [the longest x1 0.65 us: per_device(): jnp.sum(parts_all[:, :mod_size].reshape(win_count, seq_count, windows, 6...]
    all_gather x2, waiting for transfers between devices: 28.3 us -> 0.01 us  [the longest x1 0.01 us: per_device(): tokens_all = lax.all_gather(tokens, 'seq', axis=1, tiled=True)]
  transfers between devices with their start and end apart: 5 -> 23, of which waited for: 3 -> 9; matrix products, arithmetic and copies ran while one was open for 9% -> 33% of each run, Pallas kernels for 0% -> 0%
where the time goes in v1:
time: 376 us; the launch traced here: 371 us
  matrix products  113 us (30%)
  local copies, waits for them, and re-layouts  89.3 us (24%)
  waiting for transfers between devices  77.6 us (21%)
  other arithmetic  42.9 us (11%)
  starting transfers between devices  22.2 us (6%)
  between operations  15.5 us (4%)
  blocking collectives  10.7 us (3%)
    ppermute x20, waiting for transfers between devices, exchange(): return lax.ppermute(values, axis, [(i, i ^ 1 << bit) for i in range(size)])  67.7 us
    unnamed x152, local copies, waits for them, and re-layouts  24 us
    ppermute x20, starting transfers between devices, exchange(): return lax.ppermute(values, axis, [(i, i ^ 1 << bit) for i in range(size)])  22.1 us
    dot_general x6, matrix products, dot_tn(): lax.dot_general(a, b, (((0,), (0,)), ((), ())), preferred_element_type=f32)  17.9 us
    convert_element_type x16, other arithmetic, reduce_owned(): current = current.astype(bf16)  16.2 us
    dot_general x1, matrix products, per_device(): jnp.einsum('kh,gkrl->ghrl', table_bias, pair_onehot, preferred_element_ty...  15 us
    dot_general x6, matrix products, dot_nt(): lax.dot_general(a, b, (((1,), (1,)), ((), ())), preferred_element_type=f32)  14 us
    dynamic_slice x10, local copies, waits for them, and re-layouts, reduce_owned(): lax.dynamic_index_in_dim(view, mine, 1, keepdims=False)  13.2 us
  transfers between devices with their start and end apart: 23, of which 9 were waited for; matrix products, arithmetic and copies ran while one was open for 33% of the time, Pallas kernels for 0%

profile of v1, /device:TPU:0, one launch (start us, length us, event | category | flops | bytes accessed | tf_op | source)
XLA Modules:
  0.0 371.0 jit_solution(2220331934278973549)
XLA Ops:
  14.3 5.9 %fusion.107 = f32[2,4608]{1,0:T(2,128)S(1)} fusion(bf16[768,4608]{1,0:T(8,128)(2,1)} %param.22, f32[2,768]{1,0:T(2,128)S(1)} %convolution_add_fusion.2), kind=kOutput, calls=%fused_computation.212 | convolution fusion | flops 84940800 | bytes 7120896 | tf_op jit(solution)/shard_map/dot_general | solution.py:125
  22.0 1.7 convolution_convert_fusion.9
  23.9 10.7 %all-gather.2 = f32[8,2,772]{2,1,0:T(2,128)S(1)} all-gather(f32[1,2,772]{2,1,0:T(2,128)S(1)} %maximum_bitcast_fusion), channel_id=1, replica_groups=mesh['win'=8,'seq'=4] {'win'}, dimensions={0}, use_global_device_ids=true | all-gather | bytes 55584 | tf_op jit(solution)/shard_map/all_gather | solution.py:121
  35.2 15.0 %fusion.2 = f32[2,128,512,12]{1,3,2,0:T(8,128)} fusion(s32[2,128,512]{1,2,0:T(8,128)S(1)} %copy.73, bf16[128,256]{1,0:T(8,128)(2,1)} %param.25, bf16[256,12]{0,1:T(8,128)(2,1)} %param.26), kind=kOutput, calls=%fused_computation.3 | convolution fusion | flops 420218368 | bytes 6887424 | tf_op jit(solution)/shard_map/kh,gkrl->ghrl/dot_general | solution.py:162
  50.2 9.3 %copy.74 = f32[2,128,512,12]{2,1,3,0:T(8,128)} copy(f32[2,128,512,12]{1,3,2,0:T(8,128)} %fusion.2) | data formatting | bytes 12582912 | tf_op jit(solution)/shard_map/kh,gkrl->ghrl/dot_general | solution.py:162
  62.9 1.8 convert_reduce_fusion
  65.4 1.7 fusion.14
  68.3 2.8 convolution_convert_fusion.3
  72.5 1.6 copy.70
  74.2 2.9 reshape.462
  77.0 3.1 copy.68
  80.2 4.0 %reshape.459 = bf16[2,512,12,64]{1,0,3,2:T(2,128)(2,1)} reshape(bf16[1024,768]{0,1:T(8,128)(2,1)} %copy.68) | data formatting | bytes 3145728 | tf_op jit(solution)/shard_map/reshape | solution.py:153
  84.2 3.8 %bitcast_add_fusion = f32[2,12,128,512]{3,2,1,0:T(8,128)S(1)} fusion(f32[2,128,512,12]{2,1,3,0:T(8,128)} %copy.74, bf16[2,512,12,64]{1,0,3,2:T(2,128)(2,1)S(1)} %reshape.462, bf16[2,128,12,64]{1,0,3,2:T(2,128)(2,1)S(1)} %reshape.461), kind=kOutput, calls=%fused_computation.6 | convolution fusion | flops 204472320 | bytes 14548992 | tf_op jit(solution)/shard_map/grhe,glhe->ghrl/dot_general | solution.py:161
  88.1 2.7 copy-done.2
  90.8 4.3 %fusion.125 = (f32[2,12,128]{2,1,0:T(8,128)}, f32[2,12,128,512]{3,2,1,0:T(8,128)}) fusion(f32[2,12,128,512]{3,2,1,0:T(8,128)S(1)} %bitcast_add_fusion), kind=kOutput, calls=%fused_computation.260 | output fusion | flops 3146239 | bytes 12595200 | tf_op jit(solution)/shard_map/sub | solution.py:165
  95.0 10.2 %fusion.45 = bf16[2,12,64,128]{3,2,1,0:T(8,128)(2,1)S(1)} fusion(bf16[2,512,12,64]{1,0,3,2:T(2,128)(2,1)S(1)} %copy-done.24, f32[2,12,128]{2,1,0:T(8,128)} %get-tuple-element.63, f32[2,12,128,512]{3,2,1,0:T(8,128)} %copy-done.2), kind=kOutput, calls=%fused_computation.70 | convolution fusion | flops 206245376 | bytes 8269824 | tf_op jit(solution)/shard_map/ghrl,glhe->grhe/dot_general | solution.py:169
  106.3 4.0 %fusion.127 = f32[256,3072]{1,0:T(8,128)S(1)} fusion(bf16[256,768]{1,0:T(8,128)(2,1)S(1)} %bitcast.294, bf16[768,3072]{1,0:T(8,128)(2,1)} %param.28), kind=kOutput, calls=%fused_computation.262 | convolution fusion | flops 1207959552 | bytes 8257536 | tf_op jit(solution)/shard_map/dot_general | solution.py:37
  111.8 3.1 multiply_convert_fusion.2
  116.4 3.7 convolution_convert_fusion
  121.5 3.5 convolution_convert_fusion.2
  125.0 3.6 convolution_convert_fusion.1
  131.1 2.0 multiply_reduce_fusion.1
  134.0 11.7 %fusion.29 = bf16[2,512,12,64]{1,3,2,0:T(8,128)(2,1)} fusion(bf16[2,128,12,64]{1,0,3,2:T(2,128)(2,1)S(1)} %reshape.468, f32[2,12,128]{2,1,0:T(8,128)S(1)} %copy-done.40, f32[2,12,128,512]{3,2,1,0:T(8,128)} %copy-done.2), kind=kOutput, calls=%fused_computation.57 | convolution fusion | flops 206835200 | bytes 8269824 | tf_op jit(solution)/shard_map/ghrl,grhe->glhe/dot_general | solution.py:218
  145.7 4.1 %multiply_reduce_fusion = (f32[2,12,128]{2,1,0:T(8,128)S(1)}, f32[2,12,128,512]{3,2,1,0:T(8,128)S(1)}) fusion(f32[2,12,128,512]{3,2,1,0:T(8,128)} %get-tuple-element.64, f32[2,12,128]{2,1,0:T(8,128)S(1)} %copy-done.40, bf16[2,512,12,64]{1,0,3,2:T(2,128)(2,1)S(1)} %copy-done.25, bf16[2,128,12,64]{1,0,3,2:T(2,128)(2,1)S(1)} %reshape.468), kind=kOutput, calls=%fused_computation.8 | convolution fusion | flops 206042112 | bytes 14573568 | tf_op jit(solution)/shard_map/grhe,glhe->ghrl/dot_general | solution.py:207
  151.9 1.9 fusion.42
  153.8 1.8 fusion.32
  155.6 5.5 %copy.86 = bf16[2,12,128,512]{2,1,3,0:T(8,128)(2,1)} copy(bf16[2,12,128,512]{3,2,1,0:T(8,128)(2,1)S(1)} %multiply_convert_fusion) | data formatting | bytes 6291456 | tf_op jit(solution)/shard_map/convert_element_type | solution.py:210
  161.1 2.1 copy.89
  163.2 3.0 copy.85
  167.8 5.0 %constant_dynamic-slice_fusion.6 = (bf16[4,1,384,768]{3,2,1,0:T(8,128)(2,1)}, bf16[4,1,384,768]{3,2,1,0:T(8,128)(2,1)}) fusion(bf16[4,2,384,768]{3,2,1,0:T(8,128)(2,1)} %bitcast.271, s32[]{:T(128)S(6)} %select_n.104, s32[]{:T(128)S(6)} %select_n.105), kind=kLoop, calls=%fused_computation.185 | loop fusion | bytes 9437192 | tf_op jit(solution)/shard_map/jit(dynamic_index_in_dim)/dynamic_slice | solution.py:76
  173.2 2.7 constant_dynamic-slice_fusion.12
  177.2 1.8 constant_dynamic-slice_fusion.16
  179.6 1.6 convolution_convert_fusion.6
  181.1 2.4 copy.91
  183.6 3.2 copy.83
  186.8 1.6 copy.108
  188.4 9.2 %fusion.57 = f32[128,12]{1,0:T(8,128)S(1)} fusion(bf16[2,12,128,512]{2,1,3,0:T(8,128)(2,1)S(1)} %copy-done.17, s32[2,128,512]{1,2,0:T(8,128)S(1)} %copy-done.35), kind=kOutput, calls=%fused_computation.93 | convolution fusion | flops 419430400 | bytes 3676160 | tf_op jit(solution)/shard_map/ghrl,gkrl->kh/dot_general | solution.py:219
  197.7 1.7 constant_dynamic-update-slice_fusion.1
  200.6 3.8 %fusion.23 = bf16[1024,768]{1,0:T(8,128)(2,1)} fusion(bf16[1024,1536]{0,1:T(8,128)(2,1)S(1)} %constant_dynamic-update-slice_fusion, bf16[768,2304]{1,0:T(8,128)(2,1)S(1)} %copy-done.54), kind=kOutput, calls=%fused_computation.51 | convolution fusion | flops 2416705536 | bytes 7077888 | tf_op jit(solution)/shard_map/dot_general | solution.py:41
  205.0 5.1 %convolution_convert_fusion.4 = bf16[768,1536]{1,0:T(8,128)(2,1)S(1)} fusion(bf16[1024,768]{1,0:T(8,128)(2,1)} %bitcast.318, bf16[1024,1536]{0,1:T(8,128)(2,1)} %copy-done.33), kind=kOutput, calls=%fused_computation.27 | convolution fusion | flops 2417098752 | bytes 7077888 | tf_op jit(solution)/shard_map/dot_general | solution.py:45
  212.7 2.3 fusion.5
  215.0 1.6 constant_dynamic-slice_fusion.4
  218.1 2.6 fusion.6
  223.1 2.6 fusion.7
  231.2 9.1 %reduce-scatter.2.cloned.1.call-done = bf16[2,128,768]{2,1,0:T(8,128)(2,1)} async-done(((bf16[2,512,768]{2,1,0:T(8,128)(2,1)}), bf16[2,128,768]{2,1,0:T(8,128)(2,1)}) %reduce-scatter.2.cloned.1.call-update) | async-done | bytes 393232 | tf_op jit(solution)/shard_map/reduce_scatter | solution.py:229
  240.4 3.7 %fusion.78 = (f32[2,768]{1,0:T(2,128)S(1)}, f32[2,128]{1,0:T(2,128)}, f32[2,128]{1,0:T(2,128)}, f32[2,768]{1,0:T(2,128)S(1)}, f32[2,128,768]{2,1,0:T(8,128)}) fusion(bf16[2,128,768]{2,1,0:T(8,128)(2,1)S(1)} %copy-done.6, f32[2,128]{1,0:T(2,128)} %copy-done.50, f32[2,128]{1,0:T(2,128)} %copy-done.49, f32[2,768]{1,0:T(2,128)S(1)} %copy-done.38, ...), kind=kOutput, calls=%fused_computation.118 | convolution fusion | flops 304345600 | bytes 3168256 | tf_op jit(solution)/shard_map/dot_general | solution.py:41
  254.7 2.2 fusion.77
  257.0 1.7 fusion.16
  260.2 10.5 %collective-permute-done.11 = bf16[192,3072]{1,0:T(8,128)(2,1)} collective-permute-done((bf16[192,3072]{1,0:T(8,128)(2,1)}, bf16[192,3072]{1,0:T(8,128)(2,1)}, u32[]{:S(2)}, u32[]{:S(2)}) %collective-permute-start.11) | collective-permute-done | bytes 1179680 | tf_op jit(solution)/shard_map/ppermute | solution.py:59
  270.7 1.8 fusion.17
  274.2 1.7 fusion.18
  276.7 5.6 %collective-permute-done.1 = bf16[192,3072]{1,0:T(8,128)(2,1)} collective-permute-done((bf16[192,3072]{1,0:T(8,128)(2,1)}, bf16[192,3072]{1,0:T(8,128)(2,1)}, u32[]{:S(2)}, u32[]{:S(2)}) %collective-permute-start.1) | collective-permute-done | bytes 1179680 | tf_op jit(solution)/shard_map/ppermute | solution.py:59
  282.3 1.7 fusion.19
  285.3 9.6 %collective-permute-done.17 = bf16[384,768]{1,0:T(8,128)(2,1)S(1)} collective-permute-done((bf16[384,768]{1,0:T(8,128)(2,1)S(1)}, bf16[384,768]{1,0:T(8,128)(2,1)S(1)}, u32[]{:S(2)}, u32[]{:S(2)}) %collective-permute-start.17) | collective-permute-done | bytes 589856 | tf_op jit(solution)/shard_map/ppermute | solution.py:59
  295.1 1.6 collective-permute-start.18
  296.7 12.3 %collective-permute-done.12 = bf16[96,3072]{1,0:T(8,128)(2,1)S(1)} collective-permute-done((bf16[96,3072]{1,0:T(8,128)(2,1)S(1)}, bf16[96,3072]{1,0:T(8,128)(2,1)S(1)}, u32[]{:S(2)}, u32[]{:S(2)}) %collective-permute-start.12) | collective-permute-done | bytes 589856 | tf_op jit(solution)/shard_map/ppermute | solution.py:59
  309.3 1.6 collective-permute-start.13
  311.9 1.6 collective-permute-start.3
  313.6 2.7 collective-permute-start.19
  316.3 7.6 %collective-permute-done.13 = bf16[48,3072]{1,0:T(8,128)(2,1)S(1)} collective-permute-done((bf16[48,3072]{1,0:T(8,128)(2,1)S(1)}, bf16[48,3072]{1,0:T(8,128)(2,1)S(1)}, u32[]{:S(2)}, u32[]{:S(2)}) %collective-permute-start.13) | collective-permute-done | bytes 294944 | tf_op jit(solution)/shard_map/ppermute | solution.py:59
  324.3 12.2 %collective-permute-done.3 = bf16[48,3072]{1,0:T(8,128)(2,1)S(1)} collective-permute-done((bf16[48,3072]{1,0:T(8,128)(2,1)S(1)}, bf16[48,3072]{1,0:T(8,128)(2,1)S(1)}, u32[]{:S(2)}, u32[]{:S(2)}) %collective-permute-start.3) | collective-permute-done | bytes 294944 | tf_op jit(solution)/shard_map/ppermute | solution.py:59
  336.7 1.8 collective-permute-start.4
  339.8 9.3 %collective-permute-done.4 = bf16[24,3072]{1,0:T(8,128)(2,1)S(1)} collective-permute-done((bf16[24,3072]{1,0:T(8,128)(2,1)S(1)}, bf16[24,3072]{1,0:T(8,128)(2,1)S(1)}, u32[]{:S(2)}, u32[]{:S(2)}) %collective-permute-start.4) | collective-permute-done | bytes 147488 | tf_op jit(solution)/shard_map/ppermute | solution.py:59
  360.2 2.5 fusion.60
  (294 shorter events, 75.9 us)
Async XLA Ops:
  7.2 98.0 %copy-start = (bf16[768,768]{1,0:T(8,128)(2,1)S(1)}, bf16[768,768]{1,0:T(8,128)(2,1)}, u32[]{:S(2)}) copy-start(bf16[768,768]{1,0:T(8,128)(2,1)} %param.24) | copy-start | bytes 3538948
  7.2 55.7 %all-gather.6.cloned.1.call-start = ((), (), s32[]{:S(2)}) async-start(), calls=%async_computation.1 | async-start | bytes 1966080 | tf_op jit(solution)/shard_map/all_gather | solution.py:114
  7.9 232.4 %reduce-scatter.2.cloned.1.call-start = ((), (), s32[]{:S(2)}) async-start(), calls=%async_computation.2 | async-start | bytes 1966080 | tf_op jit(solution)/shard_map/reduce_scatter | solution.py:229
  12.0 8.9 %copy-start.49 = (f32[2,128]{1,0:T(2,128)}, f32[2,128]{1,0:T(2,128)S(1)}, u32[]{:S(2)}) copy-start(f32[2,128]{1,0:T(2,128)S(1)} %broadcast_multiply_fusion.5) | copy-start | bytes 3076
  13.3 7.7 %copy-start.50 = (f32[2,128]{1,0:T(2,128)}, f32[2,128]{1,0:T(2,128)S(1)}, u32[]{:S(2)}) copy-start(f32[2,128]{1,0:T(2,128)S(1)} %add_rsqrt_fusion.2) | copy-start | bytes 3076
  14.3 6.7 %copy-start.6 = (bf16[2,128,768]{2,1,0:T(8,128)(2,1)S(1)}, bf16[2,128,768]{2,1,0:T(8,128)(2,1)}, u32[]{:S(2)}) copy-start(bf16[2,128,768]{2,1,0:T(8,128)(2,1)} %param.15) | copy-start | bytes 1179652
  20.2 3.5 copy-start.36
  35.0 49.3 %copy-start.18 = (bf16[2,128,12,64]{1,0,3,2:T(2,128)(2,1)}, bf16[2,128,12,64]{1,0,3,2:T(2,128)(2,1)S(1)}, u32[]{:S(2)}) copy-start(bf16[2,128,12,64]{1,0,3,2:T(2,128)(2,1)S(1)} %reshape.461) | copy-start | bytes 1179652
  35.2 15.1 %copy-start.34 = (s32[2,128,512]{1,2,0:T(8,128)}, s32[2,128,512]{1,2,0:T(8,128)S(1)}, u32[]{:S(2)}) copy-start(s32[2,128,512]{1,2,0:T(8,128)S(1)} %copy.73) | copy-start | bytes 1572868
  50.2 10.0 %copy-start.48 = (f32[2,1,768]{2,1,0:T(1,128)S(1)}, f32[2,1,768]{2,1,0:T(1,128)}, u32[]{:S(2)}) copy-start(f32[2,1,768]{2,1,0:T(1,128)} %get-tuple-element.59) | copy-start | bytes 18436
  50.2 10.6 %copy-start.47 = (f32[2,1,768]{2,1,0:T(1,128)S(1)}, f32[2,1,768]{2,1,0:T(1,128)}, u32[]{:S(2)}) copy-start(f32[2,1,768]{2,1,0:T(1,128)} %get-tuple-element.60) | copy-start | bytes 18436
  50.2 11.9 %copy-start.26 = (bf16[2,128,768]{2,1,0:T(8,128)(2,1)S(1)}, bf16[2,128,768]{2,1,0:T(8,128)(2,1)}, u32[]{:S(2)}) copy-start(bf16[2,128,768]{2,1,0:T(8,128)(2,1)} %param.16) | copy-start | bytes 1179652
  60.9 4.6 %copy-start.42 = (f32[2,768]{1,0:T(2,128)}, f32[2,768]{1,0:T(2,128)S(1)}, u32[]{:S(2)}) copy-start(f32[2,768]{1,0:T(2,128)S(1)} %get-tuple-element.75) | copy-start | bytes 18436
  64.8 3.5 copy-start.53
  77.0 7.2 %copy-start.4 = (bf16[2,512,12,64]{1,0,3,2:T(2,128)(2,1)}, bf16[2,512,12,64]{1,0,3,2:T(2,128)(2,1)S(1)}, u32[]{:S(2)}) copy-start(bf16[2,512,12,64]{1,0,3,2:T(2,128)(2,1)S(1)} %reshape.462) | copy-start | bytes 4718596
  90.8 4.3 %copy-start.24 = (bf16[2,512,12,64]{1,0,3,2:T(2,128)(2,1)S(1)}, bf16[2,512,12,64]{1,0,3,2:T(2,128)(2,1)}, u32[]{:S(2)}) copy-start(bf16[2,512,12,64]{1,0,3,2:T(2,128)(2,1)} %reshape.459) | copy-start | bytes 4718596
  105.8 4.5 %slice-start.10 = ((s8[4718592]{0:T(1024)(128)(4,1)}), s8[4194304]{0:T(1024)(128)(4,1)S(1)}, s32[]{:S(2)}) async-start(s8[4718592]{0:T(1024)(128)(4,1)} %bitcast.345), calls=%async_computation.14 | async-start | bytes 8388608
  106.3 4.0 %slice-start.11 = ((s8[4718592]{0:T(1024)(128)(4,1)}), s8[524288]{0:T(1024)(128)(4,1)S(1)}, s32[]{:S(2)}) async-start(s8[4718592]{0:T(1024)(128)(4,1)} %bitcast.345), calls=%async_computation.15 | async-start | bytes 1048576
  106.3 5.5 %slice-start.8 = ((s8[4718592]{0:T(1024)(128)(4,1)}), s8[4194304]{0:T(1024)(128)(4,1)S(1)}, s32[]{:S(2)}) async-start(s8[4718592]{0:T(1024)(128)(4,1)} %bitcast.343), calls=%async_computation.12 | async-start | bytes 8388608
  121.5 7.1 %slice-start.6 = ((s8[4718592]{0:T(1024)(128)(4,1)}), s8[4194304]{0:T(1024)(128)(4,1)S(1)}, s32[]{:S(2)}) async-start(s8[4718592]{0:T(1024)(128)(4,1)} %bitcast.302), calls=%async_computation.10 | async-start | bytes 8388608
  125.0 3.6 slice-start.7
  133.2 12.6 %copy-start.20 = (bf16[2,128,768]{2,1,0:T(8,128)(2,1)}, bf16[2,128,768]{2,1,0:T(8,128)(2,1)S(1)}, u32[]{:S(2)}) copy-start(bf16[2,128,768]{2,1,0:T(8,128)(2,1)S(1)} %multiply_convert_fusion.5) | copy-start | bytes 1179652
  134.0 11.7 %copy-start.25 = (bf16[2,512,12,64]{1,0,3,2:T(2,128)(2,1)S(1)}, bf16[2,512,12,64]{1,0,3,2:T(2,128)(2,1)}, u32[]{:S(2)}) copy-start(bf16[2,512,12,64]{1,0,3,2:T(2,128)(2,1)} %reshape.459) | copy-start | bytes 4718596
  145.7 4.1 %slice-start.4 = ((s8[6291456]{0:T(1024)(128)(4,1)}), s8[4194304]{0:T(1024)(128)(4,1)S(1)}, s32[]{:S(2)}) async-start(s8[6291456]{0:T(1024)(128)(4,1)} %bitcast.278), calls=%async_computation.8 | async-start | bytes 8388608
  145.7 4.7 %slice-start.5 = ((s8[6291456]{0:T(1024)(128)(4,1)}), s8[2097152]{0:T(1024)(128)(4,1)S(1)}, s32[]{:S(2)}) async-start(s8[6291456]{0:T(1024)(128)(4,1)} %bitcast.278), calls=%async_computation.9 | async-start | bytes 4194304
  167.8 5.4 %slice-start.2 = ((s8[4718592]{0:T(1024)(128)(4,1)}), s8[4194304]{0:T(1024)(128)(4,1)S(1)}, s32[]{:S(2)}) async-start(s8[4718592]{0:T(1024)(128)(4,1)} %bitcast.275), calls=%async_computation.6 | async-start | bytes 8388608
  167.8 5.4 %slice-start.3 = ((s8[4718592]{0:T(1024)(128)(4,1)}), s8[524288]{0:T(1024)(128)(4,1)S(1)}, s32[]{:S(2)}) async-start(s8[4718592]{0:T(1024)(128)(4,1)} %bitcast.275), calls=%async_computation.7 | async-start | bytes 1048576
  172.9 38.9 %collective-permute-start.15 = (bf16[1536,768]{1,0:T(8,128)(2,1)}, bf16[1536,768]{1,0:T(8,128)(2,1)}, u32[]{:S(2)}, u32[]{:S(2)}) collective-permute-start(bf16[1536,768]{1,0:T(8,128)(2,1)} %bitcast.71), channel_id=1, source_target_pairs={{0,4},{4,0},{8,12},{12,8},{16,20},{20,16},{24,28},{28,24},{1,5},{5... | collective-permute-start | bytes 7077896 | tf_op jit(solution)/shard_map/ppermute | solution.py:59
  173.2 3.9 %slice-start = ((s8[4718592]{0:T(1024)(128)(4,1)}), s8[4194304]{0:T(1024)(128)(4,1)S(1)}, s32[]{:S(2)}) async-start(s8[4718592]{0:T(1024)(128)(4,1)} %bitcast.272), calls=%async_computation.4 | async-start | bytes 8388608
  173.2 4.0 %slice-start.1 = ((s8[4718592]{0:T(1024)(128)(4,1)}), s8[524288]{0:T(1024)(128)(4,1)S(1)}, s32[]{:S(2)}) async-start(s8[4718592]{0:T(1024)(128)(4,1)} %bitcast.272), calls=%async_computation.5 | async-start | bytes 1048576
  176.0 42.1 %collective-permute-start.10 = (bf16[384,3072]{1,0:T(8,128)(2,1)}, bf16[384,3072]{1,0:T(8,128)(2,1)}, u32[]{:S(2)}, u32[]{:S(2)}) collective-permute-start(bf16[384,3072]{1,0:T(8,128)(2,1)} %bitcast.56), channel_id=1, source_target_pairs={{0,4},{4,0},{8,12},{12,8},{16,20},{20,16},{24,28},{28,24},{1,5},{5... | collective-permute-start | bytes 7077896 | tf_op jit(solution)/shard_map/ppermute | solution.py:59
  179.0 44.2 %collective-permute-start.5 = (bf16[384,3072]{1,0:T(8,128)(2,1)}, bf16[384,3072]{1,0:T(8,128)(2,1)}, u32[]{:S(2)}, u32[]{:S(2)}) collective-permute-start(bf16[384,3072]{1,0:T(8,128)(2,1)} %bitcast.41), channel_id=1, source_target_pairs={{0,4},{4,0},{8,12},{12,8},{16,20},{20,16},{24,28},{28,24},{1,5},{5... | collective-permute-start | bytes 7077896 | tf_op jit(solution)/shard_map/ppermute | solution.py:59
  183.6 4.8 %copy-start.17 = (bf16[2,12,128,512]{2,1,3,0:T(8,128)(2,1)S(1)}, bf16[2,12,128,512]{2,1,3,0:T(8,128)(2,1)}, u32[]{:S(2)}) copy-start(bf16[2,12,128,512]{2,1,3,0:T(8,128)(2,1)} %copy.86) | copy-start | bytes 9437188
  200.6 3.8 %copy-start.33 = (bf16[1024,1536]{0,1:T(8,128)(2,1)}, bf16[1024,1536]{0,1:T(8,128)(2,1)S(1)}, u32[]{:S(2)}) copy-start(bf16[1024,1536]{0,1:T(8,128)(2,1)S(1)} %constant_dynamic-update-slice_fusion) | copy-start | bytes 9437188
  200.6 3.9 %copy-start.21 = (bf16[2,128,768]{2,1,0:T(8,128)(2,1)S(1)}, bf16[2,128,768]{2,1,0:T(8,128)(2,1)}, u32[]{:S(2)}) copy-start(bf16[2,128,768]{2,1,0:T(8,128)(2,1)} %copy-done.20) | copy-start | bytes 1179652
  200.6 3.9 %copy-start.32 = (bf16[2,128,12,64]{1,0,3,2:T(2,128)(2,1)S(1)}, bf16[2,128,12,64]{1,0,3,2:T(2,128)(2,1)}, u32[]{:S(2)}) copy-start(bf16[2,128,12,64]{1,0,3,2:T(2,128)(2,1)} %copy.89) | copy-start | bytes 1179652
  204.5 149.0 %all-gather.8.cloned.1.call-start = ((), (), s32[]{:S(2)}) async-start(), calls=%async_computation.3 | async-start | bytes 1419264 | tf_op jit(solution)/shard_map/all_gather | solution.py:261
  205.0 5.1 %copy-start.14 = (bf16[768,768]{1,0:T(8,128)(2,1)S(1)}, bf16[768,768]{1,0:T(8,128)(2,1)}, u32[]{:S(2)}) copy-start(bf16[768,768]{1,0:T(8,128)(2,1)} %copy.91) | copy-start | bytes 3538948
  211.4 16.7 %collective-permute-start = (bf16[384,3072]{1,0:T(8,128)(2,1)S(1)}, bf16[384,3072]{1,0:T(8,128)(2,1)S(1)}, u32[]{:S(2)}, u32[]{:S(2)}) collective-permute-start(bf16[384,3072]{1,0:T(8,128)(2,1)S(1)} %bitcast.310), channel_id=1, source_target_pairs={{0,4},{4,0},{8,12},{12,8},{16,20},{20,16},{24,28},{28,24},{1,5},{5... | collective-permute-start | bytes 7077896 | tf_op jit(solution)/shard_map/ppermute | solution.py:59
  215.0 3.1 copy-start.7
  216.6 40.4 %collective-permute-start.16 = (bf16[768,768]{1,0:T(8,128)(2,1)}, bf16[768,768]{1,0:T(8,128)(2,1)}, u32[]{:S(2)}, u32[]{:S(2)}) collective-permute-start(bf16[768,768]{1,0:T(8,128)(2,1)} %bitcast.74), channel_id=1, source_target_pairs={{0,8},{4,12},{8,0},{12,4},{16,24},{20,28},{24,16},{28,20},{1,9},{5... | collective-permute-start | bytes 3538952 | tf_op jit(solution)/shard_map/ppermute | solution.py:59
  222.2 48.5 %collective-permute-start.11 = (bf16[192,3072]{1,0:T(8,128)(2,1)}, bf16[192,3072]{1,0:T(8,128)(2,1)}, u32[]{:S(2)}, u32[]{:S(2)}) collective-permute-start(bf16[192,3072]{1,0:T(8,128)(2,1)} %bitcast.59), channel_id=1, source_target_pairs={{0,8},{4,12},{8,0},{12,4},{16,24},{20,28},{24,16},{28,20},{1,9},{5... | collective-permute-start | bytes 3538952 | tf_op jit(solution)/shard_map/ppermute | solution.py:59
  225.7 3.4 copy-start.9
  227.0 47.2 %collective-permute-start.6 = (bf16[192,3072]{1,0:T(8,128)(2,1)}, bf16[192,3072]{1,0:T(8,128)(2,1)}, u32[]{:S(2)}, u32[]{:S(2)}) collective-permute-start(bf16[192,3072]{1,0:T(8,128)(2,1)} %dynamic-slice_bitcast_fusion), channel_id=1, source_target_pairs={{0,16},{4,20},{8,24},{12,28},{16,0},{20,4},{24,8},{28,12},{1,17},{... | collective-permute-start | bytes 3538952 | tf_op jit(solution)/shard_map/ppermute | solution.py:59
  229.2 11.2 %copy-start.38 = (f32[2,768]{1,0:T(2,128)S(1)}, f32[2,768]{1,0:T(2,128)}, u32[]{:S(2)}) copy-start(f32[2,768]{1,0:T(2,128)} %copy-done.37) | copy-start | bytes 18436
  230.3 52.0 %collective-permute-start.1 = (bf16[192,3072]{1,0:T(8,128)(2,1)}, bf16[192,3072]{1,0:T(8,128)(2,1)}, u32[]{:S(2)}, u32[]{:S(2)}) collective-permute-start(bf16[192,3072]{1,0:T(8,128)(2,1)} %dynamic-slice_bitcast_fusion.1), channel_id=1, source_target_pairs={{0,16},{4,20},{8,24},{12,28},{16,0},{20,4},{24,8},{28,12},{1,17},{... | collective-permute-start | bytes 3538952 | tf_op jit(solution)/shard_map/ppermute | solution.py:59
  240.4 14.4 %copy-start.12 = (f32[2,128,768]{2,1,0:T(8,128)S(1)}, f32[2,128,768]{2,1,0:T(8,128)}, u32[]{:S(2)}) copy-start(f32[2,128,768]{2,1,0:T(8,128)} %copy-done.11) | copy-start | bytes 2359300
  253.3 3.7 copy-start.15
  256.9 13.8 %copy-start.16 = (bf16[2,1,96,3072]{3,2,1,0:T(8,128)(2,1)S(1)}, bf16[2,1,96,3072]{3,2,1,0:T(8,128)(2,1)}, u32[]{:S(2)}) copy-start(bf16[2,1,96,3072]{3,2,1,0:T(8,128)(2,1)} %get-tuple-element.41) | copy-start | bytes 3538948
  258.7 36.2 %collective-permute-start.17 = (bf16[384,768]{1,0:T(8,128)(2,1)S(1)}, bf16[384,768]{1,0:T(8,128)(2,1)S(1)}, u32[]{:S(2)}, u32[]{:S(2)}) collective-permute-start(bf16[384,768]{1,0:T(8,128)(2,1)S(1)} %dynamic-slice_bitcast_fusion.2), channel_id=1, source_target_pairs={{0,16},{4,20},{8,24},{12,28},{16,0},{20,4},{24,8},{28,12},{1,17},{... | collective-permute-start | bytes 1769480 | tf_op jit(solution)/shard_map/ppermute | solution.py:59
  270.7 3.5 copy-start.10
  272.6 36.5 %collective-permute-start.12 = (bf16[96,3072]{1,0:T(8,128)(2,1)S(1)}, bf16[96,3072]{1,0:T(8,128)(2,1)S(1)}, u32[]{:S(2)}, u32[]{:S(2)}) collective-permute-start(bf16[96,3072]{1,0:T(8,128)(2,1)S(1)} %dynamic-slice_bitcast_fusion.3), channel_id=1, source_target_pairs={{0,16},{4,20},{8,24},{12,28},{16,0},{20,4},{24,8},{28,12},{1,17},{... | collective-permute-start | bytes 1769480 | tf_op jit(solution)/shard_map/ppermute | solution.py:59
  275.9 35.0 %collective-permute-start.7 = (bf16[96,3072]{1,0:T(8,128)(2,1)S(1)}, bf16[96,3072]{1,0:T(8,128)(2,1)S(1)}, u32[]{:S(2)}, u32[]{:S(2)}) collective-permute-start(bf16[96,3072]{1,0:T(8,128)(2,1)S(1)} %dynamic-slice_bitcast_fusion.4), channel_id=1, source_target_pairs={{0,8},{4,12},{8,0},{12,4},{16,24},{20,28},{24,16},{28,20},{1,9},{5... | collective-permute-start | bytes 1769480 | tf_op jit(solution)/shard_map/ppermute | solution.py:59
  284.1 27.6 %collective-permute-start.2 = (bf16[96,3072]{1,0:T(8,128)(2,1)S(1)}, bf16[96,3072]{1,0:T(8,128)(2,1)S(1)}, u32[]{:S(2)}, u32[]{:S(2)}) collective-permute-start(bf16[96,3072]{1,0:T(8,128)(2,1)S(1)} %dynamic-slice_bitcast_fusion.5), channel_id=1, source_target_pairs={{0,8},{4,12},{8,0},{12,4},{16,24},{20,28},{24,16},{28,20},{1,9},{5... | collective-permute-start | bytes 1769480 | tf_op jit(solution)/shard_map/ppermute | solution.py:59
  295.1 18.4 %collective-permute-start.18 = (bf16[192,768]{1,0:T(8,128)(2,1)S(1)}, bf16[192,768]{1,0:T(8,128)(2,1)S(1)}, u32[]{:S(2)}, u32[]{:S(2)}) collective-permute-start(bf16[192,768]{1,0:T(8,128)(2,1)S(1)} %bitcast.339), channel_id=1, source_target_pairs={{0,1},{1,0},{2,3},{3,2},{4,5},{5,4},{6,7},{7,6},{8,9},{9,8},{10,11... | collective-permute-start | bytes 884744 | tf_op jit(solution)/shard_map/ppermute | solution.py:59
  309.3 14.7 %collective-permute-start.13 = (bf16[48,3072]{1,0:T(8,128)(2,1)S(1)}, bf16[48,3072]{1,0:T(8,128)(2,1)S(1)}, u32[]{:S(2)}, u32[]{:S(2)}) collective-permute-start(bf16[48,3072]{1,0:T(8,128)(2,1)S(1)} %bitcast.340), channel_id=1, source_target_pairs={{0,1},{1,0},{2,3},{3,2},{4,5},{5,4},{6,7},{7,6},{8,9},{9,8},{10,11... | collective-permute-start | bytes 884744 | tf_op jit(solution)/shard_map/ppermute | solution.py:59
  311.1 27.3 %collective-permute-start.8 = (bf16[48,3072]{1,0:T(8,128)(2,1)S(1)}, bf16[48,3072]{1,0:T(8,128)(2,1)S(1)}, u32[]{:S(2)}, u32[]{:S(2)}) collective-permute-start(bf16[48,3072]{1,0:T(8,128)(2,1)S(1)} %bitcast.338), channel_id=1, source_target_pairs={{0,1},{1,0},{2,3},{3,2},{4,5},{5,4},{6,7},{7,6},{8,9},{9,8},{10,11... | collective-permute-start | bytes 884744 | tf_op jit(solution)/shard_map/ppermute | solution.py:59
  311.9 24.7 %collective-permute-start.3 = (bf16[48,3072]{1,0:T(8,128)(2,1)S(1)}, bf16[48,3072]{1,0:T(8,128)(2,1)S(1)}, u32[]{:S(2)}, u32[]{:S(2)}) collective-permute-start(bf16[48,3072]{1,0:T(8,128)(2,1)S(1)} %bitcast.341), channel_id=1, source_target_pairs={{0,1},{1,0},{2,3},{3,2},{4,5},{5,4},{6,7},{7,6},{8,9},{9,8},{10,11... | collective-permute-start | bytes 884744 | tf_op jit(solution)/shard_map/ppermute | solution.py:59
  313.6 35.6 %collective-permute-start.19 = (bf16[96,768]{1,0:T(8,128)(2,1)S(1)}, bf16[96,768]{1,0:T(8,128)(2,1)S(1)}, u32[]{:S(2)}, u32[]{:S(2)}) collective-permute-start(bf16[96,768]{1,0:T(8,128)(2,1)S(1)} %dynamic-slice_bitcast_fusion.6), channel_id=1, source_target_pairs={{0,2},{1,3},{2,0},{3,1},{4,6},{5,7},{6,4},{7,5},{8,10},{9,11},{10,... | collective-permute-start | bytes 442376 | tf_op jit(solution)/shard_map/ppermute | solution.py:59
  324.1 25.9 %collective-permute-start.14 = (bf16[24,3072]{1,0:T(8,128)(2,1)S(1)}, bf16[24,3072]{1,0:T(8,128)(2,1)S(1)}, u32[]{:S(2)}, u32[]{:S(2)}) collective-permute-start(bf16[24,3072]{1,0:T(8,128)(2,1)S(1)} %dynamic-slice_bitcast_fusion.7), channel_id=1, source_target_pairs={{0,2},{1,3},{2,0},{3,1},{4,6},{5,7},{6,4},{7,5},{8,10},{9,11},{10,... | collective-permute-start | bytes 442376 | tf_op jit(solution)/shard_map/ppermute | solution.py:59
  336.7 12.5 %collective-permute-start.4 = (bf16[24,3072]{1,0:T(8,128)(2,1)S(1)}, bf16[24,3072]{1,0:T(8,128)(2,1)S(1)}, u32[]{:S(2)}, u32[]{:S(2)}) collective-permute-start(bf16[24,3072]{1,0:T(8,128)(2,1)S(1)} %dynamic-slice_bitcast_fusion.9), channel_id=1, source_target_pairs={{0,2},{1,3},{2,0},{3,1},{4,6},{5,7},{6,4},{7,5},{8,10},{9,11},{10,... | collective-permute-start | bytes 442376 | tf_op jit(solution)/shard_map/ppermute | solution.py:59
  338.5 12.8 %collective-permute-start.9 = (bf16[24,3072]{1,0:T(8,128)(2,1)S(1)}, bf16[24,3072]{1,0:T(8,128)(2,1)S(1)}, u32[]{:S(2)}, u32[]{:S(2)}) collective-permute-start(bf16[24,3072]{1,0:T(8,128)(2,1)S(1)} %dynamic-slice_bitcast_fusion.8), channel_id=1, source_target_pairs={{0,2},{1,3},{2,0},{3,1},{4,6},{5,7},{6,4},{7,5},{8,10},{9,11},{10,... | collective-permute-start | bytes 442376 | tf_op jit(solution)/shard_map/ppermute | solution.py:59
  356.9 3.4 copy-start.52
  356.9 7.0 %copy-start.1 = (bf16[768,768]{1,0:T(8,128)(2,1)S(1)}, bf16[768,768]{1,0:T(8,128)(2,1)}, u32[]{:S(2)}) copy-start(bf16[768,768]{1,0:T(8,128)(2,1)} %param.24) | copy-start | bytes 3538948
  (26 other events, 37.8 us)
Sparse Core Ops, SparseCore 0:
  9.6 39.7 all-gather.5
  204.6 35.7 reduce-scatter.1
  253.4 56.3 all-gather.7

commit v2 on v1

--- a/solution.py
+++ b/solution.py
@@ -1,8 +1,11 @@
+import functools
 import math
 
 import jax
 import jax.numpy as jnp
 from jax import lax
+from jax.experimental import pallas as pl
+from jax.experimental.pallas import tpu as pltpu
 from jax.sharding import PartitionSpec as P
 
 highest = lax.Precision.HIGHEST
@@ -43,6 +46,176 @@
 
 def dot_tn(a, b):
     return lax.dot_general(a, b, (((0,), (0,)), ((), ())), preferred_element_type=f32)
+
+
+def pair_halves(values, head_size):
+    lane = lax.broadcasted_iota(jnp.int32, values.shape, 1)
+    zero = jnp.zeros_like(values)
+    return jnp.concatenate(
+        [jnp.where(lane < head_size, values, zero), jnp.where(lane >= head_size, values, zero)], axis=0
+    )
+
+
+def pair_diagonal(values, head_size, rows):
+    return jnp.concatenate([values[:head_size, :rows], values[head_size:, rows:]], axis=0).T
+
+
+def transposed_index(facts_ref, bins_ref, bin_count):
+    window = pl.program_id(0)
+    start = facts_ref[window]
+    offset = facts_ref[pl.num_programs(0)]
+    bins = bins_ref[0].T
+    key_first = lax.broadcasted_iota(jnp.int32, bins.shape, 0) < start
+    row_first = lax.broadcasted_iota(jnp.int32, bins.shape, 1) + offset < start
+    return bins + jnp.where(key_first == row_first, bin_count, 0)
+
+
+def pair_scores(pair, cols, q_ref, k_ref, table_ref, index_ref, head_scale, head_size):
+    q_pair = pair_halves(q_ref[:, cols] * head_scale, head_size)
+    k_pair = k_ref[:, cols]
+    scores = dot_nt(k_pair, q_pair)
+    index = index_ref[...]
+    biases = []
+    for head in range(2):
+        entries = jnp.broadcast_to(table_ref[pl.ds(2 * pair + head, 1), :], index.shape)
+        biases.append(jnp.take_along_axis(entries, index, axis=1, mode="promise_in_bounds"))
+    return (q_pair, k_pair, scores + jnp.concatenate(biases, axis=1))
+
+
+def attend_kernel(
+    head_size, bin_count, facts_ref, q_ref, k_ref, v_ref, bins_ref, table_ref, out_ref, log_ref, index_ref
+):
+    rows, width = q_ref.shape
+    head_scale = 1.0 / math.sqrt(head_size)
+    index_ref[...] = transposed_index(facts_ref, bins_ref, bin_count)
+
+    def one_pair(pair, carry):
+        cols = pl.ds(pl.multiple_of(pair * 2 * head_size, 2 * head_size), 2 * head_size)
+        _, _, scores = pair_scores(
+            pair, cols, q_ref, k_ref, table_ref, index_ref, head_scale, head_size
+        )
+        top = jnp.max(scores, axis=0, keepdims=True)
+        raised = jnp.exp(scores - top)
+        total = jnp.sum(raised, axis=0, keepdims=True)
+        probs = (raised * (1.0 / total)).astype(bf16)
+        mixed = dot(v_ref[:, cols].T, probs)
+        out_ref[:, cols] = pair_diagonal(mixed, head_size, rows).astype(bf16)
+        log_ref[0, pl.ds(pair, 1), :] = top + jnp.log(total)
+        return carry
+
+    lax.fori_loop(0, width // (2 * head_size), one_pair, 0)
+
+
+def attend_back_kernel(
+    head_size,
+    bin_count,
+    facts_ref,
+    q_ref,
+    k_ref,
+    v_ref,
+    bins_ref,
+    table_ref,
+    grad_ref,
+    log_ref,
+    grad_q_ref,
+    grad_kv_ref,
+    grad_scores_ref,
+    index_ref,
+):
+    rows, width = q_ref.shape
+    head_scale = 1.0 / math.sqrt(head_size)
+    index_ref[...] = transposed_index(facts_ref, bins_ref, bin_count)
+
+    def one_pair(pair, carry):
+        start = pl.multiple_of(pair * 2 * head_size, 2 * head_size)
+        cols = pl.ds(start, 2 * head_size)
+        v_cols = pl.ds(width + start, 2 * head_size)
+        q_pair, k_pair, scores = pair_scores(
+            pair, cols, q_ref, k_ref, table_ref, index_ref, head_scale, head_size
+        )
+        probs = jnp.exp(scores - log_ref[0, pl.ds(pair, 1), :])
+        g_pair = pair_halves(grad_ref[:, cols], head_size)
+        grad_kv_ref[:, v_cols] = dot(probs.astype(bf16), g_pair).astype(bf16)
+        grad_probs = dot_nt(v_ref[:, cols], g_pair)
+        delta = jnp.sum(probs * grad_probs, axis=0, keepdims=True)
+        grad_scores = (probs * (grad_probs - delta)).astype(bf16)
+        grad_kv_ref[:, cols] = dot(grad_scores, q_pair).astype(bf16)
+        grad_q = pair_diagonal(dot(k_pair.T, grad_scores), head_size, rows) * head_scale
+        grad_q_ref[:, cols] = grad_q.astype(bf16)
+        grad_scores_ref[0, 2 * pair] = grad_scores[:, :rows]
+        grad_scores_ref[0, 2 * pair + 1] = grad_scores[:, rows:]
+        return carry
+
+    lax.fori_loop(0, width // (2 * head_size), one_pair, 0)
+
+
+def attention_specs(rows, length, width, table_shape):
+    return [
+        pl.BlockSpec(memory_space=pltpu.SMEM),
+        pl.BlockSpec((rows, width), lambda w: (w, 0)),
+        pl.BlockSpec((length, width), lambda w: (w, 0)),
+        pl.BlockSpec((length, width), lambda w: (w, 1)),
+        pl.BlockSpec((1, rows, length), lambda w: (w, 0, 0)),
+        pl.BlockSpec(table_shape, lambda w: (0, 0)),
+    ]
+
+
+def attend(facts, queries, keys_values, bins, table, head_size):
+    windows, rows, length = bins.shape
+    width = queries.shape[1]
+    pairs = width // (2 * head_size)
+    return pl.pallas_call(
+        functools.partial(attend_kernel, head_size, table.shape[1] // 2),
+        grid=(windows,),
+        in_specs=attention_specs(rows, length, width, table.shape),
+        out_specs=[
+            pl.BlockSpec((rows, width), lambda w: (w, 0)),
+            pl.BlockSpec((1, pairs, 2 * rows), lambda w: (w, 0, 0)),
+        ],
+        out_shape=[
+            jax.ShapeDtypeStruct((windows * rows, width), bf16),
+            jax.ShapeDtypeStruct((windows, pairs, 2 * rows), f32),
+        ],
+        scratch_shapes=[pltpu.VMEM((length, rows), jnp.int32)],
+        cost_estimate=pl.CostEstimate(
+            flops=8 * windows * rows * length * width,
+            bytes_accessed=4 * windows * rows * length,
+            transcendentals=windows * rows * length * 2 * pairs,
+        ),
+        name="attend",
+    )(facts, queries, keys_values, keys_values, bins, table)
+
+
+def attend_back(facts, queries, keys_values, bins, table, grads, logs, head_size):
+    windows, rows, length = bins.shape
+    width = queries.shape[1]
+    pairs = width // (2 * head_size)
+    return pl.pallas_call(
+        functools.partial(attend_back_kernel, head_size, table.shape[1] // 2),
+        grid=(windows,),
+        in_specs=attention_specs(rows, length, width, table.shape)
+        + [
+            pl.BlockSpec((rows, width), lambda w: (w, 0)),
+            pl.BlockSpec((1, pairs, 2 * rows), lambda w: (w, 0, 0)),
+        ],
+        out_specs=[
+            pl.BlockSpec((rows, width), lambda w: (w, 0)),
+            pl.BlockSpec((length, 2 * width), lambda w: (w, 0)),
+            pl.BlockSpec((1, 2 * pairs, length, rows), lambda w: (w, 0, 0, 0)),
+        ],
+        out_shape=[
+            jax.ShapeDtypeStruct((windows * rows, width), bf16),
+            jax.ShapeDtypeStruct((windows * length, 2 * width), bf16),
+            jax.ShapeDtypeStruct((windows, 2 * pairs, length, rows), bf16),
+        ],
+        scratch_shapes=[pltpu.VMEM((length, rows), jnp.int32)],
+        cost_estimate=pl.CostEstimate(
+            flops=20 * windows * rows * length * width,
+            bytes_accessed=8 * windows * rows * length * pairs,
+            transcendentals=windows * rows * length * 2 * pairs,
+        ),
+        name="attend_back",
+    )(facts, queries, keys_values, keys_values, bins, table, grads, logs)
 
 
 def halving_steps(flip):
@@ -102,7 +275,6 @@
     length = distance_bins.shape[2]
     head_count = pair_weight.shape[1]
     head_size = width // head_count
-    head_scale = 1.0 / math.sqrt(head_size)
     table_rows = pair_table.shape[0]
     bin_count = table_rows // 2
     classes = class_table.shape[0]
@@ -118,9 +290,7 @@
     ) + time_embed(noise_times, width)
     cond_sig = jax.nn.sigmoid(pre_cond)
     condition = pre_cond * cond_sig
-    window_facts = lax.all_gather(
-        jnp.concatenate([pre_cond, class_onehot], axis=-1), "win", axis=0, tiled=True
-    )
+    window_facts = jnp.concatenate([pre_cond, class_onehot], axis=-1)
     ada_float = ada_weight.astype(f32)
     modulation = jnp.dot(condition, ada_float, precision=highest).reshape(windows, 6, width)
     shift_attn = modulation[:, 0][:, None, :]
@@ -130,13 +300,10 @@
     scale_ffn = modulation[:, 4][:, None, :]
     gate_ffn = modulation[:, 5][:, None, :]
     table_bias = dot(pair_table, pair_weight).astype(bf16)
-    row_pos = lax.axis_index("seq") * row_count + jnp.arange(row_count, dtype=jnp.int32)
-    key_pos = jnp.arange(length, dtype=jnp.int32)
-    row_first = row_pos[None, :] < chain_start[:, None]
-    key_first = key_pos[None, :] < chain_start[:, None]
-    pair_index = distance_bins + bin_count * (
-        row_first[:, :, None] == key_first[:, None, :]
-    ).astype(jnp.int32)
+    facts = jnp.concatenate(
+        [chain_start, jnp.full((1,), lax.axis_index("seq") * row_count, jnp.int32)]
+    )
+    table = table_bias.astype(f32).T
     tokens_float = tokens.astype(f32)
     normed_x, inv_x = layer_norm_parts(tokens_float)
     attn_in = (normed_x * (1.0 + scale_attn) + shift_attn).astype(bf16).reshape(total_rows, width)
@@ -146,29 +313,7 @@
     )
     queries = dot(attn_in, qkv_weight[:, :width]).astype(bf16)
     keys_values = dot(attn_in_all, qkv_weight[:, width:]).astype(bf16)
-    keys_all = keys_values[:, :width]
-    values_all = keys_values[:, width:]
-
-    def head_split(array, rows):
-        return array.reshape(windows, rows, head_count, head_size)
-
-    query_heads = head_split(queries, row_count)
-    key_heads = head_split(keys_all, length)
-    value_heads = head_split(values_all, length)
-    pair_onehot = (
-        pair_index[:, None, :, :] == jnp.arange(table_rows, dtype=jnp.int32)[None, :, None, None]
-    ).astype(bf16)
-    raw_scores = jnp.einsum("grhe,glhe->ghrl", query_heads, key_heads, preferred_element_type=f32)
-    pair_bias = jnp.einsum("kh,gkrl->ghrl", table_bias, pair_onehot, preferred_element_type=f32)
-    scores = raw_scores * head_scale + pair_bias
-    row_max = jnp.max(scores, axis=-1, keepdims=True)
-    exp_scores = jnp.exp(scores - row_max)
-    exp_total = jnp.sum(exp_scores, axis=-1, keepdims=True)
-    soft_probs = exp_scores / exp_total
-    probs_low = soft_probs.astype(bf16)
-    attn_mixed = jnp.einsum("ghrl,glhe->grhe", probs_low, value_heads, preferred_element_type=f32)
-    attn_mixed = attn_mixed.astype(bf16).reshape(total_rows, width)
-
+    attn_mixed, log_totals = attend(facts, queries, keys_values, distance_bins, table, head_size)
     attn_out = dot(attn_mixed, out_weight).reshape(windows, row_count, width)
     gate_attn_sig = jax.nn.sigmoid(gate_attn)
     hidden_state = tokens_float + gate_attn_sig * attn_out
@@ -203,28 +348,16 @@
     grad_out = dot_tn(attn_mixed, grad_attn_out).astype(bf16)
     grad_mixed = dot_nt(grad_attn_out, out_weight).astype(bf16)
 
-    grad_heads = head_split(grad_mixed, row_count)
-    grad_probs = jnp.einsum("grhe,glhe->ghrl", grad_heads, value_heads, preferred_element_type=f32)
-    grad_scores = (
-        soft_probs * (grad_probs - jnp.sum(soft_probs * grad_probs, axis=-1, keepdims=True))
+    grad_query, grad_kv, grad_scores = attend_back(
+        facts, queries, keys_values, distance_bins, table, grad_mixed, log_totals, head_size
+    )
+    row_first = lax.axis_index("seq") * row_count + jnp.arange(row_count)[None, None, :] < chain_start[:, None, None]
+    key_first = jnp.arange(length)[None, :, None] < chain_start[:, None, None]
+    index_back = jnp.swapaxes(distance_bins, 1, 2) + bin_count * (row_first == key_first).astype(jnp.int32)
+    pair_onehot = (
+        index_back[:, None, :, :] == jnp.arange(table_rows, dtype=jnp.int32)[None, :, None, None]
     ).astype(bf16)
-    grad_query = (
-        jnp.einsum("ghrl,glhe->grhe", grad_scores, key_heads, preferred_element_type=f32) * head_scale
-    )
-    grad_key = (
-        jnp.einsum("ghrl,grhe->glhe", grad_scores, query_heads, preferred_element_type=f32)
-        * head_scale
-    )
-    grad_value = jnp.einsum("ghrl,grhe->glhe", probs_low, grad_heads, preferred_element_type=f32)
-    grad_table = jnp.einsum("ghrl,gkrl->kh", grad_scores, pair_onehot, preferred_element_type=f32)
-    grad_query = grad_query.astype(bf16).reshape(total_rows, width)
-    grad_kv = jnp.concatenate(
-        [
-            grad_key.astype(bf16).reshape(windows * length, width),
-            grad_value.astype(bf16).reshape(windows * length, width),
-        ],
-        axis=-1,
-    )
+    grad_table = jnp.einsum("whji,wkji->kh", grad_scores, pair_onehot, preferred_element_type=f32)
     grad_in_part = dot_nt(grad_kv, qkv_weight[:, width:]).astype(bf16)
     grad_in_far = lax.psum_scatter(
         grad_in_part.reshape(windows, length, width), "seq", scatter_dimension=1, tiled=True
@@ -257,13 +390,16 @@
         ],
         axis=1,
     )
-    parts = jnp.concatenate([grad_mod.reshape(-1), grad_table.reshape(-1)])
+    parts = jnp.concatenate([grad_mod.reshape(-1), grad_table.reshape(-1), window_facts.reshape(-1)])
+    parts = jnp.pad(parts, (0, -parts.shape[0] % 1024))
     parts_all = lax.all_gather(parts, ("win", "seq"), axis=0)
     mod_size = windows * 6 * width
     mod_all = jnp.sum(
         parts_all[:, :mod_size].reshape(win_count, seq_count, windows, 6 * width), axis=1
     ).reshape(win_count * windows, 6 * width)
-    table_all = jnp.sum(parts_all[:, mod_size:], axis=0).reshape(table_rows, head_count)
+    table_end = mod_size + table_rows * head_count
+    table_all = jnp.sum(parts_all[:, mod_size:table_end], axis=0).reshape(table_rows, head_count)
+    window_facts = parts_all[::seq_count, table_end : table_end + windows * (width + classes)].reshape(win_count * windows, width + classes)
     pre_all = window_facts[:, :width]
     onehot_all = window_facts[:, width:]
     ada_rows = width // devices

time: 376 us -> 316 us (0.84)
  matrix products: 113 us -> 67.1 us
  local copies, waits for them, and re-layouts: 89.3 us -> 45.4 us
  waiting for transfers between devices: 77.6 us -> 104 us
  Pallas kernels: 0 us -> 26.1 us
  blocking collectives: 10.7 us -> 0 us
  other arithmetic: 42.9 us -> 35.6 us
  starting transfers between devices: 22.2 us -> 16.4 us
    dot_general x8 -> x1, matrix products: 57.6 us -> 9.34 us  [per_device(): jnp.einsum('whji,wkji->kh', grad_scores, pair_onehot, preferred_element_t...]
    pallas_call x0 -> x2, Pallas kernels: none -> 26.1 us  [the longest x1 13.4 us: attend_back(): pl.pallas_call(functools.partial(attend_back_kernel, head_size, table.sha...]
    all_gather x1, waiting for transfers between devices: 0.01 us -> 23.3 us  [per_device(): tokens_all = lax.all_gather(tokens, 'seq', axis=1, tiled=True)]
    convert_element_type x7 -> x0, local copies, waits for them, and re-layouts: 14.6 us -> none  [the longest x1 5.52 us: per_device(): grad_scores = (soft_probs * (grad_probs - jnp.sum(soft_probs * grad_probs...]
    unnamed x152 -> x94, local copies, waits for them, and re-layouts: 24 us -> 11 us
    ppermute x20, waiting for transfers between devices: 67.7 us -> 80.4 us  [exchange(): return lax.ppermute(values, axis, [(i, i ^ 1 << bit) for i in range(size)])]
    all_gather x1 -> x0, blocking collectives: 10.7 us -> none  [per_device(): lax.all_gather(jnp.concatenate([pre_cond, class_onehot], axis=-1), 'win',...]
    dot_general x1 -> x0, local copies, waits for them, and re-layouts: 9.29 us -> none  [per_device(): jnp.einsum('kh,gkrl->ghrl', table_bias, pair_onehot, preferred_element_ty...]
  transfers between devices with their start and end apart: 23 -> 23, of which waited for: 9 -> 12; matrix products, arithmetic and copies ran while one was open for 33% -> 29% of each run, Pallas kernels for 0% -> 0%
where the time goes in v2:
time: 316 us; the launch traced here: 310 us
  waiting for transfers between devices  104 us (33%)
  matrix products  67.1 us (21%)
  local copies, waits for them, and re-layouts  45.4 us (14%)
  other arithmetic  35.6 us (11%)
  Pallas kernels  26.1 us (8%)
  starting transfers between devices  16.4 us (5%)
  between operations  15 us (5%)
    ppermute x20, waiting for transfers between devices, exchange(): return lax.ppermute(values, axis, [(i, i ^ 1 << bit) for i in range(size)])  80.4 us
    all_gather x1, waiting for transfers between devices, per_device(): tokens_all = lax.all_gather(tokens, 'seq', axis=1, tiled=True)  23.3 us
    dot_general x7, matrix products, dot(): return jnp.dot(a, b, preferred_element_type=f32)  17.2 us
    dot_general x6, matrix products, dot_nt(): lax.dot_general(a, b, (((1,), (1,)), ((), ())), preferred_element_type=f32)  16.6 us
    ppermute x20, starting transfers between devices, exchange(): return lax.ppermute(values, axis, [(i, i ^ 1 << bit) for i in range(size)])  16.3 us
    convert_element_type x16, other arithmetic, reduce_owned(): current = current.astype(bf16)  13.9 us
    dot_general x6, matrix products, dot_tn(): lax.dot_general(a, b, (((0,), (0,)), ((), ())), preferred_element_type=f32)  13.6 us
    pallas_call x1, Pallas kernels, attend_back(): pl.pallas_call(functools.partial(attend_back_kernel, head_size, table.sha...  13.4 us
  transfers between devices with their start and end apart: 23, of which 12 were waited for; matrix products, arithmetic and copies ran while one was open for 29% of the time, Pallas kernels for 0%

profile of v2, /device:TPU:0, one launch (start us, length us, event | category | flops | bytes accessed | tf_op | source)
XLA Modules:
  0.0 310.0 jit_solution(9373577336586007671)
XLA Ops:
  12.8 5.9 %fusion.70 = f32[2,4608]{1,0:T(2,128)S(1)} fusion(bf16[768,4608]{1,0:T(8,128)(2,1)} %param.22, f32[2,768]{1,0:T(2,128)S(1)} %convolution_add_fusion.1), kind=kOutput, calls=%fused_computation.177 | convolution fusion | flops 84940800 | bytes 7120896 | tf_op jit(solution)/shard_map/dot_general | solution.py:295
  23.5 2.5 convolution_convert_fusion.8.q_ref
  26.0 23.3 %all-gather.4.cloned.1.call-done = bf16[2,512,768]{2,1,0:T(8,128)(2,1)} async-done(((bf16[2,128,768]{2,1,0:T(8,128)(2,1)}), bf16[2,512,768]{2,1,0:T(8,128)(2,1)}) %all-gather.4.cloned.1.call-update) | async-done | bytes 1572880 | tf_op jit(solution)/shard_map/all_gather | solution.py:286
  49.4 1.8 convert_reduce_fusion
  53.7 4.2 %convolution_convert_fusion.3.k_ref.v_ref = bf16[1024,1536]{1,0:T(8,128)(2,1)} fusion(bf16[1024,768]{1,0:T(8,128)(2,1)S(1)} %bitcast.252, bf16[768,2304]{1,0:T(8,128)(2,1)S(1)} %copy-done.27), kind=kOutput, calls=%fused_computation.17 | convolution fusion | flops 2417491968 | bytes 7077888 | tf_op jit(solution)/shard_map/dot_general | solution.py:40
  57.9 12.7 %attend.1 = (bf16[256,768]{1,0:T(8,128)(2,1)}, f32[2,6,256]{2,1,0:T(8,128)}) custom-call(s32[3]{0:T(128)} %pad_add_fusion.facts_ref, bf16[256,768]{1,0:T(8,128)(2,1)} %convolution_convert_fusion.8.q_ref, bf16[1024,1536]{1,0:T(8,128)(2,1)} %convolution_convert_fusion.3.k_ref.v_ref, bf16[1024,1536]{1,0:T(8,128)(2,1)} %convolution_convert_fusion.3.k_ref.v_ref, ...), custom_call_target="tpu_custom_call" | custom-call | flops 805306368 | bytes 524288 | tf_op jit(solution)/shard_map/attend/pallas_call | solution.py:167
  70.6 1.5 fusion.88
  72.7 3.9 %fusion.89 = f32[256,3072]{1,0:T(8,128)S(1)} fusion(bf16[256,768]{1,0:T(8,128)(2,1)S(1)} %bitcast.226, bf16[768,3072]{1,0:T(8,128)(2,1)} %param.27), kind=kOutput, calls=%fused_computation.227 | convolution fusion | flops 1207959552 | bytes 8257536 | tf_op jit(solution)/shard_map/dot_general | solution.py:40
  76.7 3.1 fusion.90
  79.8 3.9 %multiply_convert_fusion = (bf16[256,3072]{1,0:T(8,128)(2,1)S(1)}, bf16[256,3072]{1,0:T(8,128)(2,1)S(1)}, bf16[256,3072]{1,0:T(8,128)(2,1)S(1)}) fusion(f32[256,3072]{1,0:T(8,128)S(1)} %fusion.89, f32[256,3072]{1,0:T(8,128)} %fusion.90, bf16[256,768]{1,0:T(8,128)(2,1)S(1)} %bitcast.249, bf16[3072,768]{1,0:T(8,128)(2,1)S(1)} %bitcast.274), kind=kOutput, calls=%fused_computation.25 | convolution fusion | flops 1219756032 | bytes 16121856 | tf_op jit(solution)/shard_map/dot_general | solution.py:44
  83.8 1.4 fusion.92
  85.4 1.5 fusion.55
  87.8 1.4 fusion.91
  89.2 2.0 multiply_reduce_fusion
  91.2 1.3 convolution_convert_fusion.7.grad_ref
  92.5 1.6 convolution_convert_fusion.5
  94.0 13.4 %attend_back.1 = (bf16[256,768]{1,0:T(8,128)(2,1)}, bf16[1024,1536]{1,0:T(8,128)(2,1)}, bf16[2,12,512,128]{3,2,1,0:T(8,128)(2,1)}) custom-call(s32[3]{0:T(128)} %pad_add_fusion.facts_ref, bf16[256,768]{1,0:T(8,128)(2,1)} %convolution_convert_fusion.8.q_ref, bf16[1024,1536]{1,0:T(8,128)(2,1)} %convolution_convert_fusion.3.k_ref.v_ref, ...), custom_call_target="tpu_custom_call" | custom-call | flops 2013265920 | bytes 6291456 | tf_op jit(solution)/shard_map/attend_back/pallas_call | solution.py:193
  107.5 6.6 %fusion.20 = bf16[1024,768]{1,0:T(8,128)(2,1)} fusion(bf16[1024,1536]{1,0:T(8,128)(2,1)} %get-tuple-element.19, bf16[768,2304]{1,0:T(8,128)(2,1)} %param.23), kind=kOutput, calls=%fused_computation.41 | convolution fusion | flops 2416705536 | bytes 7077888 | tf_op jit(solution)/shard_map/dot_general | solution.py:44
  114.0 4.0 %convolution_convert_fusion.4 = bf16[768,1536]{1,0:T(8,128)(2,1)} fusion(bf16[1024,768]{1,0:T(8,128)(2,1)S(1)} %bitcast.253, bf16[1024,1536]{1,0:T(8,128)(2,1)S(1)} %copy-done.34), kind=kOutput, calls=%fused_computation.20 | convolution fusion | flops 2417098752 | bytes 7077888 | tf_op jit(solution)/shard_map/dot_general | solution.py:48
  118.1 3.6 %convolution_convert_fusion.2 = bf16[768,3072]{1,0:T(8,128)(2,1)} fusion(bf16[256,768]{1,0:T(8,128)(2,1)S(1)} %bitcast.228, bf16[256,3072]{1,0:T(8,128)(2,1)S(1)} %copy-done.16), kind=kOutput, calls=%fused_computation.5 | convolution fusion | flops 1210318848 | bytes 6684672 | tf_op jit(solution)/shard_map/dot_general | solution.py:48
  121.7 7.9 %copy.37 = bf16[2,12,512,128]{2,1,0,3:T(8,128)(2,1)} copy(bf16[2,12,512,128]{3,2,1,0:T(8,128)(2,1)} %get-tuple-element.20) | data formatting | bytes 6291456 | tf_op jit(solution)/shard_map/attend_back/pallas_call | solution.py:193
  129.6 1.6 convolution_convert_fusion.6
  131.2 1.6 copy.40
  132.8 2.3 pad_maximum_fusion
  135.1 2.7 constant_dynamic-slice_fusion.20
  139.2 9.3 %fusion.27 = f32[128,12]{1,0:T(8,128)S(1)} fusion(bf16[2,12,512,128]{2,1,0,3:T(8,128)(2,1)S(1)} %copy-done.12, s32[2,512,128]{1,0,2:T(2,128)S(1)} %copy-done.26), kind=kOutput, calls=%fused_computation.64 | convolution fusion | flops 419430400 | bytes 3676160 | tf_op jit(solution)/shard_map/whji,wkji->kh/dot_general | solution.py:360
  149.2 2.8 constant_dynamic-slice_fusion.16
  152.1 1.4 convolution_convert_fusion.1
  155.0 1.5 convolution_convert_fusion
  157.3 1.9 fusion.32
  159.3 2.6 fusion.5
  163.1 1.5 collective-permute-start.1
  169.7 1.5 collective-permute-start.11
  172.0 1.7 constant_dynamic-slice_fusion.4
  174.2 2.2 fusion.49
  177.6 1.3 constant_dynamic-update-slice_fusion.3
  178.9 1.3 constant_dynamic-update-slice_fusion.2
  180.2 1.3 constant_dynamic-update-slice_fusion.1
  181.5 1.3 constant_dynamic-update-slice_fusion
  182.7 1.4 reshape.458
  184.2 1.4 select_maximum_fusion
  187.0 1.8 fusion.48
  188.7 3.5 %collective-permute-done.1 = bf16[192,3072]{1,0:T(8,128)(2,1)} collective-permute-done((bf16[192,3072]{1,0:T(8,128)(2,1)}, bf16[192,3072]{1,0:T(8,128)(2,1)}, u32[]{:S(2)}, u32[]{:S(2)}) %collective-permute-start.1) | collective-permute-done | bytes 1179680 | tf_op jit(solution)/shard_map/ppermute | solution.py:232
  192.2 2.0 fusion.16
  194.3 1.5 collective-permute-start.2
  195.9 21.8 %collective-permute-done.6 = bf16[192,3072]{1,0:T(8,128)(2,1)} collective-permute-done((bf16[192,3072]{1,0:T(8,128)(2,1)}, bf16[192,3072]{1,0:T(8,128)(2,1)}, u32[]{:S(2)}, u32[]{:S(2)}) %collective-permute-start.6) | collective-permute-done | bytes 1179680 | tf_op jit(solution)/shard_map/ppermute | solution.py:232
  217.7 1.7 fusion.15
  219.5 1.5 collective-permute-start.7
  221.0 1.8 fusion.14
  222.8 1.5 collective-permute-start.12
  224.4 1.6 collective-permute-done.16
  226.0 2.0 fusion.13
  228.0 1.3 collective-permute-start.17
  229.3 12.2 %collective-permute-done.2 = bf16[96,3072]{1,0:T(8,128)(2,1)S(1)} collective-permute-done((bf16[96,3072]{1,0:T(8,128)(2,1)S(1)}, bf16[96,3072]{1,0:T(8,128)(2,1)S(1)}, u32[]{:S(2)}, u32[]{:S(2)}) %collective-permute-start.2) | collective-permute-done | bytes 589856 | tf_op jit(solution)/shard_map/ppermute | solution.py:232
  242.4 10.2 %collective-permute-done.7 = bf16[96,3072]{1,0:T(8,128)(2,1)S(1)} collective-permute-done((bf16[96,3072]{1,0:T(8,128)(2,1)S(1)}, bf16[96,3072]{1,0:T(8,128)(2,1)S(1)}, u32[]{:S(2)}, u32[]{:S(2)}) %collective-permute-start.7) | collective-permute-done | bytes 589856 | tf_op jit(solution)/shard_map/ppermute | solution.py:232
  253.8 1.4 collective-permute-start.13
  256.3 1.3 collective-permute-start.4
  257.6 9.9 %collective-permute-done.8 = bf16[48,3072]{1,0:T(8,128)(2,1)S(1)} collective-permute-done((bf16[48,3072]{1,0:T(8,128)(2,1)S(1)}, bf16[48,3072]{1,0:T(8,128)(2,1)S(1)}, u32[]{:S(2)}, u32[]{:S(2)}) %collective-permute-start.8) | collective-permute-done | bytes 294944 | tf_op jit(solution)/shard_map/ppermute | solution.py:232
  267.7 7.8 %collective-permute-done.13 = bf16[48,3072]{1,0:T(8,128)(2,1)S(1)} collective-permute-done((bf16[48,3072]{1,0:T(8,128)(2,1)S(1)}, bf16[48,3072]{1,0:T(8,128)(2,1)S(1)}, u32[]{:S(2)}, u32[]{:S(2)}) %collective-permute-start.13) | collective-permute-done | bytes 294944 | tf_op jit(solution)/shard_map/ppermute | solution.py:232
  275.7 4.2 %collective-permute-done.18 = bf16[192,768]{1,0:T(8,128)(2,1)S(1)} collective-permute-done((bf16[192,768]{1,0:T(8,128)(2,1)S(1)}, bf16[192,768]{1,0:T(8,128)(2,1)S(1)}, u32[]{:S(2)}, u32[]{:S(2)}) %collective-permute-start.18) | collective-permute-done | bytes 294944 | tf_op jit(solution)/shard_map/ppermute | solution.py:232
  281.6 5.7 %collective-permute-done.9 = bf16[24,3072]{1,0:T(8,128)(2,1)S(1)} collective-permute-done((bf16[24,3072]{1,0:T(8,128)(2,1)S(1)}, bf16[24,3072]{1,0:T(8,128)(2,1)S(1)}, u32[]{:S(2)}, u32[]{:S(2)}) %collective-permute-start.9) | collective-permute-done | bytes 147488 | tf_op jit(solution)/shard_map/ppermute | solution.py:232
  288.1 2.4 collective-permute-done.14
  293.2 1.6 reshape.533
  299.6 2.5 fusion.31
  (218 shorter events, 44.0 us)
Async XLA Ops:
  7.2 63.4 %copy-start = (bf16[768,768]{1,0:T(8,128)(2,1)S(1)}, bf16[768,768]{1,0:T(8,128)(2,1)}, u32[]{:S(2)}) copy-start(bf16[768,768]{1,0:T(8,128)(2,1)} %param.24) | copy-start | bytes 3538948
  7.2 42.2 %all-gather.4.cloned.1.call-start = ((), (), s32[]{:S(2)}) async-start(), calls=%async_computation.1 | async-start | bytes 1966080 | tf_op jit(solution)/shard_map/all_gather | solution.py:286
  7.9 166.3 %reduce-scatter.2.cloned.1.call-start = ((), (), s32[]{:S(2)}) async-start(), calls=%async_computation.2 | async-start | bytes 1966080 | tf_op jit(solution)/shard_map/reduce_scatter | solution.py:362
  9.8 12.7 %copy-start.31 = (f32[2,128]{1,0:T(2,128)}, f32[2,128]{1,0:T(2,128)S(1)}, u32[]{:S(2)}) copy-start(f32[2,128]{1,0:T(2,128)S(1)} %broadcast_multiply_fusion.5) | copy-start | bytes 3076
  12.8 6.0 %copy-start.33 = (s32[2]{0:T(128)S(1)}, s32[2]{0:T(128)}, u32[]{:S(2)}) copy-start(s32[2]{0:T(128)} %param.19) | copy-start | bytes 28
  12.8 6.1 %copy-start.11 = (s32[2,128,512]{2,1,0:T(8,128)S(1)}, s32[2,128,512]{2,1,0:T(8,128)}, u32[]{:S(2)}) copy-start(s32[2,128,512]{2,1,0:T(8,128)} %bins_ref.3) | copy-start | bytes 1572868
  18.7 3.0 copy-start.28
  18.7 3.0 copy-start.30
  18.7 3.7 %copy-start.19 = (bf16[2,128,768]{2,1,0:T(8,128)(2,1)S(1)}, bf16[2,128,768]{2,1,0:T(8,128)(2,1)}, u32[]{:S(2)}) copy-start(bf16[2,128,768]{2,1,0:T(8,128)(2,1)} %param.16) | copy-start | bytes 1179652
  18.7 3.8 %copy-start.2 = (bf16[2,128,768]{2,1,0:T(8,128)(2,1)S(1)}, bf16[2,128,768]{2,1,0:T(8,128)(2,1)}, u32[]{:S(2)}) copy-start(bf16[2,128,768]{2,1,0:T(8,128)(2,1)} %param.15) | copy-start | bytes 1179652
  21.5 29.6 %copy-start.32 = (f32[2,128]{1,0:T(2,128)}, f32[2,128]{1,0:T(2,128)S(1)}, u32[]{:S(2)}) copy-start(f32[2,128]{1,0:T(2,128)S(1)} %add_rsqrt_fusion.2) | copy-start | bytes 3076
  22.8 0.7 copy-start.24
  49.4 1.9 copy-start.3
  51.2 2.5 copy-start.27
  52.5 1.2 copy-start.17
  72.5 4.1 %slice-start = ((s8[4718592]{0:T(1024)(128)(4,1)}), s8[4194304]{0:T(1024)(128)(4,1)S(1)}, s32[]{:S(2)}) async-start(s8[4718592]{0:T(1024)(128)(4,1)} %bitcast.234), calls=%async_computation.4 | async-start | bytes 8388608
  72.7 3.9 %slice-start.1 = ((s8[4718592]{0:T(1024)(128)(4,1)}), s8[524288]{0:T(1024)(128)(4,1)S(1)}, s32[]{:S(2)}) async-start(s8[4718592]{0:T(1024)(128)(4,1)} %bitcast.234), calls=%async_computation.5 | async-start | bytes 1048576
  72.7 7.0 %slice-start.4 = ((s8[4718592]{0:T(1024)(128)(4,1)}), s8[4194304]{0:T(1024)(128)(4,1)S(1)}, s32[]{:S(2)}) async-start(s8[4718592]{0:T(1024)(128)(4,1)} %bitcast.273), calls=%async_computation.8 | async-start | bytes 8388608
  76.7 3.1 %slice-start.5 = ((s8[4718592]{0:T(1024)(128)(4,1)}), s8[524288]{0:T(1024)(128)(4,1)S(1)}, s32[]{:S(2)}) async-start(s8[4718592]{0:T(1024)(128)(4,1)} %bitcast.273), calls=%async_computation.9 | async-start | bytes 1048576
  76.7 7.1 %slice-start.2 = ((s8[4718592]{0:T(1024)(128)(4,1)}), s8[4194304]{0:T(1024)(128)(4,1)S(1)}, s32[]{:S(2)}) async-start(s8[4718592]{0:T(1024)(128)(4,1)} %bitcast.271), calls=%async_computation.6 | async-start | bytes 8388608
  79.8 4.0 %slice-start.3 = ((s8[4718592]{0:T(1024)(128)(4,1)}), s8[524288]{0:T(1024)(128)(4,1)S(1)}, s32[]{:S(2)}) async-start(s8[4718592]{0:T(1024)(128)(4,1)} %bitcast.271), calls=%async_computation.7 | async-start | bytes 1048576
  83.7 1.5 copy-start.15
  83.7 1.6 copy-start.8
  83.7 4.1 %copy-start.13 = (bf16[256,3072]{1,0:T(8,128)(2,1)}, bf16[256,3072]{1,0:T(8,128)(2,1)S(1)}, u32[]{:S(2)}) copy-start(bf16[256,3072]{1,0:T(8,128)(2,1)S(1)} %get-tuple-element.40) | copy-start | bytes 4718596
  87.8 1.4 copy-start.20
  91.1 1.3 copy-start.23
  107.5 6.6 %copy-start.18 = (bf16[2,512,768]{2,1,0:T(8,128)(2,1)S(1)}, bf16[2,512,768]{2,1,0:T(8,128)(2,1)}, u32[]{:S(2)}) copy-start(bf16[2,512,768]{2,1,0:T(8,128)(2,1)} %copy-done.17) | copy-start | bytes 4718596
  107.5 6.6 %copy-start.34 = (bf16[1024,1536]{1,0:T(8,128)(2,1)S(1)}, bf16[1024,1536]{1,0:T(8,128)(2,1)}, u32[]{:S(2)}) copy-start(bf16[1024,1536]{1,0:T(8,128)(2,1)} %get-tuple-element.19) | copy-start | bytes 9437188
  114.0 4.0 %copy-start.16 = (bf16[256,3072]{1,0:T(8,128)(2,1)S(1)}, bf16[256,3072]{1,0:T(8,128)(2,1)}, u32[]{:S(2)}) copy-start(bf16[256,3072]{1,0:T(8,128)(2,1)} %copy-done.15) | copy-start | bytes 4718596
  121.7 171.5 %all-gather.6.cloned.1.call-start = ((), (), s32[]{:S(2)}) async-start(), calls=%async_computation.3 | async-start | bytes 1757184 | tf_op jit(solution)/shard_map/all_gather | solution.py:395
  121.7 7.9 %copy-start.22 = (bf16[256,768]{1,0:T(8,128)(2,1)S(1)}, bf16[256,768]{1,0:T(8,128)(2,1)}, u32[]{:S(2)}) copy-start(bf16[256,768]{1,0:T(8,128)(2,1)} %get-tuple-element.18) | copy-start | bytes 1179652
  121.7 7.9 %copy-start.25 = (bf16[2,128,768]{2,1,0:T(8,128)(2,1)S(1)}, bf16[2,128,768]{2,1,0:T(8,128)(2,1)}, u32[]{:S(2)}) copy-start(bf16[2,128,768]{2,1,0:T(8,128)(2,1)} %copy-done.24) | copy-start | bytes 1179652
  135.1 3.9 %copy-start.12 = (bf16[2,12,512,128]{2,1,0,3:T(8,128)(2,1)S(1)}, bf16[2,12,512,128]{2,1,0,3:T(8,128)(2,1)}, u32[]{:S(2)}) copy-start(bf16[2,12,512,128]{2,1,0,3:T(8,128)(2,1)} %copy.37) | copy-start | bytes 9437188
  135.1 4.0 %copy-start.26 = (s32[2,512,128]{1,0,2:T(2,128)S(1)}, s32[2,512,128]{1,0,2:T(2,128)}, u32[]{:S(2)}) copy-start(s32[2,512,128]{1,0,2:T(2,128)} %copy.36) | copy-start | bytes 1572868
  137.9 21.4 %collective-permute-start = (bf16[384,3072]{1,0:T(8,128)(2,1)}, bf16[384,3072]{1,0:T(8,128)(2,1)}, u32[]{:S(2)}, u32[]{:S(2)}) collective-permute-start(bf16[384,3072]{1,0:T(8,128)(2,1)} %bitcast.17), channel_id=1, source_target_pairs={{0,4},{4,0},{8,12},{12,8},{16,20},{20,16},{24,28},{28,24},{1,5},{5... | collective-permute-start | bytes 7077896 | tf_op jit(solution)/shard_map/ppermute | solution.py:232
  149.2 2.9 copy-start.9
  152.0 12.5 %collective-permute-start.5 = (bf16[384,3072]{1,0:T(8,128)(2,1)S(1)}, bf16[384,3072]{1,0:T(8,128)(2,1)S(1)}, u32[]{:S(2)}, u32[]{:S(2)}) collective-permute-start(bf16[384,3072]{1,0:T(8,128)(2,1)S(1)} %bitcast.244), channel_id=1, source_target_pairs={{0,4},{4,0},{8,12},{12,8},{16,20},{20,16},{24,28},{28,24},{1,5},{5... | collective-permute-start | bytes 7077896 | tf_op jit(solution)/shard_map/ppermute | solution.py:232
  153.6 1.4 copy-start.14
  153.9 13.5 %collective-permute-start.10 = (bf16[384,3072]{1,0:T(8,128)(2,1)S(1)}, bf16[384,3072]{1,0:T(8,128)(2,1)S(1)}, u32[]{:S(2)}, u32[]{:S(2)}) collective-permute-start(bf16[384,3072]{1,0:T(8,128)(2,1)S(1)} %bitcast.243), channel_id=1, source_target_pairs={{0,4},{4,0},{8,12},{12,8},{16,20},{20,16},{24,28},{28,24},{1,5},{5... | collective-permute-start | bytes 7077896 | tf_op jit(solution)/shard_map/ppermute | solution.py:232
  156.8 2.5 copy-start.4
  156.8 14.3 %collective-permute-start.15 = (bf16[1536,768]{1,0:T(8,128)(2,1)S(1)}, bf16[1536,768]{1,0:T(8,128)(2,1)S(1)}, u32[]{:S(2)}, u32[]{:S(2)}) collective-permute-start(bf16[1536,768]{1,0:T(8,128)(2,1)S(1)} %bitcast.242), channel_id=1, source_target_pairs={{0,4},{4,0},{8,12},{12,8},{16,20},{20,16},{24,28},{28,24},{1,5},{5... | collective-permute-start | bytes 7077896 | tf_op jit(solution)/shard_map/ppermute | solution.py:232
  161.9 3.7 %copy-start.5 = (bf16[384,3072]{1,0:T(8,128)(2,1)}, bf16[384,3072]{1,0:T(8,128)(2,1)S(1)}, u32[]{:S(2)}) copy-start(bf16[384,3072]{1,0:T(8,128)(2,1)S(1)} %fusion.5) | copy-start | bytes 7077892
  163.1 29.2 %collective-permute-start.1 = (bf16[192,3072]{1,0:T(8,128)(2,1)}, bf16[192,3072]{1,0:T(8,128)(2,1)}, u32[]{:S(2)}, u32[]{:S(2)}) collective-permute-start(bf16[192,3072]{1,0:T(8,128)(2,1)} %dynamic-slice_bitcast_fusion.1), channel_id=1, source_target_pairs={{0,16},{4,20},{8,24},{12,28},{16,0},{20,4},{24,8},{28,12},{1,17},{... | collective-permute-start | bytes 3538952 | tf_op jit(solution)/shard_map/ppermute | solution.py:232
  165.6 2.8 copy-start.6
  166.8 50.9 %collective-permute-start.6 = (bf16[192,3072]{1,0:T(8,128)(2,1)}, bf16[192,3072]{1,0:T(8,128)(2,1)}, u32[]{:S(2)}, u32[]{:S(2)}) collective-permute-start(bf16[192,3072]{1,0:T(8,128)(2,1)} %dynamic-slice_bitcast_fusion), channel_id=1, source_target_pairs={{0,16},{4,20},{8,24},{12,28},{16,0},{20,4},{24,8},{28,12},{1,17},{... | collective-permute-start | bytes 3538952 | tf_op jit(solution)/shard_map/ppermute | solution.py:232
  169.7 51.4 %collective-permute-start.11 = (bf16[192,3072]{1,0:T(8,128)(2,1)}, bf16[192,3072]{1,0:T(8,128)(2,1)}, u32[]{:S(2)}, u32[]{:S(2)}) collective-permute-start(bf16[192,3072]{1,0:T(8,128)(2,1)} %bitcast.51), channel_id=1, source_target_pairs={{0,8},{4,12},{8,0},{12,4},{16,24},{20,28},{24,16},{28,20},{1,9},{5... | collective-permute-start | bytes 3538952 | tf_op jit(solution)/shard_map/ppermute | solution.py:232
  173.7 52.3 %collective-permute-start.16 = (bf16[768,768]{1,0:T(8,128)(2,1)}, bf16[768,768]{1,0:T(8,128)(2,1)}, u32[]{:S(2)}, u32[]{:S(2)}) collective-permute-start(bf16[768,768]{1,0:T(8,128)(2,1)} %bitcast.66), channel_id=1, source_target_pairs={{0,8},{4,12},{8,0},{12,4},{16,24},{20,28},{24,16},{28,20},{1,9},{5... | collective-permute-start | bytes 3538952 | tf_op jit(solution)/shard_map/ppermute | solution.py:232
  174.2 12.7 %copy-start.21 = (bf16[2,128,768]{2,1,0:T(8,128)(2,1)S(1)}, bf16[2,128,768]{2,1,0:T(8,128)(2,1)}, u32[]{:S(2)}) copy-start(bf16[2,128,768]{2,1,0:T(8,128)(2,1)} %reduce-scatter.2.cloned.1.call-done) | copy-start | bytes 1179652
  188.7 29.0 %copy-start.7 = (bf16[384,3072]{1,0:T(8,128)(2,1)S(1)}, bf16[384,3072]{1,0:T(8,128)(2,1)}, u32[]{:S(2)}) copy-start(bf16[384,3072]{1,0:T(8,128)(2,1)} %copy-done.6) | copy-start | bytes 7077892
  194.3 47.2 %collective-permute-start.2 = (bf16[96,3072]{1,0:T(8,128)(2,1)S(1)}, bf16[96,3072]{1,0:T(8,128)(2,1)S(1)}, u32[]{:S(2)}, u32[]{:S(2)}) collective-permute-start(bf16[96,3072]{1,0:T(8,128)(2,1)S(1)} %dynamic-slice_bitcast_fusion.5), channel_id=1, source_target_pairs={{0,8},{4,12},{8,0},{12,4},{16,24},{20,28},{24,16},{28,20},{1,9},{5... | collective-permute-start | bytes 1769480 | tf_op jit(solution)/shard_map/ppermute | solution.py:232
  219.5 33.2 %collective-permute-start.7 = (bf16[96,3072]{1,0:T(8,128)(2,1)S(1)}, bf16[96,3072]{1,0:T(8,128)(2,1)S(1)}, u32[]{:S(2)}, u32[]{:S(2)}) collective-permute-start(bf16[96,3072]{1,0:T(8,128)(2,1)S(1)} %dynamic-slice_bitcast_fusion.4), channel_id=1, source_target_pairs={{0,8},{4,12},{8,0},{12,4},{16,24},{20,28},{24,16},{28,20},{1,9},{5... | collective-permute-start | bytes 1769480 | tf_op jit(solution)/shard_map/ppermute | solution.py:232
  221.0 5.0 %copy-start.10 = (bf16[2,1,384,768]{3,2,1,0:T(8,128)(2,1)S(1)}, bf16[2,1,384,768]{3,2,1,0:T(8,128)(2,1)}, u32[]{:S(2)}) copy-start(bf16[2,1,384,768]{3,2,1,0:T(8,128)(2,1)} %get-tuple-element.49) | copy-start | bytes 3538948
  222.8 30.7 %collective-permute-start.12 = (bf16[96,3072]{1,0:T(8,128)(2,1)S(1)}, bf16[96,3072]{1,0:T(8,128)(2,1)S(1)}, u32[]{:S(2)}, u32[]{:S(2)}) collective-permute-start(bf16[96,3072]{1,0:T(8,128)(2,1)S(1)} %dynamic-slice_bitcast_fusion.3), channel_id=1, source_target_pairs={{0,16},{4,20},{8,24},{12,28},{16,0},{20,4},{24,8},{28,12},{1,17},{... | collective-permute-start | bytes 1769480 | tf_op jit(solution)/shard_map/ppermute | solution.py:232
  228.0 27.2 %collective-permute-start.17 = (bf16[384,768]{1,0:T(8,128)(2,1)S(1)}, bf16[384,768]{1,0:T(8,128)(2,1)S(1)}, u32[]{:S(2)}, u32[]{:S(2)}) collective-permute-start(bf16[384,768]{1,0:T(8,128)(2,1)S(1)} %dynamic-slice_bitcast_fusion.2), channel_id=1, source_target_pairs={{0,16},{4,20},{8,24},{12,28},{16,0},{20,4},{24,8},{28,12},{1,17},{... | collective-permute-start | bytes 1769480 | tf_op jit(solution)/shard_map/ppermute | solution.py:232
  241.7 14.5 %collective-permute-start.3 = (bf16[48,3072]{1,0:T(8,128)(2,1)S(1)}, bf16[48,3072]{1,0:T(8,128)(2,1)S(1)}, u32[]{:S(2)}, u32[]{:S(2)}) collective-permute-start(bf16[48,3072]{1,0:T(8,128)(2,1)S(1)} %bitcast.266), channel_id=1, source_target_pairs={{0,1},{1,0},{2,3},{3,2},{4,5},{5,4},{6,7},{7,6},{8,9},{9,8},{10,11... | collective-permute-start | bytes 884744 | tf_op jit(solution)/shard_map/ppermute | solution.py:232
  252.8 14.7 %collective-permute-start.8 = (bf16[48,3072]{1,0:T(8,128)(2,1)S(1)}, bf16[48,3072]{1,0:T(8,128)(2,1)S(1)}, u32[]{:S(2)}, u32[]{:S(2)}) collective-permute-start(bf16[48,3072]{1,0:T(8,128)(2,1)S(1)} %bitcast.267), channel_id=1, source_target_pairs={{0,1},{1,0},{2,3},{3,2},{4,5},{5,4},{6,7},{7,6},{8,9},{9,8},{10,11... | collective-permute-start | bytes 884744 | tf_op jit(solution)/shard_map/ppermute | solution.py:232
  253.8 21.7 %collective-permute-start.13 = (bf16[48,3072]{1,0:T(8,128)(2,1)S(1)}, bf16[48,3072]{1,0:T(8,128)(2,1)S(1)}, u32[]{:S(2)}, u32[]{:S(2)}) collective-permute-start(bf16[48,3072]{1,0:T(8,128)(2,1)S(1)} %bitcast.268), channel_id=1, source_target_pairs={{0,1},{1,0},{2,3},{3,2},{4,5},{5,4},{6,7},{7,6},{8,9},{9,8},{10,11... | collective-permute-start | bytes 884744 | tf_op jit(solution)/shard_map/ppermute | solution.py:232
  255.4 24.5 %collective-permute-start.18 = (bf16[192,768]{1,0:T(8,128)(2,1)S(1)}, bf16[192,768]{1,0:T(8,128)(2,1)S(1)}, u32[]{:S(2)}, u32[]{:S(2)}) collective-permute-start(bf16[192,768]{1,0:T(8,128)(2,1)S(1)} %bitcast.269), channel_id=1, source_target_pairs={{0,1},{1,0},{2,3},{3,2},{4,5},{5,4},{6,7},{7,6},{8,9},{9,8},{10,11... | collective-permute-start | bytes 884744 | tf_op jit(solution)/shard_map/ppermute | solution.py:232
  256.3 23.8 %collective-permute-start.4 = (bf16[24,3072]{1,0:T(8,128)(2,1)S(1)}, bf16[24,3072]{1,0:T(8,128)(2,1)S(1)}, u32[]{:S(2)}, u32[]{:S(2)}) collective-permute-start(bf16[24,3072]{1,0:T(8,128)(2,1)S(1)} %dynamic-slice_bitcast_fusion.9), channel_id=1, source_target_pairs={{0,2},{1,3},{2,0},{3,1},{4,6},{5,7},{6,4},{7,5},{8,10},{9,11},{10,... | collective-permute-start | bytes 442376 | tf_op jit(solution)/shard_map/ppermute | solution.py:232
  267.6 19.6 %collective-permute-start.9 = (bf16[24,3072]{1,0:T(8,128)(2,1)S(1)}, bf16[24,3072]{1,0:T(8,128)(2,1)S(1)}, u32[]{:S(2)}, u32[]{:S(2)}) collective-permute-start(bf16[24,3072]{1,0:T(8,128)(2,1)S(1)} %dynamic-slice_bitcast_fusion.8), channel_id=1, source_target_pairs={{0,2},{1,3},{2,0},{3,1},{4,6},{5,7},{6,4},{7,5},{8,10},{9,11},{10,... | collective-permute-start | bytes 442376 | tf_op jit(solution)/shard_map/ppermute | solution.py:232
  275.6 14.8 %collective-permute-start.14 = (bf16[24,3072]{1,0:T(8,128)(2,1)S(1)}, bf16[24,3072]{1,0:T(8,128)(2,1)S(1)}, u32[]{:S(2)}, u32[]{:S(2)}) collective-permute-start(bf16[24,3072]{1,0:T(8,128)(2,1)S(1)} %dynamic-slice_bitcast_fusion.7), channel_id=1, source_target_pairs={{0,2},{1,3},{2,0},{3,1},{4,6},{5,7},{6,4},{7,5},{8,10},{9,11},{10,... | collective-permute-start | bytes 442376 | tf_op jit(solution)/shard_map/ppermute | solution.py:232
  280.1 12.3 %collective-permute-start.19 = (bf16[96,768]{1,0:T(8,128)(2,1)S(1)}, bf16[96,768]{1,0:T(8,128)(2,1)S(1)}, u32[]{:S(2)}, u32[]{:S(2)}) collective-permute-start(bf16[96,768]{1,0:T(8,128)(2,1)S(1)} %dynamic-slice_bitcast_fusion.6), channel_id=1, source_target_pairs={{0,2},{1,3},{2,0},{3,1},{4,6},{5,7},{6,4},{7,5},{8,10},{9,11},{10,... | collective-permute-start | bytes 442376 | tf_op jit(solution)/shard_map/ppermute | solution.py:232
  294.8 0.8 copy-start.29
  296.8 6.5 %copy-start.1 = (bf16[768,768]{1,0:T(8,128)(2,1)S(1)}, bf16[768,768]{1,0:T(8,128)(2,1)}, u32[]{:S(2)}) copy-start(bf16[768,768]{1,0:T(8,128)(2,1)} %param.24) | copy-start | bytes 3538948
Sparse Core Ops, SparseCore 0:
  9.6 39.7 all-gather.3
  121.8 34.3 reduce-scatter.1
  185.7 57.6 all-gather.5

commit v3 on v2

--- a/solution.py
+++ b/solution.py
@@ -218,40 +218,283 @@
     )(facts, queries, keys_values, keys_values, bins, table, grads, logs)
 
 
-def halving_steps(flip):
+def bit_steps():
     win_bits = int(math.log2(lax.axis_size("win")))
     seq_bits = int(math.log2(lax.axis_size("seq")))
-    far = list(range(1, win_bits))
-    if flip:
-        far = far[::-1]
-    return [("win", bit) for bit in [0] + far] + [("seq", bit) for bit in range(seq_bits)]
-
-
-def exchange(values, axis, bit):
-    size = lax.axis_size(axis)
-    return lax.ppermute(values, axis, [(i, i ^ (1 << bit)) for i in range(size)])
-
-
-def reduce_owned(grad, flip):
-    win_bits = int(math.log2(lax.axis_size("win")))
-    seq_bits = int(math.log2(lax.axis_size("seq")))
-    columns = grad.shape[1]
-    names = [("win", bit) for bit in range(win_bits)[::-1]] + [("seq", bit) for bit in range(seq_bits)[::-1]]
-    current = grad
-    for step in halving_steps(flip):
-        at = names.index(step)
-        before = 2**at
-        rows = current.shape[0]
-        view = current.reshape(before, 2, rows // (2 * before), columns)
-        mine = (lax.axis_index(step[0]) >> step[1]) & 1
-        send = lax.dynamic_index_in_dim(view, 1 - mine, 1, keepdims=False).astype(bf16)
-        got = exchange(send.reshape(rows // 2, columns), *step)
-        keep = lax.dynamic_index_in_dim(view, mine, 1, keepdims=False).reshape(rows // 2, columns)
-        current = keep.astype(f32) + got.astype(f32)
-        names.remove(step)
-        if names:
-            current = current.astype(bf16)
-    return current
+    return [("win", bit) for bit in range(win_bits)[::-1]] + [
+        ("seq", bit) for bit in range(seq_bits)[::-1]
+    ]
+
+
+CORE = ("win", 0)
+
+
+def my_bit(step):
+    return lax.rem(lax.axis_index(step[0]) // (1 << step[1]), 2)
+
+
+def partner(step):
+    return {step[0]: lax.axis_index(step[0]) + (1 - 2 * my_bit(step)) * (1 << step[1])}
+
+
+def greet():
+    barrier = pltpu.get_barrier_semaphore()
+    for step in bit_steps():
+        pl.semaphore_signal(barrier, inc=1, device_id=partner(step), device_id_type=pl.DeviceIdType.MESH)
+    pl.semaphore_wait(barrier, len(bit_steps()))
+
+
+def remote(source, target, send_sem, recv_sem, step):
+    return pltpu.make_async_remote_copy(
+        src_ref=source,
+        dst_ref=target,
+        send_sem=send_sem,
+        recv_sem=recv_sem,
+        device_id=partner(step),
+        device_id_type=pl.DeviceIdType.MESH,
+    )
+
+
+def each_block(shape, body):
+    lead = shape[:-2]
+    count = math.prod(lead)
+
+    def one(flat, carry):
+        index = []
+        for size in lead[::-1]:
+            index.append(lax.rem(flat, size))
+            flat = flat // size
+        body(tuple(index[::-1]))
+        return carry
+
+    if count == 1:
+        body((0,) * len(lead))
+    else:
+        lax.fori_loop(0, count, one, 0)
+
+
+class Flow:
+    def __init__(self, rows, columns, chunks, flip):
+        steps = bit_steps()
+        win_steps = [step for step in steps if step[0] == "win" and step != CORE]
+        self.seq_steps = [step for step in steps if step[0] == "seq"]
+        self.far = win_steps if flip else win_steps[::-1]
+        self.names = win_steps
+        self.near = self.seq_steps[::-1]
+        self.chunks = chunks
+        self.width = columns // chunks
+        self.share = rows // 2 ** len(steps)
+        self.block = self.share * 2 ** len(self.seq_steps)
+        self.columns = columns
+
+    def view(self, grad):
+        return grad.reshape((2,) * (len(self.far) + 1) + (self.block, self.columns))
+
+    def scratch(self):
+        chunks, width = (self.chunks, self.width)
+        far, near = (len(self.far), len(self.near))
+        shapes = [(2,) * far + (self.block, width)] * 2
+        shapes += [(2,) * (far - 1 - i) + (self.block, width) for i in range(far)]
+        shapes += [(2,) * near + (self.share, width)]
+        shapes += [(2,) * (near - 1 - i) + (self.share, width) for i in range(near)]
+        buffers = [pltpu.VMEM((chunks,) + shape, bf16) for shape in shapes]
+        count = 1 + far + near
+        return buffers + [
+            pltpu.SemaphoreType.DMA((chunks,)),
+            pltpu.SemaphoreType.DMA((count, chunks)),
+            pltpu.SemaphoreType.DMA((count, chunks)),
+        ]
+
+    def bind(self, grad, out, scratch):
+        self.grad, self.out = grad, out
+        far, near = (len(self.far), len(self.near))
+        self.mine = scratch[0]
+        self.first = scratch[1]
+        self.far_bufs = list(scratch[2 : 2 + far])
+        self.turn = scratch[2 + far]
+        self.near_bufs = list(scratch[3 + far : 3 + far + near])
+        self.local_sem, self.send_sem, self.recv_sem = scratch[3 + far + near :]
+
+    def piece(self, bit, chunk):
+        index = (slice(None),) * len(self.far) + (bit, slice(None))
+        return self.grad.at[index + (pl.ds(pl.multiple_of(chunk * self.width, 128), self.width),)]
+
+    def local_copy(self, chunk):
+        return pltpu.make_async_copy(
+            self.piece(my_bit(CORE), chunk), self.mine.at[chunk], self.local_sem.at[chunk]
+        )
+
+    def copy(self, stage, chunk):
+        send, recv = (self.send_sem.at[stage, chunk], self.recv_sem.at[stage, chunk])
+        far = len(self.far)
+        if stage == 0:
+            return remote(
+                self.piece(1 - my_bit(CORE), chunk), self.first.at[chunk], send, recv, CORE
+            )
+        if stage <= far:
+            step = self.far[stage - 1]
+            source = ([self.first] + self.far_bufs)[stage - 1]
+            target = self.far_bufs[stage - 1]
+            axis = self.axis_of(step, self.far[: stage - 1], self.names)
+        else:
+            at = stage - 1 - far
+            step = self.near[at]
+            source = ([self.turn] + self.near_bufs)[at]
+            target = self.near_bufs[at]
+            axis = self.axis_of(step, self.near[:at], self.seq_steps)
+        index = (chunk,) + (slice(None),) * axis + (1 - my_bit(step),)
+        return remote(source.at[index], target.at[chunk], send, recv, step)
+
+    def axis_of(self, step, gone, names):
+        return [name for name in names if name not in gone].index(step)
+
+    def stages(self):
+        return 2 + len(self.far) + len(self.near)
+
+    def run(self, stage, chunk):
+        far, near = (len(self.far), len(self.near))
+        if stage == 0:
+            self.local_copy(chunk).start()
+            self.copy(0, chunk).start()
+            return
+        self.copy(stage - 1, chunk).wait_recv()
+        if stage == 1:
+            self.local_copy(chunk).wait()
+            shape = self.first.shape[1:]
+
+            def add_first(index):
+                at = (chunk,) + index
+                self.first[at] = (self.first[at].astype(f32) + self.mine[at].astype(f32)).astype(bf16)
+
+            each_block(shape, add_first)
+        elif stage < 1 + far:
+            target = self.far_bufs[stage - 2]
+            source = ([self.first] + self.far_bufs)[stage - 2]
+            self.add_half(target, source, self.far, self.names, stage - 2, chunk)
+        elif stage == 1 + far:
+            step = self.far[-1]
+            source = ([self.first] + self.far_bufs)[far - 1]
+            target = self.far_bufs[far - 1]
+            total = target[chunk].astype(f32) + source[chunk, my_bit(step)].astype(f32)
+            total = total.astype(bf16)
+            count = 2**near
+            for owner in range(count):
+                at, rest = ((), owner)
+                for _ in range(near):
+                    at = (rest % 2,) + at
+                    rest = rest // 2
+                self.turn[(chunk,) + at] = total[owner * self.share : (owner + 1) * self.share]
+        elif stage < 1 + far + near:
+            at = stage - 2 - far
+            source = ([self.turn] + self.near_bufs)[at]
+            self.add_half(self.near_bufs[at], source, self.near, self.seq_steps, at, chunk)
+        else:
+            source = ([self.turn] + self.near_bufs)[near - 1]
+            kept = source[chunk, my_bit(self.near[-1])]
+            total = self.near_bufs[near - 1][chunk].astype(f32) + kept.astype(f32)
+            self.out[:, pl.ds(pl.multiple_of(chunk * self.width, 128), self.width)] = total
+        if stage < 1 + far + near:
+            self.copy(stage, chunk).start()
+
+    def add_half(self, target, source, steps, names, at, chunk):
+        step = steps[at]
+        axis = self.axis_of(step, steps[:at], names)
+        bit = my_bit(step)
+
+        def add(index):
+            from_at = (chunk,) + index[:axis] + (bit,) + index[axis:]
+            to_at = (chunk,) + index
+            target[to_at] = (target[to_at].astype(f32) + source[from_at].astype(f32)).astype(bf16)
+
+        each_block(target.shape[1:], add)
+
+    def drain(self, chunk):
+        for stage in range(self.stages() - 1):
+            self.copy(stage, chunk).wait_send()
+
+
+def reduce_kernel(flows, *refs):
+    count = len(flows)
+    scratch = list(refs[2 * count :])
+    for at, flow in enumerate(flows):
+        size = len(flow.scratch())
+        flow.bind(refs[at], refs[count + at], scratch[:size])
+        scratch = scratch[size:]
+    chunks = flows[0].chunks
+    stages = flows[0].stages()
+    greet()
+    order = [1, 0] + list(range(2, stages))
+
+    def step(at, carry):
+        for stage in order:
+            chunk = at - stage
+
+            @pl.when((chunk >= 0) & (chunk < chunks))
+            def _(stage=stage, chunk=chunk):
+                for flow in flows:
+                    flow.run(stage, chunk)
+
+        return carry
+
+    lax.fori_loop(0, chunks + stages - 1, step, 0)
+
+    def finish(chunk, carry):
+        for flow in flows:
+            flow.drain(chunk)
+        return carry
+
+    lax.fori_loop(0, chunks, finish, 0)
+
+
+def reduce_grads(grads, chunks, flips, name, collective_id):
+    flows = [Flow(g.shape[0], g.shape[1], chunks, flip) for g, flip in zip(grads, flips)]
+    scratch = []
+    for flow in flows:
+        scratch += flow.scratch()
+    return pl.pallas_call(
+        functools.partial(reduce_kernel, flows),
+        in_specs=[pl.BlockSpec(memory_space=pl.ANY)] * len(flows),
+        out_specs=[pl.BlockSpec(memory_space=pltpu.VMEM)] * len(flows),
+        out_shape=[jax.ShapeDtypeStruct((flow.share, flow.columns), f32) for flow in flows],
+        scratch_shapes=scratch,
+        compiler_params=pltpu.CompilerParams(
+            collective_id=collective_id, has_side_effects=True, vmem_limit_bytes=48 * 2**20
+        ),
+        cost_estimate=pl.CostEstimate(
+            flops=0, bytes_accessed=200 * 2**20, transcendentals=0
+        ),
+        name=name,
+    )(*[flow.view(grad) for flow, grad in zip(flows, grads)])
+
+
+def sum_seq(values):
+    for bit in range(int(math.log2(lax.axis_size("seq")))):
+        values = values + exchange(values, ("seq", bit))
+    return values
+
+
+def exchange(values, step):
+    size = lax.axis_size(step[0])
+    return lax.ppermute(values, step[0], [(i, i ^ (1 << step[1])) for i in range(size)])
+
+
+def gather_win(values):
+    out = values[None]
+    for bit in range(int(math.log2(lax.axis_size("win")))):
+        step = ("win", bit)
+        got = exchange(out, step)
+        low = my_bit(step) == 0
+        out = jnp.concatenate([jnp.where(low, out, got), jnp.where(low, got, out)], axis=0)
+    return out
+
+
+def three_parts(values):
+    parts = []
+    for _ in range(3):
+        part = lax.reduce_precision(values, 8, 7)
+        parts.append(part.astype(bf16))
+        values = values - part
+    return parts
 
 
 def per_device(
@@ -290,9 +533,8 @@
     ) + time_embed(noise_times, width)
     cond_sig = jax.nn.sigmoid(pre_cond)
     condition = pre_cond * cond_sig
-    window_facts = jnp.concatenate([pre_cond, class_onehot], axis=-1)
-    ada_float = ada_weight.astype(f32)
-    modulation = jnp.dot(condition, ada_float, precision=highest).reshape(windows, 6, width)
+    modulation = dot(jnp.concatenate(three_parts(condition), axis=0), ada_weight)
+    modulation = jnp.sum(modulation.reshape(3, windows, 6, width), axis=0)
     shift_attn = modulation[:, 0][:, None, :]
     scale_attn = modulation[:, 1][:, None, :]
     gate_attn = modulation[:, 2][:, None, :]
@@ -327,7 +569,7 @@
     gate_ffn_sig = jax.nn.sigmoid(gate_ffn)
     grad_layer = cotangent.astype(f32)
     grad_ffn = (gate_ffn_sig * grad_layer).astype(bf16).reshape(total_rows, width)
-    owned_down = reduce_owned(dot_tn(ffn_hidden, grad_ffn).astype(bf16), False)
+    grad_down = dot_tn(ffn_hidden, grad_ffn).astype(bf16)
     ffn_out = dot(ffn_hidden, down_weight).reshape(windows, row_count, width)
     layer_out = (hidden_state + gate_ffn_sig * ffn_out).astype(bf16)
     grad_gate_ffn = jnp.sum(grad_layer * ffn_out * gate_ffn_sig * (1.0 - gate_ffn_sig), axis=1)
@@ -336,8 +578,8 @@
     grad_gate_val = (
         grad_hidden_ffn * up_val * gate_sig * (1.0 + gate_val * (1.0 - gate_sig))
     ).astype(bf16)
-    owned_gate = reduce_owned(dot_tn(ffn_in, grad_gate_val).astype(bf16), True)
-    owned_up = reduce_owned(dot_tn(ffn_in, grad_up_val).astype(bf16), False)
+    grad_gate = dot_tn(ffn_in, grad_gate_val).astype(bf16)
+    grad_up = dot_tn(ffn_in, grad_up_val).astype(bf16)
     grad_ffn_in = dot_nt(grad_gate_val, gate_weight) + dot_nt(grad_up_val, up_weight)
     grad_ffn_in = grad_ffn_in.reshape(windows, row_count, width)
     grad_scale_ffn = jnp.sum(grad_ffn_in * normed_h, axis=1)
@@ -362,15 +604,15 @@
     grad_in_far = lax.psum_scatter(
         grad_in_part.reshape(windows, length, width), "seq", scatter_dimension=1, tiled=True
     )
-    grad_qkv = jnp.concatenate(
-        [
-            dot_tn(attn_in, grad_query).astype(bf16),
-            dot_tn(attn_in_all, grad_kv).astype(bf16),
-            grad_out,
-        ],
-        axis=-1,
-    )
-    owned_qkv_out = reduce_owned(grad_qkv, True)
+    grad_q_weight = dot_tn(attn_in, grad_query).astype(bf16)
+    grad_kv_weight = dot_tn(attn_in_all, grad_kv).astype(bf16)
+    owned_gate, owned_up, owned_down, owned_kv, owned_q, owned_out = reduce_grads(
+        [grad_gate, grad_up, grad_down, grad_kv_weight, grad_q_weight, grad_out],
+        6,
+        [False, True, False, True, True, True],
+        "reduce_all",
+        1,
+    )
     grad_attn_in = dot_nt(grad_query, qkv_weight[:, :width]).reshape(
         windows, row_count, width
     ) + grad_in_far.astype(f32)
@@ -379,29 +621,26 @@
     grad_tokens = (
         grad_hidden + norm_back(grad_attn_in * (1.0 + scale_attn), normed_x, inv_x)
     ).astype(bf16)
-    grad_mod = jnp.concatenate(
+    early_mod = jnp.stack([grad_gate_attn, grad_shift_ffn, grad_scale_ffn, grad_gate_ffn], axis=0)
+    early_mod = sum_seq(early_mod.reshape(4 * windows, width))
+    onehot_rows = jnp.pad(class_onehot, ((0, 0), (0, width - classes)))
+    early_all = gather_win(jnp.concatenate([early_mod, pre_cond, onehot_rows], axis=0))
+    late_mod = jnp.concatenate([grad_shift_attn, grad_scale_attn], axis=0)
+    table_size = table_rows * head_count
+    late = jnp.concatenate([late_mod, grad_table.reshape(table_size // width, width)], axis=0)
+    late_all = gather_win(sum_seq(late))
+    mod_all = jnp.concatenate(
         [
-            grad_shift_attn,
-            grad_scale_attn,
-            grad_gate_attn,
-            grad_shift_ffn,
-            grad_scale_ffn,
-            grad_gate_ffn,
+            late_all[:, : 2 * windows].reshape(win_count, 2, windows, width),
+            early_all[:, : 4 * windows].reshape(win_count, 4, windows, width),
         ],
         axis=1,
     )
-    parts = jnp.concatenate([grad_mod.reshape(-1), grad_table.reshape(-1), window_facts.reshape(-1)])
-    parts = jnp.pad(parts, (0, -parts.shape[0] % 1024))
-    parts_all = lax.all_gather(parts, ("win", "seq"), axis=0)
-    mod_size = windows * 6 * width
-    mod_all = jnp.sum(
-        parts_all[:, :mod_size].reshape(win_count, seq_count, windows, 6 * width), axis=1
-    ).reshape(win_count * windows, 6 * width)
-    table_end = mod_size + table_rows * head_count
-    table_all = jnp.sum(parts_all[:, mod_size:table_end], axis=0).reshape(table_rows, head_count)
-    window_facts = parts_all[::seq_count, table_end : table_end + windows * (width + classes)].reshape(win_count * windows, width + classes)
-    pre_all = window_facts[:, :width]
-    onehot_all = window_facts[:, width:]
+    mod_all = jnp.swapaxes(mod_all, 1, 2).reshape(win_count * windows, 6 * width)
+    table_all = jnp.sum(late_all[:, 2 * windows :], axis=0).reshape(table_rows, head_count)
+    facts_all = early_all[:, 4 * windows :].reshape(win_count, 2, windows, width)
+    pre_all = facts_all[:, 0].reshape(win_count * windows, width)
+    onehot_all = facts_all[:, 1].reshape(win_count * windows, width)
     ada_rows = width // devices
     sig_all = jax.nn.sigmoid(pre_all)
     condition_rows = lax.dynamic_slice_in_dim(pre_all * sig_all, owner * ada_rows, ada_rows, 1)
@@ -429,8 +668,8 @@
         grad_tokens,
         owned_class,
         owned_ada.reshape(-1),
-        owned_qkv_out[:, : 3 * width].reshape(-1),
-        owned_qkv_out[:, 3 * width :].reshape(-1),
+        jnp.concatenate([owned_q, owned_kv], axis=-1).reshape(-1),
+        owned_out.reshape(-1),
         owned_pair_table,
         owned_pair_weight,
         owned_gate.reshape(-1),

time: 316 us -> 299 us (0.946); the launches traced: 310 us -> 298 us
  Pallas kernels: 26.1 us -> 123 us
  waiting for transfers between devices: 104 us -> 41.5 us
  local copies, waits for them, and re-layouts: 45.4 us -> 21.4 us
  other arithmetic: 35.6 us -> 21.1 us
  starting transfers between devices: 16.4 us -> 10.8 us
    pallas_call x0 -> x1, Pallas kernels: none -> 96.9 us  [reduce_grads(): pl.pallas_call(functools.partial(reduce_kernel, flows), in_specs=[pl.Bloc...]
    ppermute x20 -> x10, waiting for transfers between devices: 80.4 us -> 19.9 us  [exchange(): lax.ppermute(values, step[0], [(i, i ^ 1 << step[1]) for i in range(size)])]
    convert_element_type x17 -> x1, other arithmetic: 14.6 us -> 0.01 us  [three_parts(): parts.append(part.astype(bf16))]
    dynamic_slice x10 -> x0, local copies, waits for them, and re-layouts: 9.32 us -> none  [reduce_owned(): lax.dynamic_index_in_dim(view, mine, 1, keepdims=False)]
    reshape x20 -> x9, local copies, waits for them, and re-layouts: 8.24 us -> 1.87 us  [the longest x1 0.7 us: per_device(): jnp.concatenate([owned_q, owned_kv], axis=-1).reshape(-1)]
    dot_general x1 -> x0, matrix products: 5.9 us -> none  [per_device(): jnp.dot(condition, ada_float, precision=highest).reshape(windows, 6, width)]
    ppermute x20 -> x10, starting transfers between devices: 16.3 us -> 10.7 us  [exchange(): lax.ppermute(values, step[0], [(i, i ^ 1 << step[1]) for i in range(size)])]
    dot_general x6, matrix products: 16.6 us -> 12.2 us  [dot_nt(): lax.dot_general(a, b, (((1,), (1,)), ((), ())), preferred_element_type=f32)]
  transfers between devices with their start and end apart: 23 -> 12, of which waited for: 12 -> 8; matrix products, arithmetic and copies ran while one was open for 29% -> 18% of each run, Pallas kernels for 0% -> 32%
where the time goes in v3:
time: 299 us; the launch traced here: 298 us
  Pallas kernels  123 us (41%)
  matrix products  65.2 us (22%)
  waiting for transfers between devices  41.5 us (14%)
  local copies, waits for them, and re-layouts  21.4 us (7%)
  other arithmetic  21.1 us (7%)
  between operations  15.1 us (5%)
  starting transfers between devices  10.8 us (4%)
    pallas_call x1, Pallas kernels, reduce_grads(): pl.pallas_call(functools.partial(reduce_kernel, flows), in_specs=[pl.Bloc...  96.9 us
    all_gather x1, waiting for transfers between devices, per_device(): tokens_all = lax.all_gather(tokens, 'seq', axis=1, tiled=True)  20.9 us
    dot_general x8, matrix products, dot(): return jnp.dot(a, b, preferred_element_type=f32)  20 us
    ppermute x10, waiting for transfers between devices, exchange(): lax.ppermute(values, step[0], [(i, i ^ 1 << step[1]) for i in range(size)])  19.9 us
    dot_general x6, matrix products, dot_tn(): lax.dot_general(a, b, (((0,), (0,)), ((), ())), preferred_element_type=f32)  17 us
    pallas_call x1, Pallas kernels, attend_back(): pl.pallas_call(functools.partial(attend_back_kernel, head_size, table.sha...  13.2 us
    pallas_call x1, Pallas kernels, attend(): pl.pallas_call(functools.partial(attend_kernel, head_size, table.shape[1]...  12.7 us
    dot_general x6, matrix products, dot_nt(): lax.dot_general(a, b, (((1,), (1,)), ((), ())), preferred_element_type=f32)  12.2 us
  transfers between devices with their start and end apart: 12, of which 8 were waited for; matrix products, arithmetic and copies ran while one was open for 18% of the time, Pallas kernels for 32%

profile of v3, /device:TPU:0, one launch (start us, length us, event | category | flops | bytes accessed | tf_op | source)
XLA Modules:
  0.0 298.1 jit_solution(13364728046447222196)
XLA Ops:
  7.2 0.7 all-gather.2.cloned.1.call-update
  8.0 1.1 convert_reduce_fusion.1
  9.1 0.7 broadcast_multiply_fusion.6
  9.8 0.7 iota_compare_fusion.5
  10.5 0.7 iota_compare_fusion.4
  11.2 0.7 broadcast_compare_fusion
  12.0 1.2 fusion.38
  13.9 1.5 reduce-precision_convert_fusion.1
  15.4 1.2 bitcast_add_fusion
  16.7 4.3 %fusion.48 = f32[6,4608]{1,0:T(8,128)S(1)} fusion(bf16[768,4608]{1,0:T(8,128)(2,1)} %param.22, bf16[2,768]{1,0:T(2,128)(2,1)S(1)} %get-tuple-element.78, bf16[2,768]{1,0:T(2,128)(2,1)S(1)} %get-tuple-element.77, bf16[2,768]{1,0:T(2,128)(2,1)S(1)} %get-tuple-element.50), kind=kOutput, calls=%fused_computation.114 | convolution fusion | flops 42494976 | bytes 7197696 | tf_op jit(solution)/shard_map/dot_general | solution.py:40
  21.6 1.2 copy.45
  24.7 0.7 fusion.18.table_ref
  25.8 2.6 convolution_convert_fusion.8.q_ref
  28.5 20.9 %all-gather.2.cloned.1.call-done = bf16[2,512,768]{2,1,0:T(8,128)(2,1)} async-done(((bf16[2,128,768]{2,1,0:T(8,128)(2,1)}), bf16[2,512,768]{2,1,0:T(8,128)(2,1)}) %all-gather.2.cloned.1.call-update) | async-done | bytes 1572880 | tf_op jit(solution)/shard_map/all_gather | solution.py:529
  49.4 1.8 convert_reduce_fusion
  51.2 2.1 fusion.4
  53.4 1.3 fusion.7
  54.8 4.2 %convolution_convert_fusion.3.k_ref.v_ref = bf16[1024,1536]{1,0:T(8,128)(2,1)} fusion(bf16[1024,768]{1,0:T(8,128)(2,1)S(1)} %bitcast.147, bf16[768,2304]{1,0:T(8,128)(2,1)S(1)} %copy-done.22), kind=kOutput, calls=%fused_computation.8 | convolution fusion | flops 2417491968 | bytes 7077888 | tf_op jit(solution)/shard_map/dot_general | solution.py:40
  59.0 12.7 %attend.1 = (bf16[256,768]{1,0:T(8,128)(2,1)}, f32[2,6,256]{2,1,0:T(8,128)}) custom-call(s32[3]{0:T(128)} %pad_add_fusion.facts_ref, bf16[256,768]{1,0:T(8,128)(2,1)} %convolution_convert_fusion.8.q_ref, bf16[1024,1536]{1,0:T(8,128)(2,1)} %convolution_convert_fusion.3.k_ref.v_ref, bf16[1024,1536]{1,0:T(8,128)(2,1)} %convolution_convert_fusion.3.k_ref.v_ref, ...), custom_call_target="tpu_custom_call" | custom-call | flops 805306368 | bytes 524288 | tf_op jit(solution)/shard_map/attend/pallas_call | solution.py:167
  71.8 1.5 fusion.73
  73.3 0.9 fusion.71
  74.6 3.9 %fusion.75 = f32[256,3072]{1,0:T(8,128)S(1)} fusion(bf16[256,768]{1,0:T(8,128)(2,1)S(1)} %bitcast.134, bf16[768,3072]{1,0:T(8,128)(2,1)} %param.28), kind=kOutput, calls=%fused_computation.182 | convolution fusion | flops 1207959552 | bytes 8257536 | tf_op jit(solution)/shard_map/dot_general | solution.py:40
  78.6 1.4 fusion.74
  80.0 2.5 multiply_convert_fusion
  82.5 1.4 fusion.77
  84.1 2.3 slice-done
  86.5 1.5 fusion.43
  88.0 0.9 fusion.44
  88.9 1.4 fusion.76
  90.4 2.0 multiply_reduce_fusion
  92.4 0.9 copy-done.5
  93.3 1.3 convolution_convert_fusion.7.grad_ref
  94.6 13.2 %attend_back.1 = (bf16[256,768]{1,0:T(8,128)(2,1)}, bf16[1024,1536]{1,0:T(8,128)(2,1)}, bf16[2,12,512,128]{3,2,1,0:T(8,128)(2,1)}) custom-call(s32[3]{0:T(128)} %pad_add_fusion.facts_ref, bf16[256,768]{1,0:T(8,128)(2,1)} %convolution_convert_fusion.8.q_ref, bf16[1024,1536]{1,0:T(8,128)(2,1)} %convolution_convert_fusion.3.k_ref.v_ref, ...), custom_call_target="tpu_custom_call" | custom-call | flops 2013265920 | bytes 6291456 | tf_op jit(solution)/shard_map/attend_back/pallas_call | solution.py:193
  107.9 5.2 %convolution_convert_fusion.4 = bf16[768,1536]{1,0:T(8,128)(2,1)S(1)} fusion(bf16[1024,768]{1,0:T(8,128)(2,1)} %bitcast.148, bf16[1024,1536]{1,0:T(8,128)(2,1)} %get-tuple-element.25), kind=kOutput, calls=%fused_computation.11 | convolution fusion | flops 2417098752 | bytes 7077888 | tf_op jit(solution)/shard_map/dot_general | solution.py:48
  113.1 3.8 %fusion.12 = bf16[1024,768]{1,0:T(8,128)(2,1)} fusion(bf16[1024,1536]{1,0:T(8,128)(2,1)S(1)} %copy-done.46, bf16[768,2304]{1,0:T(8,128)(2,1)S(1)} %copy-done.23), kind=kOutput, calls=%fused_computation.24 | convolution fusion | flops 2416705536 | bytes 7077888 | tf_op jit(solution)/shard_map/dot_general | solution.py:44
  116.9 3.6 %convolution_convert_fusion = bf16[3072,768]{1,0:T(8,128)(2,1)} fusion(bf16[256,3072]{1,0:T(8,128)(2,1)S(1)} %copy-done.10, bf16[256,768]{1,0:T(8,128)(2,1)S(1)} %bitcast.145), kind=kOutput, calls=%fused_computation.3 | convolution fusion | flops 1210318848 | bytes 6684672 | tf_op jit(solution)/shard_map/dot_general | solution.py:48
  120.5 0.7 collective-permute-start.5
  121.2 7.9 %copy.46 = bf16[2,12,512,128]{2,1,0,3:T(8,128)(2,1)} copy(bf16[2,12,512,128]{3,2,1,0:T(8,128)(2,1)} %get-tuple-element.26) | data formatting | bytes 6291456 | tf_op jit(solution)/shard_map/attend_back/pallas_call | solution.py:193
  129.1 11.0 %fusion.15 = f32[128,12]{1,0:T(8,128)S(1)} fusion(bf16[2,12,512,128]{2,1,0,3:T(8,128)(2,1)} %copy.46, s32[2,512,128]{1,0,2:T(2,128)} %copy.45), kind=kOutput, calls=%fused_computation.37 | convolution fusion | flops 419430400 | bytes 3676160 | tf_op jit(solution)/shard_map/whji,wkji->kh/dot_general | solution.py:602
  140.1 3.6 %convolution_convert_fusion.1 = bf16[768,3072]{1,0:T(8,128)(2,1)} fusion(bf16[256,768]{1,0:T(8,128)(2,1)S(1)} %bitcast.136, bf16[256,3072]{1,0:T(8,128)(2,1)S(1)} %copy-done.8), kind=kOutput, calls=%fused_computation.4 | convolution fusion | flops 1210318848 | bytes 6684672 | tf_op jit(solution)/shard_map/dot_general | solution.py:48
  143.7 3.7 %convolution_convert_fusion.2 = bf16[768,3072]{1,0:T(8,128)(2,1)} fusion(bf16[256,768]{1,0:T(8,128)(2,1)S(1)} %bitcast.137, bf16[256,3072]{1,0:T(8,128)(2,1)S(1)} %copy-done.12), kind=kOutput, calls=%fused_computation.5 | convolution fusion | flops 1210318848 | bytes 6684672 | tf_op jit(solution)/shard_map/dot_general | solution.py:48
  147.4 1.3 collective-permute-start.6
  149.2 4.8 %collective-permute-done.6 = f32[8,768]{1,0:T(8,128)S(1)} collective-permute-done((f32[8,768]{1,0:T(8,128)S(1)}, f32[8,768]{1,0:T(8,128)S(1)}, u32[]{:S(2)}, u32[]{:S(2)}) %collective-permute-start.6) | collective-permute-done | bytes 24608 | tf_op jit(solution)/shard_map/ppermute | solution.py:478
  154.7 96.9 %reduce_all.1 = (f32[24,3072]{1,0:T(8,128)S(1)}, f32[24,3072]{1,0:T(8,128)S(1)}, f32[96,768]{1,0:T(8,128)S(1)}, f32[24,1536]{1,0:T(8,128)S(1)}, f32[24,768]{1,0:T(8,128)S(1)}, /*index=5*/f32[24,768]{1,0:T(8,128)S(1)}) custom-call(bf16[2,2,2,96,3072]{4,3,2,1,0:T(8,128)(2,1)} %bitcast.130, bf16[2,2,2,96,3072]{4,3,2,1,0:T(8,128)(2,1)} %bitcast.129, ...), custom_call_target="tpu_custom_call" | custom-call | bytes 209715200 | tf_op jit(solution)/shard_map/reduce_all/pallas_call | solution.py:454
  251.7 2.2 collective-permute-start.8
  254.1 0.7 reshape.269
  254.8 0.6 reshape.270
  255.4 0.8 copy.65
  256.2 0.8 copy.66
  257.0 0.7 reshape.276
  258.0 1.8 fusion.20
  259.8 3.3 %collective-permute-done.9 = f32[4,12,768]{2,0,1:T(4,128)S(1)} collective-permute-done((f32[4,12,768]{2,0,1:T(4,128)S(1)}, f32[4,12,768]{2,0,1:T(4,128)S(1)}, u32[]{:S(2)}, u32[]{:S(2)}) %collective-permute-start.9) | collective-permute-done | bytes 147488 | tf_op jit(solution)/shard_map/ppermute | solution.py:478
  263.4 1.6 fusion.68
  265.0 3.1 %collective-permute-start = (f32[6,768]{1,0:T(8,128)S(1)}, f32[6,768]{1,0:T(8,128)S(1)}, u32[]{:S(2)}, u32[]{:S(2)}) collective-permute-start(f32[6,768]{1,0:T(8,128)S(1)} %pad_maximum_fusion.9), channel_id=1, source_target_pairs={{0,1},{1,0},{2,3},{3,2},{4,5},{5,4},{6,7},{7,6},{8,9},{9,8},{10,11... | collective-permute-start | bytes 55304 | tf_op jit(solution)/shard_map/ppermute | solution.py:478
  268.1 1.8 collective-permute-done
  269.9 2.6 collective-permute-start.1
  273.0 1.8 collective-permute-done.1
  274.8 1.2 collective-permute-done.2
  276.0 0.7 collective-permute-start.3
  276.6 3.5 %collective-permute-done.3 = f32[2,6,768]{2,1,0:T(8,128)S(1)} collective-permute-done((f32[2,6,768]{2,1,0:T(8,128)S(1)}, f32[2,6,768]{2,1,0:T(8,128)S(1)}, u32[]{:S(2)}, u32[]{:S(2)}) %collective-permute-start.3) | collective-permute-done | bytes 36896 | tf_op jit(solution)/shard_map/ppermute | solution.py:478
  280.2 1.1 fusion.36
  281.3 3.5 %collective-permute-done.4 = f32[4,6,768]{2,1,0:T(8,128)S(1)} collective-permute-done((f32[4,6,768]{2,1,0:T(8,128)S(1)}, f32[4,6,768]{2,1,0:T(8,128)S(1)}, u32[]{:S(2)}, u32[]{:S(2)}) %collective-permute-start.4) | collective-permute-done | bytes 73760 | tf_op jit(solution)/shard_map/ppermute | solution.py:478
  286.5 0.8 reshape.262
  288.1 2.5 fusion.19
  (194 shorter events, 10.2 us)
Async XLA Ops:
  7.2 64.6 %copy-start = (bf16[768,768]{1,0:T(8,128)(2,1)S(1)}, bf16[768,768]{1,0:T(8,128)(2,1)}, u32[]{:S(2)}) copy-start(bf16[768,768]{1,0:T(8,128)(2,1)} %param.24) | copy-start | bytes 3538948
  7.2 42.2 %all-gather.2.cloned.1.call-start = ((), (), s32[]{:S(2)}) async-start(), calls=%async_computation.1 | async-start | bytes 1966080 | tf_op jit(solution)/shard_map/all_gather | solution.py:529
  7.9 255.4 %reduce-scatter.2.cloned.1.call-start = ((), (), s32[]{:S(2)}) async-start(), calls=%async_computation.2 | async-start | bytes 1966080 | tf_op jit(solution)/shard_map/reduce_scatter | solution.py:604
  12.0 13.6 %copy-start.32 = (f32[2,128]{1,0:T(2,128)}, f32[2,128]{1,0:T(2,128)S(1)}, u32[]{:S(2)}) copy-start(f32[2,128]{1,0:T(2,128)S(1)} %broadcast_multiply_fusion.5) | copy-start | bytes 3076
  16.6 4.3 %copy-start.45 = (s32[2]{0:T(128)S(1)}, s32[2]{0:T(128)}, u32[]{:S(2)}) copy-start(s32[2]{0:T(128)} %param.19) | copy-start | bytes 28
  16.6 8.1 %copy-start.24 = (bf16[128,256]{1,0:T(8,128)(2,1)S(1)}, bf16[128,256]{1,0:T(8,128)(2,1)}, u32[]{:S(2)}) copy-start(bf16[128,256]{1,0:T(8,128)(2,1)} %param.25) | copy-start | bytes 196612
  16.6 8.1 %copy-start.30 = (bf16[256,12]{0,1:T(8,128)(2,1)S(1)}, bf16[256,12]{0,1:T(8,128)(2,1)}, u32[]{:S(2)}) copy-start(bf16[256,12]{0,1:T(8,128)(2,1)} %param.26) | copy-start | bytes 18436
  16.6 8.8 %copy-start.14 = (bf16[2,128,768]{2,1,0:T(8,128)(2,1)S(1)}, bf16[2,128,768]{2,1,0:T(8,128)(2,1)}, u32[]{:S(2)}) copy-start(bf16[2,128,768]{2,1,0:T(8,128)(2,1)} %param.16) | copy-start | bytes 1179652
  16.7 8.9 %copy-start.2 = (bf16[2,128,768]{2,1,0:T(8,128)(2,1)S(1)}, bf16[2,128,768]{2,1,0:T(8,128)(2,1)}, u32[]{:S(2)}) copy-start(bf16[2,128,768]{2,1,0:T(8,128)(2,1)} %param.15) | copy-start | bytes 1179652
  22.8 30.6 %copy-start.42 = (f32[2,128]{1,0:T(2,128)}, f32[2,128]{1,0:T(2,128)S(1)}, u32[]{:S(2)}) copy-start(f32[2,128]{1,0:T(2,128)S(1)} %add_rsqrt_fusion.2) | copy-start | bytes 3076
  24.1 29.3 %copy-start.27 = (f32[2,768]{1,0:T(2,128)}, f32[2,768]{1,0:T(2,128)S(1)}, u32[]{:S(2)}) copy-start(f32[2,768]{1,0:T(2,128)S(1)} %get-tuple-element.88) | copy-start | bytes 18436
  24.7 28.7 %copy-start.29 = (f32[2,768]{1,0:T(2,128)}, f32[2,768]{1,0:T(2,128)S(1)}, u32[]{:S(2)}) copy-start(f32[2,768]{1,0:T(2,128)S(1)} %get-tuple-element.90) | copy-start | bytes 18436
  25.8 27.6 %copy-start.20 = (bf16[2,128,768]{2,1,0:T(8,128)(2,1)}, bf16[2,128,768]{2,1,0:T(8,128)(2,1)S(1)}, u32[]{:S(2)}) copy-start(bf16[2,128,768]{2,1,0:T(8,128)(2,1)S(1)} %fusion.31) | copy-start | bytes 1179652
  49.4 4.1 %copy-start.4 = (bf16[2,512,768]{2,1,0:T(8,128)(2,1)S(1)}, bf16[2,512,768]{2,1,0:T(8,128)(2,1)}, u32[]{:S(2)}) copy-start(bf16[2,512,768]{2,1,0:T(8,128)(2,1)} %all-gather.2.cloned.1.call-done) | copy-start | bytes 4718596
  49.4 5.4 %copy-start.22 = (bf16[768,2304]{1,0:T(8,128)(2,1)S(1)}, bf16[768,2304]{1,0:T(8,128)(2,1)}, u32[]{:S(2)}) copy-start(bf16[768,2304]{1,0:T(8,128)(2,1)} %param.23) | copy-start | bytes 10616836
  54.8 4.3 %copy-start.13 = (bf16[2,512,768]{2,1,0:T(8,128)(2,1)}, bf16[2,512,768]{2,1,0:T(8,128)(2,1)S(1)}, u32[]{:S(2)}) copy-start(bf16[2,512,768]{2,1,0:T(8,128)(2,1)S(1)} %fusion.7) | copy-start | bytes 4718596
  71.8 2.6 copy-start.38
  74.4 4.1 %slice-start.2 = ((s8[4718592]{0:T(1024)(128)(4,1)}), s8[4194304]{0:T(1024)(128)(4,1)S(1)}, s32[]{:S(2)}) async-start(s8[4718592]{0:T(1024)(128)(4,1)} %bitcast.161), calls=%async_computation.5 | async-start | bytes 8388608
  74.6 3.9 %slice-start.3 = ((s8[4718592]{0:T(1024)(128)(4,1)}), s8[524288]{0:T(1024)(128)(4,1)S(1)}, s32[]{:S(2)}) async-start(s8[4718592]{0:T(1024)(128)(4,1)} %bitcast.161), calls=%async_computation.6 | async-start | bytes 1048576
  74.6 5.3 %slice-start.4 = ((s8[4718592]{0:T(1024)(128)(4,1)}), s8[4194304]{0:T(1024)(128)(4,1)S(1)}, s32[]{:S(2)}) async-start(s8[4718592]{0:T(1024)(128)(4,1)} %bitcast.163), calls=%async_computation.7 | async-start | bytes 8388608
  78.5 1.4 slice-start.5
  82.4 1.5 copy-start.11
  82.4 1.6 copy-start.7
  82.5 6.4 %copy-start.9 = (bf16[256,3072]{1,0:T(8,128)(2,1)}, bf16[256,3072]{1,0:T(8,128)(2,1)S(1)}, u32[]{:S(2)}) copy-start(bf16[256,3072]{1,0:T(8,128)(2,1)S(1)} %get-tuple-element.54) | copy-start | bytes 4718596
  82.5 3.9 %slice-start = ((s8[4718592]{0:T(1024)(128)(4,1)}), s8[4194304]{0:T(1024)(128)(4,1)S(1)}, s32[]{:S(2)}) async-start(s8[4718592]{0:T(1024)(128)(4,1)} %bitcast.138), calls=%async_computation.3 | async-start | bytes 8388608
  82.5 4.0 %slice-start.1 = ((s8[4718592]{0:T(1024)(128)(4,1)}), s8[524288]{0:T(1024)(128)(4,1)S(1)}, s32[]{:S(2)}) async-start(s8[4718592]{0:T(1024)(128)(4,1)} %bitcast.138), calls=%async_computation.4 | async-start | bytes 1048576
  88.9 1.4 copy-start.15
  88.9 1.4 copy-start.26
  88.9 1.4 copy-start.28
  88.9 1.4 copy-start.36
  88.9 1.4 copy-start.37
  107.9 5.2 %copy-start.23 = (bf16[768,2304]{1,0:T(8,128)(2,1)S(1)}, bf16[768,2304]{1,0:T(8,128)(2,1)}, u32[]{:S(2)}) copy-start(bf16[768,2304]{1,0:T(8,128)(2,1)} %param.23) | copy-start | bytes 10616836
  107.9 5.2 %copy-start.46 = (bf16[1024,1536]{1,0:T(8,128)(2,1)S(1)}, bf16[1024,1536]{1,0:T(8,128)(2,1)}, u32[]{:S(2)}) copy-start(bf16[1024,1536]{1,0:T(8,128)(2,1)} %get-tuple-element.25) | copy-start | bytes 9437188
  113.1 3.8 %copy-start.10 = (bf16[256,3072]{1,0:T(8,128)(2,1)S(1)}, bf16[256,3072]{1,0:T(8,128)(2,1)}, u32[]{:S(2)}) copy-start(bf16[256,3072]{1,0:T(8,128)(2,1)} %copy-done.9) | copy-start | bytes 4718596
  116.9 3.6 %copy-start.34 = (f32[2,768]{1,0:T(2,128)S(1)}, f32[2,768]{1,0:T(2,128)}, u32[]{:S(2)}) copy-start(f32[2,768]{1,0:T(2,128)} %get-tuple-element.42) | copy-start | bytes 18436
  116.9 3.6 %copy-start.35 = (f32[2,768]{1,0:T(2,128)S(1)}, f32[2,768]{1,0:T(2,128)}, u32[]{:S(2)}) copy-start(f32[2,768]{1,0:T(2,128)} %get-tuple-element.56) | copy-start | bytes 18436
  116.9 3.6 %copy-start.40 = (f32[2,768]{1,0:T(2,128)S(1)}, f32[2,768]{1,0:T(2,128)}, u32[]{:S(2)}) copy-start(f32[2,768]{1,0:T(2,128)} %get-tuple-element.39) | copy-start | bytes 18436
  116.9 3.6 %copy-start.41 = (f32[2,768]{1,0:T(2,128)S(1)}, f32[2,768]{1,0:T(2,128)}, u32[]{:S(2)}) copy-start(f32[2,768]{1,0:T(2,128)} %get-tuple-element.41) | copy-start | bytes 18436
  120.5 26.9 %collective-permute-start.5 = (f32[8,768]{1,0:T(8,128)S(1)}, f32[8,768]{1,0:T(8,128)S(1)}, u32[]{:S(2)}, u32[]{:S(2)}) collective-permute-start(f32[8,768]{1,0:T(8,128)S(1)} %reshape.258), channel_id=1, source_target_pairs={{0,1},{1,0},{2,3},{3,2},{4,5},{5,4},{6,7},{7,6},{8,9},{9,8},{10,11... | collective-permute-start | bytes 73736 | tf_op jit(solution)/shard_map/ppermute | solution.py:478
  129.1 11.0 %copy-start.8 = (bf16[256,3072]{1,0:T(8,128)(2,1)S(1)}, bf16[256,3072]{1,0:T(8,128)(2,1)}, u32[]{:S(2)}) copy-start(bf16[256,3072]{1,0:T(8,128)(2,1)} %copy-done.7) | copy-start | bytes 4718596
  140.1 3.6 %copy-start.12 = (bf16[256,3072]{1,0:T(8,128)(2,1)S(1)}, bf16[256,3072]{1,0:T(8,128)(2,1)}, u32[]{:S(2)}) copy-start(bf16[256,3072]{1,0:T(8,128)(2,1)} %copy-done.11) | copy-start | bytes 4718596
  143.7 5.0 %copy-start.19 = (bf16[256,768]{1,0:T(8,128)(2,1)S(1)}, bf16[256,768]{1,0:T(8,128)(2,1)}, u32[]{:S(2)}) copy-start(bf16[256,768]{1,0:T(8,128)(2,1)} %get-tuple-element.22) | copy-start | bytes 1179652
  143.7 10.3 %copy-start.39 = (f32[2,768]{1,0:T(2,128)S(1)}, f32[2,768]{1,0:T(2,128)}, u32[]{:S(2)}) copy-start(f32[2,768]{1,0:T(2,128)} %pad_convert_fusion) | copy-start | bytes 18436
  143.7 10.3 %copy-start.44 = (f32[2,768]{1,0:T(2,128)S(1)}, f32[2,768]{1,0:T(2,128)}, u32[]{:S(2)}) copy-start(f32[2,768]{1,0:T(2,128)} %get-tuple-element.81) | copy-start | bytes 18436
  143.7 10.5 %copy-start.17 = (bf16[256,768]{1,0:T(8,128)(2,1)S(1)}, bf16[256,768]{1,0:T(8,128)(2,1)}, u32[]{:S(2)}) copy-start(bf16[256,768]{1,0:T(8,128)(2,1)} %get-tuple-element.24) | copy-start | bytes 1179652
  143.7 10.5 %copy-start.21 = (bf16[2,128,768]{2,1,0:T(8,128)(2,1)S(1)}, bf16[2,128,768]{2,1,0:T(8,128)(2,1)}, u32[]{:S(2)}) copy-start(bf16[2,128,768]{2,1,0:T(8,128)(2,1)} %copy-done.20) | copy-start | bytes 1179652
  147.4 6.6 %collective-permute-start.6 = (f32[8,768]{1,0:T(8,128)S(1)}, f32[8,768]{1,0:T(8,128)S(1)}, u32[]{:S(2)}, u32[]{:S(2)}) collective-permute-start(f32[8,768]{1,0:T(8,128)S(1)} %add.193), channel_id=1, source_target_pairs={{0,2},{1,3},{2,0},{3,1},{4,6},{5,7},{6,4},{7,5},{8,10},{9,11},{10,... | collective-permute-start | bytes 73736 | tf_op jit(solution)/shard_map/ppermute | solution.py:478
  154.1 97.5 %collective-permute-start.7 = (f32[1,12,768]{2,0,1:T(1,128)S(1)}, f32[1,12,768]{2,0,1:T(1,128)S(1)}, u32[]{:S(2)}, u32[]{:S(2)}) collective-permute-start(f32[1,12,768]{2,0,1:T(1,128)S(1)} %broadcast_in_dim.8), channel_id=1, source_target_pairs={{0,4},{4,0},{8,12},{12,8},{16,20},{20,16},{24,28},{28,24},{1,5},{5... | collective-permute-start | bytes 110600 | tf_op jit(solution)/shard_map/ppermute | solution.py:478
  251.6 6.4 %copy-start.18 = (bf16[256,768]{1,0:T(8,128)(2,1)S(1)}, bf16[256,768]{1,0:T(8,128)(2,1)}, u32[]{:S(2)}) copy-start(bf16[256,768]{1,0:T(8,128)(2,1)} %get-tuple-element.24) | copy-start | bytes 1179652
  251.7 6.0 %collective-permute-start.8 = (f32[2,12,768]{2,0,1:T(2,128)S(1)}, f32[2,12,768]{2,0,1:T(2,128)S(1)}, u32[]{:S(2)}, u32[]{:S(2)}) collective-permute-start(f32[2,12,768]{2,0,1:T(2,128)S(1)} %pad_maximum_fusion.5), channel_id=1, source_target_pairs={{0,8},{4,12},{8,0},{12,4},{16,24},{20,28},{24,16},{28,20},{1,9},{5... | collective-permute-start | bytes 221192 | tf_op jit(solution)/shard_map/ppermute | solution.py:478
  254.8 8.6 %copy-start.3 = (bf16[2,128,768]{2,1,0:T(8,128)(2,1)S(1)}, bf16[2,128,768]{2,1,0:T(8,128)(2,1)}, u32[]{:S(2)}) copy-start(bf16[2,128,768]{2,1,0:T(8,128)(2,1)} %param.15) | copy-start | bytes 1179652
  254.8 8.6 %copy-start.33 = (f32[2,128]{1,0:T(2,128)S(1)}, f32[2,128]{1,0:T(2,128)}, u32[]{:S(2)}) copy-start(f32[2,128]{1,0:T(2,128)} %copy-done.32) | copy-start | bytes 3076
  254.8 8.6 %copy-start.43 = (f32[2,128]{1,0:T(2,128)S(1)}, f32[2,128]{1,0:T(2,128)}, u32[]{:S(2)}) copy-start(f32[2,128]{1,0:T(2,128)} %copy-done.42) | copy-start | bytes 3076
  257.9 5.2 %collective-permute-start.9 = (f32[4,12,768]{2,0,1:T(4,128)S(1)}, f32[4,12,768]{2,0,1:T(4,128)S(1)}, u32[]{:S(2)}, u32[]{:S(2)}) collective-permute-start(f32[4,12,768]{2,0,1:T(4,128)S(1)} %pad_maximum_fusion.2), channel_id=1, source_target_pairs={{0,16},{4,20},{8,24},{12,28},{16,0},{20,4},{24,8},{28,12},{1,17},{... | collective-permute-start | bytes 442376 | tf_op jit(solution)/shard_map/ppermute | solution.py:478
  259.7 20.5 %copy-start.6 = (f32[2,128,768]{2,1,0:T(8,128)S(1)}, f32[2,128,768]{2,1,0:T(8,128)}, u32[]{:S(2)}) copy-start(f32[2,128,768]{2,1,0:T(8,128)} %copy-done.5) | copy-start | bytes 2359300
  263.3 16.9 %copy-start.16 = (bf16[2,128,768]{2,1,0:T(8,128)(2,1)S(1)}, bf16[2,128,768]{2,1,0:T(8,128)(2,1)}, u32[]{:S(2)}) copy-start(bf16[2,128,768]{2,1,0:T(8,128)(2,1)} %reduce-scatter.2.cloned.1.call-done) | copy-start | bytes 1179652
  264.9 20.1 %copy-start.25 = (bf16[128,256]{1,0:T(8,128)(2,1)S(1)}, bf16[128,256]{1,0:T(8,128)(2,1)}, u32[]{:S(2)}) copy-start(bf16[128,256]{1,0:T(8,128)(2,1)} %param.25) | copy-start | bytes 196612
  265.0 20.3 %copy-start.31 = (bf16[256,12]{0,1:T(8,128)(2,1)S(1)}, bf16[256,12]{0,1:T(8,128)(2,1)}, u32[]{:S(2)}) copy-start(bf16[256,12]{0,1:T(8,128)(2,1)} %param.26) | copy-start | bytes 18436
  265.0 4.9 %collective-permute-start = (f32[6,768]{1,0:T(8,128)S(1)}, f32[6,768]{1,0:T(8,128)S(1)}, u32[]{:S(2)}, u32[]{:S(2)}) collective-permute-start(f32[6,768]{1,0:T(8,128)S(1)} %pad_maximum_fusion.9), channel_id=1, source_target_pairs={{0,1},{1,0},{2,3},{3,2},{4,5},{5,4},{6,7},{7,6},{8,9},{9,8},{10,11... | collective-permute-start | bytes 55304 | tf_op jit(solution)/shard_map/ppermute | solution.py:478
  269.9 4.8 %collective-permute-start.1 = (f32[6,768]{1,0:T(8,128)S(1)}, f32[6,768]{1,0:T(8,128)S(1)}, u32[]{:S(2)}, u32[]{:S(2)}) collective-permute-start(f32[6,768]{1,0:T(8,128)S(1)} %fusion.67), channel_id=1, source_target_pairs={{0,2},{1,3},{2,0},{3,1},{4,6},{5,7},{6,4},{7,5},{8,10},{9,11},{10,... | collective-permute-start | bytes 55304 | tf_op jit(solution)/shard_map/ppermute | solution.py:478
  274.7 1.2 collective-permute-start.2
  276.0 4.2 %collective-permute-start.3 = (f32[2,6,768]{2,1,0:T(8,128)S(1)}, f32[2,6,768]{2,1,0:T(8,128)S(1)}, u32[]{:S(2)}, u32[]{:S(2)}) collective-permute-start(f32[2,6,768]{2,1,0:T(8,128)S(1)} %pad_maximum_fusion.7), channel_id=1, source_target_pairs={{0,8},{4,12},{8,0},{12,4},{16,24},{20,28},{24,16},{28,20},{1,9},{5... | collective-permute-start | bytes 110600 | tf_op jit(solution)/shard_map/ppermute | solution.py:478
  280.1 4.7 %collective-permute-start.4 = (f32[4,6,768]{2,1,0:T(8,128)S(1)}, f32[4,6,768]{2,1,0:T(8,128)S(1)}, u32[]{:S(2)}, u32[]{:S(2)}) collective-permute-start(f32[4,6,768]{2,1,0:T(8,128)S(1)} %pad_maximum_fusion.4), channel_id=1, source_target_pairs={{0,16},{4,20},{8,24},{12,28},{16,0},{20,4},{24,8},{28,12},{1,17},{... | collective-permute-start | bytes 221192 | tf_op jit(solution)/shard_map/ppermute | solution.py:478
  284.8 6.4 %copy-start.1 = (bf16[768,768]{1,0:T(8,128)(2,1)S(1)}, bf16[768,768]{1,0:T(8,128)(2,1)}, u32[]{:S(2)}) copy-start(bf16[768,768]{1,0:T(8,128)(2,1)} %param.24) | copy-start | bytes 3538948
  (1 other events, 0.9 us)
Sparse Core Ops, SparseCore 0:
  9.6 39.7 all-gather.1
  121.3 35.6 reduce-scatter.1

commit v4 on v3

--- a/solution.py
+++ b/solution.py
@@ -60,104 +60,37 @@
     return jnp.concatenate([values[:head_size, :rows], values[head_size:, rows:]], axis=0).T
 
 
-def transposed_index(facts_ref, bins_ref, bin_count):
-    window = pl.program_id(0)
-    start = facts_ref[window]
+def attend_kernel(
+    head_size, bin_count, facts_ref, q_ref, k_ref, v_ref, bins_ref, table_ref, out_ref, probs_ref, index_ref
+):
+    rows, width = q_ref.shape
+    head_scale = 1.0 / math.sqrt(head_size)
+    start = facts_ref[pl.program_id(0)]
     offset = facts_ref[pl.num_programs(0)]
     bins = bins_ref[0].T
     key_first = lax.broadcasted_iota(jnp.int32, bins.shape, 0) < start
     row_first = lax.broadcasted_iota(jnp.int32, bins.shape, 1) + offset < start
-    return bins + jnp.where(key_first == row_first, bin_count, 0)
-
-
-def pair_scores(pair, cols, q_ref, k_ref, table_ref, index_ref, head_scale, head_size):
-    q_pair = pair_halves(q_ref[:, cols] * head_scale, head_size)
-    k_pair = k_ref[:, cols]
-    scores = dot_nt(k_pair, q_pair)
-    index = index_ref[...]
-    biases = []
-    for head in range(2):
-        entries = jnp.broadcast_to(table_ref[pl.ds(2 * pair + head, 1), :], index.shape)
-        biases.append(jnp.take_along_axis(entries, index, axis=1, mode="promise_in_bounds"))
-    return (q_pair, k_pair, scores + jnp.concatenate(biases, axis=1))
-
-
-def attend_kernel(
-    head_size, bin_count, facts_ref, q_ref, k_ref, v_ref, bins_ref, table_ref, out_ref, log_ref, index_ref
-):
-    rows, width = q_ref.shape
-    head_scale = 1.0 / math.sqrt(head_size)
-    index_ref[...] = transposed_index(facts_ref, bins_ref, bin_count)
+    index_ref[0] = bins + jnp.where(key_first == row_first, bin_count, 0)
 
     def one_pair(pair, carry):
         cols = pl.ds(pl.multiple_of(pair * 2 * head_size, 2 * head_size), 2 * head_size)
-        _, _, scores = pair_scores(
-            pair, cols, q_ref, k_ref, table_ref, index_ref, head_scale, head_size
-        )
+        index = index_ref[0]
+        biases = []
+        for head in range(2):
+            entries = jnp.broadcast_to(table_ref[pl.ds(2 * pair + head, 1), :], index.shape)
+            biases.append(jnp.take_along_axis(entries, index, axis=1, mode="promise_in_bounds"))
+        q_pair = pair_halves(q_ref[:, cols] * head_scale, head_size)
+        scores = dot_nt(k_ref[:, cols], q_pair) + jnp.concatenate(biases, axis=1)
         top = jnp.max(scores, axis=0, keepdims=True)
         raised = jnp.exp(scores - top)
         total = jnp.sum(raised, axis=0, keepdims=True)
         probs = (raised * (1.0 / total)).astype(bf16)
         mixed = dot(v_ref[:, cols].T, probs)
         out_ref[:, cols] = pair_diagonal(mixed, head_size, rows).astype(bf16)
-        log_ref[0, pl.ds(pair, 1), :] = top + jnp.log(total)
+        probs_ref[0, pair] = probs
         return carry
 
     lax.fori_loop(0, width // (2 * head_size), one_pair, 0)
-
-
-def attend_back_kernel(
-    head_size,
-    bin_count,
-    facts_ref,
-    q_ref,
-    k_ref,
-    v_ref,
-    bins_ref,
-    table_ref,
-    grad_ref,
-    log_ref,
-    grad_q_ref,
-    grad_kv_ref,
-    grad_scores_ref,
-    index_ref,
-):
-    rows, width = q_ref.shape
-    head_scale = 1.0 / math.sqrt(head_size)
-    index_ref[...] = transposed_index(facts_ref, bins_ref, bin_count)
-
-    def one_pair(pair, carry):
-        start = pl.multiple_of(pair * 2 * head_size, 2 * head_size)
-        cols = pl.ds(start, 2 * head_size)
-        v_cols = pl.ds(width + start, 2 * head_size)
-        q_pair, k_pair, scores = pair_scores(
-            pair, cols, q_ref, k_ref, table_ref, index_ref, head_scale, head_size
-        )
-        probs = jnp.exp(scores - log_ref[0, pl.ds(pair, 1), :])
-        g_pair = pair_halves(grad_ref[:, cols], head_size)
-        grad_kv_ref[:, v_cols] = dot(probs.astype(bf16), g_pair).astype(bf16)
-        grad_probs = dot_nt(v_ref[:, cols], g_pair)
-        delta = jnp.sum(probs * grad_probs, axis=0, keepdims=True)
-        grad_scores = (probs * (grad_probs - delta)).astype(bf16)
-        grad_kv_ref[:, cols] = dot(grad_scores, q_pair).astype(bf16)
-        grad_q = pair_diagonal(dot(k_pair.T, grad_scores), head_size, rows) * head_scale
-        grad_q_ref[:, cols] = grad_q.astype(bf16)
-        grad_scores_ref[0, 2 * pair] = grad_scores[:, :rows]
-        grad_scores_ref[0, 2 * pair + 1] = grad_scores[:, rows:]
-        return carry
-
-    lax.fori_loop(0, width // (2 * head_size), one_pair, 0)
-
-
-def attention_specs(rows, length, width, table_shape):
-    return [
-        pl.BlockSpec(memory_space=pltpu.SMEM),
-        pl.BlockSpec((rows, width), lambda w: (w, 0)),
-        pl.BlockSpec((length, width), lambda w: (w, 0)),
-        pl.BlockSpec((length, width), lambda w: (w, 1)),
-        pl.BlockSpec((1, rows, length), lambda w: (w, 0, 0)),
-        pl.BlockSpec(table_shape, lambda w: (0, 0)),
-    ]
 
 
 def attend(facts, queries, keys_values, bins, table, head_size):
@@ -167,16 +100,24 @@
     return pl.pallas_call(
         functools.partial(attend_kernel, head_size, table.shape[1] // 2),
         grid=(windows,),
-        in_specs=attention_specs(rows, length, width, table.shape),
+        in_specs=[
+            pl.BlockSpec(memory_space=pltpu.SMEM),
+            pl.BlockSpec((rows, width), lambda w: (w, 0)),
+            pl.BlockSpec((length, width), lambda w: (w, 0)),
+            pl.BlockSpec((length, width), lambda w: (w, 1)),
+            pl.BlockSpec((1, rows, length), lambda w: (w, 0, 0)),
+            pl.BlockSpec(table.shape, lambda w: (0, 0)),
+        ],
         out_specs=[
             pl.BlockSpec((rows, width), lambda w: (w, 0)),
-            pl.BlockSpec((1, pairs, 2 * rows), lambda w: (w, 0, 0)),
+            pl.BlockSpec((1, pairs, length, 2 * rows), lambda w: (w, 0, 0, 0)),
+            pl.BlockSpec((1, length, rows), lambda w: (w, 0, 0)),
         ],
         out_shape=[
             jax.ShapeDtypeStruct((windows * rows, width), bf16),
-            jax.ShapeDtypeStruct((windows, pairs, 2 * rows), f32),
+            jax.ShapeDtypeStruct((windows, pairs, length, 2 * rows), bf16),
+            jax.ShapeDtypeStruct((windows, length, rows), jnp.int32),
         ],
-        scratch_shapes=[pltpu.VMEM((length, rows), jnp.int32)],
         cost_estimate=pl.CostEstimate(
             flops=8 * windows * rows * length * width,
             bytes_accessed=4 * windows * rows * length,
@@ -184,38 +125,6 @@
         ),
         name="attend",
     )(facts, queries, keys_values, keys_values, bins, table)
-
-
-def attend_back(facts, queries, keys_values, bins, table, grads, logs, head_size):
-    windows, rows, length = bins.shape
-    width = queries.shape[1]
-    pairs = width // (2 * head_size)
-    return pl.pallas_call(
-        functools.partial(attend_back_kernel, head_size, table.shape[1] // 2),
-        grid=(windows,),
-        in_specs=attention_specs(rows, length, width, table.shape)
-        + [
-            pl.BlockSpec((rows, width), lambda w: (w, 0)),
-            pl.BlockSpec((1, pairs, 2 * rows), lambda w: (w, 0, 0)),
-        ],
-        out_specs=[
-            pl.BlockSpec((rows, width), lambda w: (w, 0)),
-            pl.BlockSpec((length, 2 * width), lambda w: (w, 0)),
-            pl.BlockSpec((1, 2 * pairs, length, rows), lambda w: (w, 0, 0, 0)),
-        ],
-        out_shape=[
-            jax.ShapeDtypeStruct((windows * rows, width), bf16),
-            jax.ShapeDtypeStruct((windows * length, 2 * width), bf16),
-            jax.ShapeDtypeStruct((windows, 2 * pairs, length, rows), bf16),
-        ],
-        scratch_shapes=[pltpu.VMEM((length, rows), jnp.int32)],
-        cost_estimate=pl.CostEstimate(
-            flops=20 * windows * rows * length * width,
-            bytes_accessed=8 * windows * rows * length * pairs,
-            transcendentals=windows * rows * length * 2 * pairs,
-        ),
-        name="attend_back",
-    )(facts, queries, keys_values, keys_values, bins, table, grads, logs)
 
 
 def bit_steps():
@@ -274,7 +183,7 @@
 
 
 class Flow:
-    def __init__(self, rows, columns, chunks, flip):
+    def __init__(self, rows, columns, chunks, flip, offset):
         steps = bit_steps()
         win_steps = [step for step in steps if step[0] == "win" and step != CORE]
         self.seq_steps = [step for step in steps if step[0] == "seq"]
@@ -282,6 +191,7 @@
         self.names = win_steps
         self.near = self.seq_steps[::-1]
         self.chunks = chunks
+        self.offset = offset
         self.width = columns // chunks
         self.share = rows // 2 ** len(steps)
         self.block = self.share * 2 ** len(self.seq_steps)
@@ -297,7 +207,7 @@
         shapes += [(2,) * (far - 1 - i) + (self.block, width) for i in range(far)]
         shapes += [(2,) * near + (self.share, width)]
         shapes += [(2,) * (near - 1 - i) + (self.share, width) for i in range(near)]
-        buffers = [pltpu.VMEM((chunks,) + shape, bf16) for shape in shapes]
+        buffers = [pltpu.VMEM((chunks if at else 2,) + shape, bf16) for at, shape in enumerate(shapes)]
         count = 1 + far + near
         return buffers + [
             pltpu.SemaphoreType.DMA((chunks,)),
@@ -321,7 +231,7 @@
 
     def local_copy(self, chunk):
         return pltpu.make_async_copy(
-            self.piece(my_bit(CORE), chunk), self.mine.at[chunk], self.local_sem.at[chunk]
+            self.piece(my_bit(CORE), chunk), self.mine.at[lax.rem(chunk, 2)], self.local_sem.at[chunk]
         )
 
     def copy(self, stage, chunk):
@@ -364,7 +274,8 @@
 
             def add_first(index):
                 at = (chunk,) + index
-                self.first[at] = (self.first[at].astype(f32) + self.mine[at].astype(f32)).astype(bf16)
+                kept = self.mine[(lax.rem(chunk, 2),) + index].astype(f32)
+                self.first[at] = (self.first[at].astype(f32) + kept).astype(bf16)
 
             each_block(shape, add_first)
         elif stage < 1 + far:
@@ -413,30 +324,269 @@
             self.copy(stage, chunk).wait_send()
 
 
-def reduce_kernel(flows, *refs):
-    count = len(flows)
-    scratch = list(refs[2 * count :])
-    for at, flow in enumerate(flows):
-        size = len(flow.scratch())
-        flow.bind(refs[at], refs[count + at], scratch[:size])
-        scratch = scratch[size:]
+class Load:
+    def __init__(self, source, target, sem):
+        self.target = target
+        self.copy = pltpu.make_async_copy(source, target, sem)
+
+
+class SmallGather:
+    def __init__(self, mine, halves, gathered, send_sem, recv_sem):
+        self.mine, self.halves, self.gathered = mine, halves, gathered
+        self.send_sem, self.recv_sem = send_sem, recv_sem
+        self.steps = bit_steps()[::-1]
+        self.seq_count = len([step for step in self.steps if step[0] == "seq"])
+
+    def copy(self, at):
+        step = self.steps[at]
+        if at < self.seq_count:
+            source, target = self.mine.at[at], self.halves.at[at]
+        else:
+            size = 1 << step[1]
+            here = lax.axis_index("win")
+            block = pl.ds(here - lax.rem(here, size), size)
+            source = target = self.gathered.at[block]
+        return remote(source, target, self.send_sem.at[at], self.recv_sem.at[at], step)
+
+    def run(self, at):
+        if at > 0:
+            self.copy(at - 1).wait_recv()
+            if at <= self.seq_count:
+                total = self.mine[at - 1] + self.halves[at - 1]
+                if at < self.seq_count:
+                    self.mine[at] = total
+                else:
+                    self.gathered[lax.axis_index("win")] = total
+        if at < len(self.steps):
+            self.copy(at).start()
+
+    def drain(self):
+        for at in range(len(self.steps)):
+            self.copy(at).wait_send()
+
+
+def norm_rows(values):
+    centered = values - jnp.mean(values, axis=-1, keepdims=True)
+    inv_std = lax.rsqrt(jnp.mean(centered * centered, axis=-1, keepdims=True) + norm_eps)
+    return (centered * inv_std, inv_std)
+
+
+def backward_kernel(flows, sizes, *refs):
+    windows, rows, length, head_size = sizes
+    refs = list(refs)
+
+    def take(count):
+        taken = refs[:count]
+        del refs[:count]
+        return taken
+
+    grads = take(4)
+    sources = take(9)
+    scale_ref, early_ref = take(2)
+    shares = take(6)
+    tokens_out, small_out = take(2)
+    targets = take(9)
+    (load_sem,) = take(1)
+    grad_q, grad_kv, grad_scores, q_weight, kv_weight, own_in = take(6)
+    far_in, far_half, far_own, far_send, far_recv = take(5)
+    (table_sum,) = take(1)
+    small = SmallGather(*take(5))
+    (small_sem,) = take(1)
+    for flow, grad, share in zip(flows, grads + [q_weight, kv_weight], shares):
+        flow.bind(grad, share, take(len(flow.scratch())))
+    loads = [Load(s, t, load_sem.at[at]) for at, (s, t) in enumerate(zip(sources, targets))]
+    q_ref, kv_ref, probs_ref, grad_ref, in_ref, weight_ref, index_ref, tokens_ref, hidden_ref = targets
+    width = q_ref.shape[1]
+    head_scale = 1.0 / math.sqrt(head_size)
+    heads = width // head_size
+    seq_steps = bit_steps()[::-1][: small.seq_count]
+    for load in loads:
+        load.copy.start()
+    greet()
+
+    def attend_back(window):
+        rows_at = pl.ds(pl.multiple_of(window * rows, rows), rows)
+        keys_at = pl.ds(pl.multiple_of(window * length, length), length)
+
+        def one_pair(pair, carry):
+            start = pl.multiple_of(pair * 2 * head_size, 2 * head_size)
+            cols = pl.ds(start, 2 * head_size)
+            v_cols = pl.ds(width + start, 2 * head_size)
+            q_pair = pair_halves(q_ref[rows_at, cols] * head_scale, head_size)
+            g_pair = pair_halves(grad_ref[rows_at, cols], head_size)
+            probs = probs_ref[window, pair]
+            grad_kv[keys_at, v_cols] = dot(probs, g_pair).astype(bf16)
+            grad_probs = dot_nt(kv_ref[keys_at, v_cols], g_pair)
+            probs = probs.astype(f32)
+            delta = jnp.sum(probs * grad_probs, axis=0, keepdims=True)
+            scores = (probs * (grad_probs - delta)).astype(bf16)
+            grad_kv[keys_at, cols] = dot(scores, q_pair).astype(bf16)
+            back = dot(kv_ref[keys_at, cols].T, scores)
+            grad_q[rows_at, cols] = (pair_diagonal(back, head_size, rows) * head_scale).astype(bf16)
+            grad_scores[window, 2 * pair] = scores[:, :rows]
+            grad_scores[window, 2 * pair + 1] = scores[:, rows:]
+            return carry
+
+        lax.fori_loop(0, heads // 2, one_pair, 0)
+
+    def split_rows(target, values, cols):
+        lead = target.shape[:-2]
+        block = target.shape[-2]
+        for at in range(math.prod(lead)):
+            index, rest = ((), at)
+            for size in lead[::-1]:
+                index = (rest % size,) + index
+                rest = rest // size
+            target[index + (slice(None), cols)] = values[at * block : (at + 1) * block].astype(bf16)
+
+    def project_back():
+        def one_window(window, carry):
+            keys_at = pl.ds(pl.multiple_of(window * length, length), length)
+            far = dot_nt(grad_kv[keys_at, :], weight_ref[:, width:]).astype(bf16)
+            split_owner(far, window)
+            return carry
+
+        def split_owner(far, window):
+            rows_at = pl.ds(pl.multiple_of(window * rows, rows), rows)
+            for owner in range(length // rows):
+                index, rest = ((), owner)
+                for _ in seq_steps:
+                    index = (rest % 2,) + index
+                    rest = rest // 2
+                far_in[index + (rows_at,)] = far[owner * rows : (owner + 1) * rows]
+
+        lax.fori_loop(0, windows, one_window, 0)
+        far_copy(0).start()
+        own_in[...] = dot_nt(grad_q[...], weight_ref[:, :width])
+
+    def weight_grads():
+        here = lax.axis_index("seq") * rows
+        own = [in_ref[pl.ds(pl.multiple_of(w * length + here, rows), rows), :] for w in range(windows)]
+        split_rows(q_weight, dot(jnp.concatenate(own, axis=0).T, grad_q[...]), slice(None))
+        turned = in_ref[...].T
+        step = 512
+        for at in range(2 * width // step):
+            cols = slice(at * step, (at + 1) * step)
+            split_rows(kv_weight, dot(turned, grad_kv[:, cols]), cols)
+
+    far_bufs = [far_in] + [far_half, far_own][-small.seq_count :]
+
+    def far_copy(at):
+        step = seq_steps[at]
+        index = (slice(None),) * (small.seq_count - 1 - at) + (1 - my_bit(step),)
+        return remote(
+            far_bufs[at].at[index], far_bufs[at + 1], far_send.at[at], far_recv.at[at], step
+        )
+
+    def far_add(at):
+        far_copy(at).wait_recv()
+        step = seq_steps[at]
+        bit = my_bit(step)
+        target, source = far_bufs[at + 1], far_bufs[at]
+        lead = target.shape[:-2]
+        for flat in range(math.prod(lead)):
+            for window in range(windows):
+                index = ((flat,) if lead else ()) + (pl.ds(window * rows, rows),)
+                kept = source[index[:-1] + (bit,) + index[-1:]].astype(f32)
+                target[index] = (target[index].astype(f32) + kept).astype(bf16)
+        if at + 1 < small.seq_count:
+            far_copy(at + 1).start()
+
+    def table_back(window):
+        group = 16
+        entries = table_sum.shape[1]
+
+        def one_group(at, carry):
+            keys = pl.ds(pl.multiple_of(at * group, group), group)
+            scores = grad_scores[window, :, keys, :].astype(f32)
+            scores = jnp.concatenate([scores, jnp.zeros((16 - heads, group, rows), f32)], axis=0)
+            scores = jnp.swapaxes(scores, 0, 1).astype(bf16)
+            index = index_ref[window, keys, :]
+            spot = lax.broadcasted_iota(jnp.int32, (entries, rows), 0)
+            total = jnp.zeros((16, entries), f32)
+            for key in range(0, group, 2):
+                terms, hots = [], []
+                for which in (key, key + 1):
+                    terms.append(scores[which])
+                    hot = spot == jnp.broadcast_to(index[which : which + 1], (entries, rows))
+                    hots.append(jnp.where(hot, 1.0, 0.0).astype(bf16))
+                total = total + dot_nt(
+                    jnp.concatenate(terms, axis=1), jnp.concatenate(hots, axis=1)
+                )
+            table_sum[...] += total
+            return carry
+
+        lax.fori_loop(0, length // group, one_group, 0)
+
+    def finish_tokens():
+        shift_rows, scale_rows = [], []
+        for window in range(windows):
+            rows_at = pl.ds(window * rows, rows)
+            normed, inv_std = norm_rows(tokens_ref[rows_at, :].astype(f32))
+            grad_in = own_in[rows_at, :] + far_own[rows_at, :].astype(f32)
+            shift_rows.append(jnp.sum(grad_in, axis=0, keepdims=True))
+            scale_rows.append(jnp.sum(grad_in * normed, axis=0, keepdims=True))
+            dy = grad_in * scale_ref[pl.ds(window, 1), :]
+            first = jnp.mean(dy, axis=-1, keepdims=True)
+            second = jnp.mean(dy * normed, axis=-1, keepdims=True)
+            back = (dy - first - normed * second) * inv_std
+            tokens_out[rows_at, :] = (hidden_ref[rows_at, :] + back).astype(bf16)
+        facts = jnp.concatenate(shift_rows + scale_rows + [early_ref[...]], axis=0)
+        small.mine[0, :, :width] = facts
+        small.mine[0, :, width:] = table_sum[...]
+
+    steps = len(small.steps)
+    jobs = {}
+    for window in range(windows):
+        jobs.setdefault(window, []).append(functools.partial(attend_back, window))
+    jobs.setdefault(windows, []).extend([project_back, weight_grads])
+    jobs.setdefault(windows + 1, []).append(functools.partial(table_back, 0))
+    jobs.setdefault(windows + 2, []).append(functools.partial(far_add, 0))
+    for window in range(1, windows):
+        jobs.setdefault(windows + 2 + window, []).append(functools.partial(table_back, window))
+    last = 2 * windows + 2
+    for at in range(1, small.seq_count):
+        jobs.setdefault(last + 2 * (at - 1), []).append(functools.partial(far_add, at))
+    last = last + 2 * (small.seq_count - 2)
+    jobs[last].append(finish_tokens)
+    for at in range(steps + 1):
+        jobs.setdefault(last + at, []).append(functools.partial(small.run, at))
     chunks = flows[0].chunks
     stages = flows[0].stages()
-    greet()
     order = [1, 0] + list(range(2, stages))
+    total = max(max(flow.offset for flow in flows) + chunks + stages - 1, max(jobs) + 1)
+    table_sum[...] = jnp.zeros_like(table_sum)
 
     def step(at, carry):
         for stage in order:
-            chunk = at - stage
-
-            @pl.when((chunk >= 0) & (chunk < chunks))
-            def _(stage=stage, chunk=chunk):
-                for flow in flows:
-                    flow.run(stage, chunk)
+            for offset in sorted({flow.offset for flow in flows}):
+                chunk = at - stage - offset
+
+                @pl.when((chunk >= 0) & (chunk < chunks))
+                def _(stage=stage, chunk=chunk, offset=offset):
+                    for flow in flows:
+                        if flow.offset == offset:
+                            flow.run(stage, chunk)
+
+            if stage == 0:
+
+                @pl.when(at == 0)
+                def _():
+                    for load in loads:
+                        load.copy.wait()
+
+                for when, work in sorted(jobs.items()):
+
+                    @pl.when(at == when)
+                    def _(work=work):
+                        for job in work:
+                            job()
 
         return carry
 
-    lax.fori_loop(0, chunks + stages - 1, step, 0)
+    lax.fori_loop(0, total, step, 0)
+    store_small = pltpu.make_async_copy(small.gathered, small_out, small_sem)
+    store_small.start()
 
     def finish(chunk, carry):
         for flow in flows:
@@ -444,48 +594,66 @@
         return carry
 
     lax.fori_loop(0, chunks, finish, 0)
-
-
-def reduce_grads(grads, chunks, flips, name, collective_id):
-    flows = [Flow(g.shape[0], g.shape[1], chunks, flip) for g, flip in zip(grads, flips)]
-    scratch = []
+    for at in range(small.seq_count):
+        far_copy(at).wait_send()
+    small.drain()
+    store_small.wait()
+
+
+def backward(grads, loads, scales, early, sizes, chunks, flips):
+    windows, rows, length, head_size = sizes
+    width = loads[0].shape[1]
+    shapes = [g.shape for g in grads] + [(width, width), (width, 2 * width)]
+    offsets = [0] * len(grads) + [windows + 1] * 2
+    flows = [Flow(s[0], s[1], chunks, flip, offset) for s, flip, offset in zip(shapes, flips, offsets)]
+    win_bits = int(math.log2(lax.axis_size("win")))
+    seq_bits = int(math.log2(lax.axis_size("seq")))
+    total_rows = windows * rows
+    small_shape = (16, width + 128)
+    heads = width // head_size
+    near = (2,) * seq_bits
+    scratch = [pltpu.VMEM(load.shape, load.dtype) for load in loads]
+    scratch += [
+        pltpu.SemaphoreType.DMA((len(loads),)),
+        pltpu.VMEM((total_rows, width), bf16),
+        pltpu.VMEM((windows * length, 2 * width), bf16),
+        pltpu.VMEM((windows, heads, length, rows), bf16),
+        pltpu.VMEM((2,) * win_bits + (flows[-2].block, width), bf16),
+        pltpu.VMEM((2,) * win_bits + (flows[-1].block, 2 * width), bf16),
+        pltpu.VMEM((total_rows, width), f32),
+        pltpu.VMEM(near + (total_rows, width), bf16),
+        pltpu.VMEM(near[1:] + (total_rows, width), bf16),
+        pltpu.VMEM((total_rows, width), bf16),
+        pltpu.SemaphoreType.DMA((seq_bits,)),
+        pltpu.SemaphoreType.DMA((seq_bits,)),
+        pltpu.VMEM((16, 128), f32),
+        pltpu.VMEM((seq_bits,) + small_shape, f32),
+        pltpu.VMEM((seq_bits,) + small_shape, f32),
+        pltpu.VMEM((2**win_bits,) + small_shape, f32),
+        pltpu.SemaphoreType.DMA((win_bits + seq_bits,)),
+        pltpu.SemaphoreType.DMA((win_bits + seq_bits,)),
+        pltpu.SemaphoreType.DMA,
+    ]
     for flow in flows:
         scratch += flow.scratch()
+    vmem = pl.BlockSpec(memory_space=pltpu.VMEM)
+    out_shape = [jax.ShapeDtypeStruct((flow.share, flow.columns), f32) for flow in flows]
+    out_shape += [
+        jax.ShapeDtypeStruct((total_rows, width), bf16),
+        jax.ShapeDtypeStruct((2**win_bits,) + small_shape, f32),
+    ]
     return pl.pallas_call(
-        functools.partial(reduce_kernel, flows),
-        in_specs=[pl.BlockSpec(memory_space=pl.ANY)] * len(flows),
-        out_specs=[pl.BlockSpec(memory_space=pltpu.VMEM)] * len(flows),
-        out_shape=[jax.ShapeDtypeStruct((flow.share, flow.columns), f32) for flow in flows],
+        functools.partial(backward_kernel, flows, sizes),
+        in_specs=[pl.BlockSpec(memory_space=pl.ANY)] * (len(grads) + len(loads)) + [vmem] * 2,
+        out_specs=[vmem] * (len(out_shape) - 1) + [pl.BlockSpec(memory_space=pl.ANY)],
+        out_shape=out_shape,
         scratch_shapes=scratch,
         compiler_params=pltpu.CompilerParams(
-            collective_id=collective_id, has_side_effects=True, vmem_limit_bytes=48 * 2**20
+            collective_id=1, has_side_effects=True, vmem_limit_bytes=62 * 2**20
         ),
-        cost_estimate=pl.CostEstimate(
-            flops=0, bytes_accessed=200 * 2**20, transcendentals=0
-        ),
-        name=name,
-    )(*[flow.view(grad) for flow, grad in zip(flows, grads)])
-
-
-def sum_seq(values):
-    for bit in range(int(math.log2(lax.axis_size("seq")))):
-        values = values + exchange(values, ("seq", bit))
-    return values
-
-
-def exchange(values, step):
-    size = lax.axis_size(step[0])
-    return lax.ppermute(values, step[0], [(i, i ^ (1 << step[1])) for i in range(size)])
-
-
-def gather_win(values):
-    out = values[None]
-    for bit in range(int(math.log2(lax.axis_size("win")))):
-        step = ("win", bit)
-        got = exchange(out, step)
-        low = my_bit(step) == 0
-        out = jnp.concatenate([jnp.where(low, out, got), jnp.where(low, got, out)], axis=0)
-    return out
+        cost_estimate=pl.CostEstimate(flops=10**10, bytes_accessed=200 * 2**20, transcendentals=0),
+        name="backward",
+    )(*[flow.view(grad) for flow, grad in zip(flows, grads)], *loads, scales, early)
 
 
 def three_parts(values):
@@ -555,7 +723,7 @@
     )
     queries = dot(attn_in, qkv_weight[:, :width]).astype(bf16)
     keys_values = dot(attn_in_all, qkv_weight[:, width:]).astype(bf16)
-    attn_mixed, log_totals = attend(facts, queries, keys_values, distance_bins, table, head_size)
+    attn_mixed, probs, pair_index = attend(facts, queries, keys_values, distance_bins, table, head_size)
     attn_out = dot(attn_mixed, out_weight).reshape(windows, row_count, width)
     gate_attn_sig = jax.nn.sigmoid(gate_attn)
     hidden_state = tokens_float + gate_attn_sig * attn_out
@@ -590,57 +758,42 @@
     grad_out = dot_tn(attn_mixed, grad_attn_out).astype(bf16)
     grad_mixed = dot_nt(grad_attn_out, out_weight).astype(bf16)
 
-    grad_query, grad_kv, grad_scores = attend_back(
-        facts, queries, keys_values, distance_bins, table, grad_mixed, log_totals, head_size
-    )
-    row_first = lax.axis_index("seq") * row_count + jnp.arange(row_count)[None, None, :] < chain_start[:, None, None]
-    key_first = jnp.arange(length)[None, :, None] < chain_start[:, None, None]
-    index_back = jnp.swapaxes(distance_bins, 1, 2) + bin_count * (row_first == key_first).astype(jnp.int32)
-    pair_onehot = (
-        index_back[:, None, :, :] == jnp.arange(table_rows, dtype=jnp.int32)[None, :, None, None]
-    ).astype(bf16)
-    grad_table = jnp.einsum("whji,wkji->kh", grad_scores, pair_onehot, preferred_element_type=f32)
-    grad_in_part = dot_nt(grad_kv, qkv_weight[:, width:]).astype(bf16)
-    grad_in_far = lax.psum_scatter(
-        grad_in_part.reshape(windows, length, width), "seq", scatter_dimension=1, tiled=True
-    )
-    grad_q_weight = dot_tn(attn_in, grad_query).astype(bf16)
-    grad_kv_weight = dot_tn(attn_in_all, grad_kv).astype(bf16)
-    owned_gate, owned_up, owned_down, owned_kv, owned_q, owned_out = reduce_grads(
-        [grad_gate, grad_up, grad_down, grad_kv_weight, grad_q_weight, grad_out],
+    early = jnp.concatenate(
+        [
+            grad_gate_attn,
+            grad_shift_ffn,
+            grad_scale_ffn,
+            grad_gate_ffn,
+            pre_cond / seq_count,
+            jnp.pad(class_onehot, ((0, 0), (0, width - classes))) / seq_count,
+        ],
+        axis=0,
+    )
+    owned_gate, owned_up, owned_down, owned_out, owned_q, owned_kv, grad_tokens, small = backward(
+        [grad_gate, grad_up, grad_down, grad_out],
+        [
+            queries,
+            keys_values,
+            probs,
+            grad_mixed,
+            attn_in_all,
+            qkv_weight,
+            pair_index,
+            tokens.reshape(total_rows, width),
+            grad_hidden.reshape(total_rows, width),
+        ],
+        1.0 + scale_attn.reshape(windows, width),
+        early,
+        (windows, row_count, length, head_size),
         6,
         [False, True, False, True, True, True],
-        "reduce_all",
-        1,
-    )
-    grad_attn_in = dot_nt(grad_query, qkv_weight[:, :width]).reshape(
-        windows, row_count, width
-    ) + grad_in_far.astype(f32)
-    grad_scale_attn = jnp.sum(grad_attn_in * normed_x, axis=1)
-    grad_shift_attn = jnp.sum(grad_attn_in, axis=1)
-    grad_tokens = (
-        grad_hidden + norm_back(grad_attn_in * (1.0 + scale_attn), normed_x, inv_x)
-    ).astype(bf16)
-    early_mod = jnp.stack([grad_gate_attn, grad_shift_ffn, grad_scale_ffn, grad_gate_ffn], axis=0)
-    early_mod = sum_seq(early_mod.reshape(4 * windows, width))
-    onehot_rows = jnp.pad(class_onehot, ((0, 0), (0, width - classes)))
-    early_all = gather_win(jnp.concatenate([early_mod, pre_cond, onehot_rows], axis=0))
-    late_mod = jnp.concatenate([grad_shift_attn, grad_scale_attn], axis=0)
-    table_size = table_rows * head_count
-    late = jnp.concatenate([late_mod, grad_table.reshape(table_size // width, width)], axis=0)
-    late_all = gather_win(sum_seq(late))
-    mod_all = jnp.concatenate(
-        [
-            late_all[:, : 2 * windows].reshape(win_count, 2, windows, width),
-            early_all[:, : 4 * windows].reshape(win_count, 4, windows, width),
-        ],
-        axis=1,
-    )
-    mod_all = jnp.swapaxes(mod_all, 1, 2).reshape(win_count * windows, 6 * width)
-    table_all = jnp.sum(late_all[:, 2 * windows :], axis=0).reshape(table_rows, head_count)
-    facts_all = early_all[:, 4 * windows :].reshape(win_count, 2, windows, width)
-    pre_all = facts_all[:, 0].reshape(win_count * windows, width)
-    onehot_all = facts_all[:, 1].reshape(win_count * windows, width)
+    )
+    grad_tokens = grad_tokens.reshape(windows, row_count, width)
+    rows_all = small[:, :, :width].reshape(win_count, 8, windows, width)
+    mod_all = jnp.swapaxes(rows_all[:, :6], 1, 2).reshape(win_count * windows, 6 * width)
+    table_all = jnp.sum(small[:, :head_count, width : width + table_rows], axis=0).T
+    pre_all = rows_all[:, 6].reshape(win_count * windows, width)
+    onehot_all = rows_all[:, 7].reshape(win_count * windows, width)
     ada_rows = width // devices
     sig_all = jax.nn.sigmoid(pre_all)
     condition_rows = lax.dynamic_slice_in_dim(pre_all * sig_all, owner * ada_rows, ada_rows, 1)

time: 299 us -> 243 us (0.81)
  matrix products: 65.2 us -> 48 us
  waiting for transfers between devices: 41.5 us -> 29.6 us
  starting transfers between devices: 10.8 us -> 0.04 us
  local copies, waits for them, and re-layouts: 21.4 us -> 13.2 us
  other arithmetic: 21.1 us -> 13.5 us
    ppermute x10 -> x0, waiting for transfers between devices: 19.9 us -> none  [exchange(): lax.ppermute(values, step[0], [(i, i ^ 1 << step[1]) for i in range(size)])]
    dot_general x1 -> x0, matrix products: 11 us -> none  [per_device(): jnp.einsum('whji,wkji->kh', grad_scores, pair_onehot, preferred_element_t...]
    ppermute x10 -> x0, starting transfers between devices: 10.7 us -> none  [exchange(): lax.ppermute(values, step[0], [(i, i ^ 1 << step[1]) for i in range(size)])]
    all_gather x1, waiting for transfers between devices: 20.9 us -> 28.9 us  [per_device(): tokens_all = lax.all_gather(tokens, 'seq', axis=1, tiled=True)]
    pallas_call x1 -> x0, local copies, waits for them, and re-layouts: 7.87 us -> none  [attend_back(): pl.pallas_call(functools.partial(attend_back_kernel, head_size, table.sha...]
    dot_general x6 -> x4, matrix products: 17 us -> 12.4 us  [dot_tn(): lax.dot_general(a, b, (((0,), (0,)), ((), ())), preferred_element_type=f32)]
    dot_general x6 -> x4, matrix products: 12.2 us -> 8.36 us  [dot_nt(): lax.dot_general(a, b, (((1,), (1,)), ((), ())), preferred_element_type=f32)]
    unnamed x114 -> x53, local copies, waits for them, and re-layouts: 7.19 us -> 3.82 us
  transfers between devices with their start and end apart: 12 -> 1, of which waited for: 8 -> 1; matrix products, arithmetic and copies ran while one was open for 18% -> 5% of each run, Pallas kernels for 32% -> 0%
where the time goes in v4:
time: 243 us; the launch traced here: 242 us
  Pallas kernels  123 us (51%)
  matrix products  48 us (20%)
  waiting for transfers between devices  29.6 us (12%)
  between operations  14.6 us (6%)
  other arithmetic  13.5 us (6%)
  local copies, waits for them, and re-layouts  13.2 us (5%)
    pallas_call x1, Pallas kernels, backward(): pl.pallas_call(functools.partial(backward_kernel, flows, sizes), in_specs...  110 us
    all_gather x1, waiting for transfers between devices, per_device(): tokens_all = lax.all_gather(tokens, 'seq', axis=1, tiled=True)  28.9 us
    dot_general x8, matrix products, dot(): return jnp.dot(a, b, preferred_element_type=f32)  21.4 us
    pallas_call x1, Pallas kernels, attend(): pl.pallas_call(functools.partial(attend_kernel, head_size, table.shape[1]...  13.3 us
    dot_general x4, matrix products, dot_tn(): lax.dot_general(a, b, (((0,), (0,)), ((), ())), preferred_element_type=f32)  12.4 us
    dot_general x4, matrix products, dot_nt(): lax.dot_general(a, b, (((1,), (1,)), ((), ())), preferred_element_type=f32)  8.36 us
  transfers between devices with their start and end apart: 1, of which 1 were waited for; matrix products, arithmetic and copies ran while one was open for 5% of the time, Pallas kernels for 0%

profile of v4, /device:TPU:0, one launch (start us, length us, event | category | flops | bytes accessed | tf_op | source)
XLA Modules:
  0.0 242.0 jit_solution(6345659352847953995)
XLA Ops:
  7.2 0.7 all-gather.2.cloned.1.call-update
  7.9 1.1 convert_reduce_fusion.1
  9.1 0.7 broadcast_multiply_fusion.5
  9.8 0.7 iota_compare_fusion
  10.5 0.1 multiply_sine_fusion
  10.6 0.9 reduce-precision_convert_fusion.1
  11.6 4.1 %fusion.26 = f32[6,4608]{1,0:T(8,128)S(1)} fusion(bf16[768,4608]{1,0:T(8,128)(2,1)} %param.22, bf16[2,768]{1,0:T(2,128)(2,1)S(1)} %get-tuple-element.61, bf16[2,768]{1,0:T(2,128)(2,1)S(1)} %get-tuple-element.60, bf16[2,768]{1,0:T(2,128)(2,1)S(1)} %get-tuple-element.44), kind=kOutput, calls=%fused_computation.65 | convolution fusion | flops 42494976 | bytes 7197696 | tf_op jit(solution)/shard_map/dot_general | solution.py:40
  15.8 0.6 pad_add_fusion.facts_ref
  16.4 0.2 fusion.16
  16.8 0.7 fusion.11.table_ref
  17.6 0.1 fusion.20
  17.6 0.3 fusion.19
  17.9 2.6 %convolution_convert_fusion.6.q_ref.refs_4_ = bf16[256,768]{1,0:T(8,128)(2,1)} fusion(bf16[256,768]{1,0:T(8,128)(2,1)S(1)} %bitcast.122, bf16[768,2304]{1,0:T(8,128)(2,1)} %refs_9_.1), kind=kOutput, calls=%fused_computation.21 | convolution fusion | flops 302186496 | bytes 1966080 | tf_op jit(solution)/shard_map/dot_general | solution.py:40
  20.5 28.9 %all-gather.2.cloned.1.call-done = bf16[2,512,768]{2,1,0:T(8,128)(2,1)} async-done(((bf16[2,128,768]{2,1,0:T(8,128)(2,1)}), bf16[2,512,768]{2,1,0:T(8,128)(2,1)}) %all-gather.2.cloned.1.call-update) | async-done | bytes 1572880 | tf_op jit(solution)/shard_map/all_gather | solution.py:697
  49.4 1.8 convert_reduce_fusion
  51.2 2.1 fusion.2
  53.4 0.7 fusion.5
  54.1 1.2 copy-done.4
  55.2 4.0 %convolution_convert_fusion.3.k_ref.v_ref.refs_5_ = bf16[1024,1536]{1,0:T(8,128)(2,1)} fusion(bf16[1024,768]{1,0:T(8,128)(2,1)S(1)} %bitcast.117, bf16[768,2304]{1,0:T(8,128)(2,1)S(1)} %copy-done.15), kind=kOutput, calls=%fused_computation.5 | convolution fusion | flops 2417491968 | bytes 7077888 | tf_op jit(solution)/shard_map/dot_general | solution.py:40
  59.2 13.3 %attend.1 = (bf16[256,768]{1,0:T(8,128)(2,1)}, bf16[2,6,512,256]{3,2,1,0:T(8,128)(2,1)}, s32[2,512,128]{2,1,0:T(8,128)}) custom-call(s32[3]{0:T(128)} %pad_add_fusion.facts_ref, bf16[256,768]{1,0:T(8,128)(2,1)} %convolution_convert_fusion.6.q_ref.refs_4_, bf16[1024,1536]{1,0:T(8,128)(2,1)} %convolution_convert_fusion.3.k_ref.v_ref.refs_5_, ...), custom_call_target="tpu_custom_call" | custom-call | flops 805306368 | bytes 524288 | tf_op jit(solution)/shard_map/attend/pallas_call | solution.py:100
  72.6 1.5 fusion.51
  74.0 0.2 fusion.49
  74.3 0.2 multiply_reduce_fusion.2
  74.5 0.2 add_convert_fusion.1
  74.7 3.9 %fusion.52 = f32[256,3072]{1,0:T(8,128)S(1)} fusion(bf16[256,768]{1,0:T(8,128)(2,1)S(1)} %bitcast.104, bf16[768,3072]{1,0:T(8,128)(2,1)} %param.27), kind=kOutput, calls=%fused_computation.120 | convolution fusion | flops 1207959552 | bytes 8257536 | tf_op jit(solution)/shard_map/dot_general | solution.py:40
  78.7 3.1 %fusion.53 = f32[256,3072]{1,0:T(8,128)} fusion(bf16[256,768]{1,0:T(8,128)(2,1)S(1)} %bitcast.105, bf16[768,3072]{1,0:T(8,128)(2,1)S(1)} %bitcast.109), kind=kOutput, calls=%fused_computation.121 | convolution fusion | flops 1207959552 | bytes 8257536 | tf_op jit(solution)/shard_map/dot_general | solution.py:40
  81.9 4.2 %multiply_convert_fusion = (bf16[256,3072]{1,0:T(8,128)(2,1)S(1)}, bf16[256,3072]{1,0:T(8,128)(2,1)S(1)}, bf16[256,3072]{1,0:T(8,128)(2,1)S(1)}) fusion(f32[256,3072]{1,0:T(8,128)S(1)} %fusion.52, f32[256,3072]{1,0:T(8,128)} %fusion.53, bf16[256,768]{1,0:T(8,128)(2,1)S(1)} %bitcast.115, bf16[3072,768]{1,0:T(8,128)(2,1)S(1)} %bitcast.136), kind=kOutput, calls=%fused_computation.12 | convolution fusion | flops 1219756032 | bytes 16121856 | tf_op jit(solution)/shard_map/dot_general | solution.py:44
  86.1 1.4 fusion.55
  87.5 3.6 %convolution_convert_fusion.2 = bf16[768,3072]{1,0:T(8,128)(2,1)} fusion(bf16[256,768]{1,0:T(8,128)(2,1)S(1)} %bitcast.106, bf16[256,3072]{1,0:T(8,128)(2,1)S(1)} %get-tuple-element.47), kind=kOutput, calls=%fused_computation.2 | convolution fusion | flops 1210318848 | bytes 6684672 | tf_op jit(solution)/shard_map/dot_general | solution.py:48
  91.1 1.4 fusion.54
  92.5 3.7 %convolution_convert_fusion = bf16[3072,768]{1,0:T(8,128)(2,1)} fusion(bf16[256,3072]{1,0:T(8,128)(2,1)S(1)} %get-tuple-element.48, bf16[256,768]{1,0:T(8,128)(2,1)S(1)} %bitcast.116), kind=kOutput, calls=%fused_computation | convolution fusion | flops 1210318848 | bytes 6684672 | tf_op jit(solution)/shard_map/dot_general | solution.py:48
  96.2 3.6 %convolution_convert_fusion.1 = bf16[768,3072]{1,0:T(8,128)(2,1)} fusion(bf16[256,768]{1,0:T(8,128)(2,1)S(1)} %bitcast.107, bf16[256,3072]{1,0:T(8,128)(2,1)S(1)} %get-tuple-element.46), kind=kOutput, calls=%fused_computation.1 | convolution fusion | flops 1210318848 | bytes 6684672 | tf_op jit(solution)/shard_map/dot_general | solution.py:48
  99.8 1.5 fusion.24
  101.3 0.4 fusion.25
  101.7 1.4 multiply_reduce_fusion
  103.2 1.6 convolution_convert_fusion.4
  104.8 1.2 convolution_convert_fusion.5.refs_7_
  106.0 1.3 concatenate.18.refs_14_
  107.3 109.7 %backward.1 = (f32[24,3072]{1,0:T(8,128)}, f32[24,3072]{1,0:T(8,128)}, f32[96,768]{1,0:T(8,128)}, f32[24,768]{1,0:T(8,128)}, f32[24,768]{1,0:T(8,128)}, /*index=...) custom-call(bf16[2,2,2,96,3072]{4,3,2,1,0:T(8,128)(2,1)} %bitcast.101, ...), custom_call_target="tpu_custom_call" | custom-call | flops 10000000000 | bytes 209715200 | tf_op jit(solution)/shard_map/backward/pallas_call | solution.py:645
  217.0 1.1 slice.47
  218.1 0.2 reshape.178
  218.4 0.9 slice_reduce_fusion
  219.3 1.0 convolution_bitcast_fusion
  220.3 0.1 convolution_bitcast_fusion.1
  220.5 0.1 copy.46
  220.5 0.1 copy.48
  220.7 0.6 add_divide_fusion.1
  221.3 0.7 reshape_squeeze.7
  222.0 1.3 fusion.32
  223.3 0.8 reshape.180
  224.1 0.9 pad_maximum_fusion
  225.0 0.7 reshape.181
  225.7 1.5 reshape.182
  227.2 0.1 copy.49
  227.3 0.1 copy.39
  227.4 0.1 reshape.184
  227.6 0.8 copy.50
  228.3 0.8 copy.51
  229.1 0.7 reshape.187
  229.8 0.9 dynamic-slice_reduce_fusion
  230.7 2.5 %fusion.12 = f32[96]{0:T(128)} fusion(f32[16,4608]{1,0:T(8,128)S(1)} %bitcast.114, bf16[768,4608]{1,0:T(8,128)(2,1)} %param.22, s32[]{:T(128)S(6)} %select_n.29, f32[16,768]{1,0:T(8,128)} %add_divide_fusion.1, f32[16,768]{1,0:T(8,128)S(1)} %reshape_squeeze.6, f32[16]{0:T(128)S(1)} %dynamic-slice_reduce_fusion), kind=kOutput, calls=%fused_computation.37 | convolution fusion | flops 84945312 | bytes 1195456 | tf_op jit(solution)/shard_map/dot_general | solution.py:809
  233.2 0.6 dynamic_slice.26
  233.8 0.6 dynamic_slice.27
  234.4 0.7 copy.77
  (70 shorter events, 0.5 us)
Async XLA Ops:
  7.2 65.4 %copy-start = (bf16[768,768]{1,0:T(8,128)(2,1)S(1)}, bf16[768,768]{1,0:T(8,128)(2,1)}, u32[]{:S(2)}) copy-start(bf16[768,768]{1,0:T(8,128)(2,1)} %param.24) | copy-start | bytes 3538948
  7.2 42.2 %all-gather.2.cloned.1.call-start = ((), (), s32[]{:S(2)}) async-start(), calls=%async_computation | async-start | bytes 1966080 | tf_op jit(solution)/shard_map/all_gather | solution.py:697
  11.6 4.3 %copy-start.16 = (s32[2]{0:T(128)S(1)}, s32[2]{0:T(128)}, u32[]{:S(2)}) copy-start(s32[2]{0:T(128)} %param.19) | copy-start | bytes 28
  11.6 4.9 %copy-start.2 = (bf16[2,128,768]{2,1,0:T(8,128)(2,1)S(1)}, bf16[2,128,768]{2,1,0:T(8,128)(2,1)}, u32[]{:S(2)}) copy-start(bf16[2,128,768]{2,1,0:T(8,128)(2,1)} %param.15) | copy-start | bytes 1179652
  11.6 5.2 %copy-start.11 = (bf16[128,256]{1,0:T(8,128)(2,1)S(1)}, bf16[128,256]{1,0:T(8,128)(2,1)}, u32[]{:S(2)}) copy-start(bf16[128,256]{1,0:T(8,128)(2,1)} %param.25) | copy-start | bytes 196612
  11.6 5.2 %copy-start.14 = (bf16[256,12]{0,1:T(8,128)(2,1)S(1)}, bf16[256,12]{0,1:T(8,128)(2,1)}, u32[]{:S(2)}) copy-start(bf16[256,12]{0,1:T(8,128)(2,1)} %param.26) | copy-start | bytes 18436
  11.6 6.0 %copy-start.5 = (bf16[2,128,768]{2,1,0:T(8,128)(2,1)S(1)}, bf16[2,128,768]{2,1,0:T(8,128)(2,1)}, u32[]{:S(2)}) copy-start(bf16[2,128,768]{2,1,0:T(8,128)(2,1)} %param.16) | copy-start | bytes 1179652
  16.8 36.6 %copy-start.13 = (f32[2,768]{1,0:T(2,128)}, f32[2,768]{1,0:T(2,128)S(1)}, u32[]{:S(2)}) copy-start(f32[2,768]{1,0:T(2,128)S(1)} %get-tuple-element.68.refs_13_) | copy-start | bytes 18436
  49.4 4.0 %copy-start.1 = (bf16[2,512,768]{2,1,0:T(8,128)(2,1)S(1)}, bf16[2,512,768]{2,1,0:T(8,128)(2,1)}, u32[]{:S(2)}) copy-start(bf16[2,512,768]{2,1,0:T(8,128)(2,1)} %all-gather.2.cloned.1.call-done) | copy-start | bytes 4718596
  49.4 5.9 %copy-start.15 = (bf16[768,2304]{1,0:T(8,128)(2,1)S(1)}, bf16[768,2304]{1,0:T(8,128)(2,1)}, u32[]{:S(2)}) copy-start(bf16[768,2304]{1,0:T(8,128)(2,1)} %refs_9_.1) | copy-start | bytes 10616836
  54.1 1.2 copy-start.4
  74.5 4.2 %slice-start = ((s8[4718592]{0:T(1024)(128)(4,1)}), s8[4194304]{0:T(1024)(128)(4,1)S(1)}, s32[]{:S(2)}) async-start(s8[4718592]{0:T(1024)(128)(4,1)} %bitcast.108), calls=%async_computation.1 | async-start | bytes 8388608
  74.7 4.0 %slice-start.1 = ((s8[4718592]{0:T(1024)(128)(4,1)}), s8[524288]{0:T(1024)(128)(4,1)S(1)}, s32[]{:S(2)}) async-start(s8[4718592]{0:T(1024)(128)(4,1)} %bitcast.108), calls=%async_computation.2 | async-start | bytes 1048576
  74.7 7.2 %slice-start.4 = ((s8[4718592]{0:T(1024)(128)(4,1)}), s8[4194304]{0:T(1024)(128)(4,1)S(1)}, s32[]{:S(2)}) async-start(s8[4718592]{0:T(1024)(128)(4,1)} %bitcast.135), calls=%async_computation.5 | async-start | bytes 8388608
  78.7 3.2 %slice-start.5 = ((s8[4718592]{0:T(1024)(128)(4,1)}), s8[524288]{0:T(1024)(128)(4,1)S(1)}, s32[]{:S(2)}) async-start(s8[4718592]{0:T(1024)(128)(4,1)} %bitcast.135), calls=%async_computation.6 | async-start | bytes 1048576
  78.7 7.4 %slice-start.2 = ((s8[4718592]{0:T(1024)(128)(4,1)}), s8[4194304]{0:T(1024)(128)(4,1)S(1)}, s32[]{:S(2)}) async-start(s8[4718592]{0:T(1024)(128)(4,1)} %bitcast.133), calls=%async_computation.3 | async-start | bytes 8388608
  81.9 4.2 %slice-start.3 = ((s8[4718592]{0:T(1024)(128)(4,1)}), s8[524288]{0:T(1024)(128)(4,1)S(1)}, s32[]{:S(2)}) async-start(s8[4718592]{0:T(1024)(128)(4,1)} %bitcast.133), calls=%async_computation.4 | async-start | bytes 1048576
  101.7 1.5 copy-start.6
  103.1 4.1 %copy-start.3 = (f32[2,128,768]{2,1,0:T(8,128)}, f32[2,128,768]{2,1,0:T(8,128)S(1)}, u32[]{:S(2)}) copy-start(f32[2,128,768]{2,1,0:T(8,128)S(1)} %get-tuple-element.39) | copy-start | bytes 2359300
  217.0 7.1 %copy-start.12 = (f32[24,1536]{1,0:T(8,128)S(1)}, f32[24,1536]{1,0:T(8,128)}, u32[]{:S(2)}) copy-start(f32[24,1536]{1,0:T(8,128)} %get-tuple-element.28) | copy-start | bytes 442372
  218.3 9.2 %copy-start.10 = (f32[24,3072]{1,0:T(8,128)S(1)}, f32[24,3072]{1,0:T(8,128)}, u32[]{:S(2)}) copy-start(f32[24,3072]{1,0:T(8,128)} %get-tuple-element.30) | copy-start | bytes 884740
  218.4 9.9 %copy-start.9 = (f32[24,3072]{1,0:T(8,128)S(1)}, f32[24,3072]{1,0:T(8,128)}, u32[]{:S(2)}) copy-start(f32[24,3072]{1,0:T(8,128)} %get-tuple-element.31) | copy-start | bytes 884740
  219.3 9.8 %copy-start.8 = (f32[96,768]{1,0:T(8,128)S(1)}, f32[96,768]{1,0:T(8,128)}, u32[]{:S(2)}) copy-start(f32[96,768]{1,0:T(8,128)} %get-tuple-element.32) | copy-start | bytes 884740
  221.3 13.1 %copy-start.7 = (bf16[256,768]{1,0:T(8,128)(2,1)S(1)}, bf16[256,768]{1,0:T(8,128)(2,1)}, u32[]{:S(2)}) copy-start(bf16[256,768]{1,0:T(8,128)(2,1)} %get-tuple-element.25) | copy-start | bytes 1179652
Sparse Core Ops, SparseCore 0:
  9.6 39.7 all-gather.1

commit v5 on v4

--- a/solution.py
+++ b/solution.py
@@ -60,71 +60,208 @@
     return jnp.concatenate([values[:head_size, :rows], values[head_size:, rows:]], axis=0).T
 
 
-def attend_kernel(
-    head_size, bin_count, facts_ref, q_ref, k_ref, v_ref, bins_ref, table_ref, out_ref, probs_ref, index_ref
+def forward_kernel(
+    sizes,
+    facts_ref,
+    tokens_ref,
+    cond_ref,
+    table_ref,
+    ada_hbm,
+    weight_hbm,
+    bins_hbm,
+    mod_ref,
+    q_ref,
+    kv_ref,
+    in_ref,
+    mixed_ref,
+    probs_ref,
+    index_ref,
+    ada_ref,
+    weight_ref,
+    bins_ref,
+    load_sem,
+    gathered,
+    send_sem,
+    recv_sem,
 ):
-    rows, width = q_ref.shape
+    windows, rows, length, head_size = sizes
+    width = q_ref.shape[1]
+    count = gathered.shape[0]
+    here = lax.axis_index("seq")
     head_scale = 1.0 / math.sqrt(head_size)
-    start = facts_ref[pl.program_id(0)]
-    offset = facts_ref[pl.num_programs(0)]
-    bins = bins_ref[0].T
-    key_first = lax.broadcasted_iota(jnp.int32, bins.shape, 0) < start
-    row_first = lax.broadcasted_iota(jnp.int32, bins.shape, 1) + offset < start
-    index_ref[0] = bins + jnp.where(key_first == row_first, bin_count, 0)
-
-    def one_pair(pair, carry):
-        cols = pl.ds(pl.multiple_of(pair * 2 * head_size, 2 * head_size), 2 * head_size)
-        index = index_ref[0]
-        biases = []
-        for head in range(2):
-            entries = jnp.broadcast_to(table_ref[pl.ds(2 * pair + head, 1), :], index.shape)
-            biases.append(jnp.take_along_axis(entries, index, axis=1, mode="promise_in_bounds"))
-        q_pair = pair_halves(q_ref[:, cols] * head_scale, head_size)
-        scores = dot_nt(k_ref[:, cols], q_pair) + jnp.concatenate(biases, axis=1)
-        top = jnp.max(scores, axis=0, keepdims=True)
-        raised = jnp.exp(scores - top)
-        total = jnp.sum(raised, axis=0, keepdims=True)
-        probs = (raised * (1.0 / total)).astype(bf16)
-        mixed = dot(v_ref[:, cols].T, probs)
-        out_ref[:, cols] = pair_diagonal(mixed, head_size, rows).astype(bf16)
-        probs_ref[0, pair] = probs
+    loads = [
+        Load(source, target, load_sem.at[at])
+        for at, (source, target) in enumerate(
+            [(ada_hbm, ada_ref), (weight_hbm, weight_ref), (bins_hbm, bins_ref)]
+        )
+    ]
+    for load in loads:
+        load.copy.start()
+    barrier = pltpu.get_barrier_semaphore()
+    for sign in (1, -1):
+
+        @pl.when((here + sign >= 0) & (here + sign < count))
+        def _(sign=sign):
+            pl.semaphore_signal(
+                barrier, inc=1, device_id={"seq": here + sign}, device_id_type=pl.DeviceIdType.MESH
+            )
+
+    pl.semaphore_wait(barrier, jnp.where((here == 0) | (here == count - 1), 1, 2))
+
+    def copy(way, hop, window, shard, source=None):
+        slot = gathered.at[shard, window]
+        return pltpu.make_async_remote_copy(
+            src_ref=slot if source is None else source,
+            dst_ref=slot,
+            send_sem=send_sem.at[way, hop, window],
+            recv_sem=recv_sem.at[way, hop, window],
+            device_id={"seq": here + 1 - 2 * way},
+            device_id_type=pl.DeviceIdType.MESH,
+        )
+
+    def for_sends(body):
+        for window in range(windows):
+            for way in range(2):
+
+                @pl.when((here + 1 - 2 * way >= 0) & (here + 1 - 2 * way < count))
+                def _(way=way, window=window):
+                    body(copy(way, 0, window, here, tokens_ref.at[window]))
+
+    for_sends(lambda each: each.start())
+    loads[0].copy.wait()
+    for part in range(mod_ref.shape[1] // width):
+        cols = slice(part * width, (part + 1) * width)
+        mod = dot(cond_ref[...], ada_ref[:, cols])
+        mod_ref[:, cols] = mod[:8] + mod[8:16] + mod[16:24]
+    loads[1].copy.wait()
+    loads[2].copy.wait()
+
+    def project(window, shard, values):
+        normed, _ = norm_rows(values.astype(f32))
+        scale = 1.0 + mod_ref[pl.ds(window, 1), width : 2 * width]
+        block = (normed * scale + mod_ref[pl.ds(window, 1), :width]).astype(bf16)
+        at = pl.ds(pl.multiple_of(window * length + shard * rows, rows), rows)
+        in_ref[at, :] = block
+        kv_ref[at, :] = dot(block, weight_ref[:, width:]).astype(bf16)
+        return block
+
+    def own(window, carry):
+        block = project(window, here, tokens_ref[window])
+        at = pl.ds(pl.multiple_of(window * rows, rows), rows)
+        q_ref[at, :] = dot(block, weight_ref[:, :width]).astype(bf16)
         return carry
 
-    lax.fori_loop(0, width // (2 * head_size), one_pair, 0)
-
-
-def attend(facts, queries, keys_values, bins, table, head_size):
+    lax.fori_loop(0, windows, own, 0)
+
+    def arrive(way, hop, window):
+        sign = 1 - 2 * way
+        shard = here - sign * (hop + 1)
+
+        @pl.when((shard >= 0) & (shard < count))
+        def _():
+            copy(way, hop, window, shard).wait_recv()
+
+            @pl.when((here + sign >= 0) & (here + sign < count))
+            def _():
+                copy(way, hop + 1, window, shard).start()
+
+            project(window, shard, gathered[shard, window])
+
+    def relay(at, carry):
+        arrive(lax.rem(at, 2), at // (2 * windows), lax.rem(at // 2, windows))
+        return carry
+
+    lax.fori_loop(0, (count - 2) * windows * 2, relay, 0)
+
+    def finish(window, carry):
+        def last(way, inner):
+            arrive(way, count - 2, window)
+            return inner
+
+        lax.fori_loop(0, 2, last, 0)
+        rows_at = pl.ds(pl.multiple_of(window * rows, rows), rows)
+        keys_at = pl.ds(pl.multiple_of(window * length, length), length)
+        start = facts_ref[window]
+        bins = bins_ref[window].T
+        key_first = lax.broadcasted_iota(jnp.int32, bins.shape, 0) < start
+        row_first = lax.broadcasted_iota(jnp.int32, bins.shape, 1) + here * rows < start
+        index_ref[window] = bins + jnp.where(key_first == row_first, table_ref.shape[1] // 2, 0)
+
+        def one_pair(pair, inner):
+            begin = pl.multiple_of(pair * 2 * head_size, 2 * head_size)
+            cols = pl.ds(begin, 2 * head_size)
+            v_cols = pl.ds(width + begin, 2 * head_size)
+            index = index_ref[window]
+            biases = []
+            for head in range(2):
+                entries = jnp.broadcast_to(table_ref[pl.ds(2 * pair + head, 1), :], index.shape)
+                biases.append(jnp.take_along_axis(entries, index, axis=1, mode="promise_in_bounds"))
+            q_pair = pair_halves(q_ref[rows_at, cols] * head_scale, head_size)
+            scores = dot_nt(kv_ref[keys_at, cols], q_pair) + jnp.concatenate(biases, axis=1)
+            top = jnp.max(scores, axis=0, keepdims=True)
+            raised = jnp.exp(scores - top)
+            total = jnp.sum(raised, axis=0, keepdims=True)
+            probs = (raised * (1.0 / total)).astype(bf16)
+            mixed = dot(kv_ref[keys_at, v_cols].T, probs)
+            mixed_ref[rows_at, cols] = pair_diagonal(mixed, head_size, rows).astype(bf16)
+            probs_ref[window, pair] = probs
+            return inner
+
+        lax.fori_loop(0, width // (2 * head_size), one_pair, 0)
+        return carry
+
+    lax.fori_loop(0, windows, finish, 0)
+    for_sends(lambda each: each.wait_send())
+
+    def sent(at, carry):
+        way, hop, window = (lax.rem(at, 2), at // (2 * windows), lax.rem(at // 2, windows))
+        sign = 1 - 2 * way
+        shard = here - sign * (hop + 1)
+
+        @pl.when((shard >= 0) & (shard < count) & (here + sign >= 0) & (here + sign < count))
+        def _():
+            copy(way, hop + 1, window, shard).wait_send()
+
+        return carry
+
+    lax.fori_loop(0, (count - 2) * windows * 2, sent, 0)
+
+
+def forward(facts, tokens, cond_parts, table, ada_weight, qkv_weight, bins, head_size):
     windows, rows, length = bins.shape
-    width = queries.shape[1]
+    width = tokens.shape[-1]
     pairs = width // (2 * head_size)
+    count = lax.axis_size("seq")
+    vmem = pl.BlockSpec(memory_space=pltpu.VMEM)
+    hbm = pl.BlockSpec(memory_space=pl.ANY)
     return pl.pallas_call(
-        functools.partial(attend_kernel, head_size, table.shape[1] // 2),
-        grid=(windows,),
-        in_specs=[
-            pl.BlockSpec(memory_space=pltpu.SMEM),
-            pl.BlockSpec((rows, width), lambda w: (w, 0)),
-            pl.BlockSpec((length, width), lambda w: (w, 0)),
-            pl.BlockSpec((length, width), lambda w: (w, 1)),
-            pl.BlockSpec((1, rows, length), lambda w: (w, 0, 0)),
-            pl.BlockSpec(table.shape, lambda w: (0, 0)),
-        ],
-        out_specs=[
-            pl.BlockSpec((rows, width), lambda w: (w, 0)),
-            pl.BlockSpec((1, pairs, length, 2 * rows), lambda w: (w, 0, 0, 0)),
-            pl.BlockSpec((1, length, rows), lambda w: (w, 0, 0)),
-        ],
+        functools.partial(forward_kernel, (windows, rows, length, head_size)),
+        in_specs=[pl.BlockSpec(memory_space=pltpu.SMEM), vmem, vmem, vmem, hbm, hbm, hbm],
+        out_specs=[vmem] * 7,
         out_shape=[
+            jax.ShapeDtypeStruct((8, ada_weight.shape[1]), f32),
+            jax.ShapeDtypeStruct((windows * rows, width), bf16),
+            jax.ShapeDtypeStruct((windows * length, 2 * width), bf16),
+            jax.ShapeDtypeStruct((windows * length, width), bf16),
             jax.ShapeDtypeStruct((windows * rows, width), bf16),
             jax.ShapeDtypeStruct((windows, pairs, length, 2 * rows), bf16),
             jax.ShapeDtypeStruct((windows, length, rows), jnp.int32),
         ],
-        cost_estimate=pl.CostEstimate(
-            flops=8 * windows * rows * length * width,
-            bytes_accessed=4 * windows * rows * length,
-            transcendentals=windows * rows * length * 2 * pairs,
+        scratch_shapes=[
+            pltpu.VMEM(ada_weight.shape, bf16),
+            pltpu.VMEM(qkv_weight.shape, bf16),
+            pltpu.VMEM(bins.shape, jnp.int32),
+            pltpu.SemaphoreType.DMA((3,)),
+            pltpu.VMEM((count, windows, rows, width), bf16),
+            pltpu.SemaphoreType.DMA((2, count - 1, windows)),
+            pltpu.SemaphoreType.DMA((2, count - 1, windows)),
+        ],
+        compiler_params=pltpu.CompilerParams(
+            collective_id=0, has_side_effects=True, vmem_limit_bytes=48 * 2**20
         ),
-        name="attend",
-    )(facts, queries, keys_values, keys_values, bins, table)
+        cost_estimate=pl.CostEstimate(flops=10**10, bytes_accessed=40 * 2**20, transcendentals=0),
+        name="forward",
+    )(facts, tokens, cond_parts, table, ada_weight, qkv_weight, bins)
 
 
 def bit_steps():
@@ -694,36 +831,34 @@
     seq_count = lax.axis_size("seq")
     devices = win_count * seq_count
     owner = lax.axis_index("win") * seq_count + lax.axis_index("seq")
-    tokens_all = lax.all_gather(tokens, "seq", axis=1, tiled=True)
     class_onehot = (cath_ids[:, None] == jnp.arange(classes, dtype=jnp.int32)[None, :]).astype(f32)
     pre_cond = jnp.dot(
         class_onehot, class_table.astype(f32), precision=highest
     ) + time_embed(noise_times, width)
     cond_sig = jax.nn.sigmoid(pre_cond)
     condition = pre_cond * cond_sig
-    modulation = dot(jnp.concatenate(three_parts(condition), axis=0), ada_weight)
-    modulation = jnp.sum(modulation.reshape(3, windows, 6, width), axis=0)
+    cond_parts = jnp.concatenate(
+        [jnp.pad(part, ((0, 8 - windows), (0, 0))) for part in three_parts(condition)], axis=0
+    )
+    table_bias = dot(pair_table, pair_weight).astype(bf16)
+    modulation, queries, keys_values, attn_in_all, attn_mixed, probs, pair_index = forward(
+        chain_start,
+        tokens,
+        cond_parts,
+        table_bias.astype(f32).T,
+        ada_weight,
+        qkv_weight,
+        distance_bins,
+        head_size,
+    )
+    modulation = modulation[:windows].reshape(windows, 6, width)
     shift_attn = modulation[:, 0][:, None, :]
     scale_attn = modulation[:, 1][:, None, :]
     gate_attn = modulation[:, 2][:, None, :]
     shift_ffn = modulation[:, 3][:, None, :]
     scale_ffn = modulation[:, 4][:, None, :]
     gate_ffn = modulation[:, 5][:, None, :]
-    table_bias = dot(pair_table, pair_weight).astype(bf16)
-    facts = jnp.concatenate(
-        [chain_start, jnp.full((1,), lax.axis_index("seq") * row_count, jnp.int32)]
-    )
-    table = table_bias.astype(f32).T
     tokens_float = tokens.astype(f32)
-    normed_x, inv_x = layer_norm_parts(tokens_float)
-    attn_in = (normed_x * (1.0 + scale_attn) + shift_attn).astype(bf16).reshape(total_rows, width)
-    normed_all, _ = layer_norm_parts(tokens_all.astype(f32))
-    attn_in_all = (
-        (normed_all * (1.0 + scale_attn) + shift_attn).astype(bf16).reshape(windows * length, width)
-    )
-    queries = dot(attn_in, qkv_weight[:, :width]).astype(bf16)
-    keys_values = dot(attn_in_all, qkv_weight[:, width:]).astype(bf16)
-    attn_mixed, probs, pair_index = attend(facts, queries, keys_values, distance_bins, table, head_size)
     attn_out = dot(attn_mixed, out_weight).reshape(windows, row_count, width)
     gate_attn_sig = jax.nn.sigmoid(gate_attn)
     hidden_state = tokens_float + gate_attn_sig * attn_out

time: 243 us -> 207 us (0.85)
  waiting for transfers between devices: 29.6 us -> 0 us
  Pallas kernels: 123 us -> 149 us
  between operations: 14.6 us -> 1.08 us
  matrix products: 48 us -> 35.2 us
  other arithmetic: 13.5 us -> 5.99 us
    pallas_call x1, Pallas kernels: 13.3 us -> 42.6 us  [forward(): pl.pallas_call(functools.partial(forward_kernel, (windows, rows, length,...]
    all_gather x1 -> x0, waiting for transfers between devices: 28.9 us -> none  [per_device(): tokens_all = lax.all_gather(tokens, 'seq', axis=1, tiled=True)]
    dot_general x8 -> x5, matrix products: 21.4 us -> 8.94 us  [dot(): return jnp.dot(a, b, preferred_element_type=f32)]
    pallas_call x1, Pallas kernels: 110 us -> 107 us  [backward(): pl.pallas_call(functools.partial(backward_kernel, flows, sizes), in_specs...]
    reduce_sum x3 -> x1, other arithmetic: 3.17 us -> 0.2 us  [layer_norm_parts(): centered = values - jnp.mean(values, axis=-1, keepdims=True)]
    unnamed x53 -> x49, local copies, waits for them, and re-layouts: 3.82 us -> 6.56 us
  transfers between devices with their start and end apart: 1 -> 0, of which waited for: 1 -> 0; matrix products, arithmetic and copies ran while one was open for 5% -> 0% of each run, Pallas kernels for 0% -> 0%
where the time goes in v5:
time: 207 us; the launch traced here: 206 us
  Pallas kernels  149 us (72%)
  matrix products  35.2 us (17%)
  local copies, waits for them, and re-layouts  14.6 us (7%)
  other arithmetic  5.99 us (3%)
    pallas_call x1, Pallas kernels, backward(): pl.pallas_call(functools.partial(backward_kernel, flows, sizes), in_specs...  107 us
    pallas_call x1, Pallas kernels, forward(): pl.pallas_call(functools.partial(forward_kernel, (windows, rows, length,...  42.6 us
    dot_general x4, matrix products, dot_tn(): lax.dot_general(a, b, (((0,), (0,)), ((), ())), preferred_element_type=f32)  12.4 us
    dot_general x5, matrix products, dot(): return jnp.dot(a, b, preferred_element_type=f32)  8.94 us
    dot_general x4, matrix products, dot_nt(): lax.dot_general(a, b, (((1,), (1,)), ((), ())), preferred_element_type=f32)  8.69 us
    unnamed x49, local copies, waits for them, and re-layouts  6.56 us

profile of v5, /device:TPU:0, one launch (start us, length us, event | category | flops | bytes accessed | tf_op | source)
XLA Modules:
  0.0 206.2 jit_solution(12379830184896227321)
XLA Ops:
  0.6 0.0 copy-start
  0.7 0.8 broadcast_multiply_fusion.3
  1.4 0.1 multiply_sine_fusion
  1.6 0.9 reduce-precision_convert_fusion.1
  2.5 1.0 fusion.3.table_ref
  3.5 1.0 copy-done.1
  4.5 1.0 copy-done.2
  5.6 0.7 copy-done.3
  6.2 42.6 %forward.1 = (f32[8,4608]{1,0:T(8,128)S(1)}, bf16[256,768]{1,0:T(8,128)(2,1)S(1)}, bf16[1024,1536]{1,0:T(8,128)(2,1)}, bf16[1024,768]{1,0:T(8,128)(2,1)S(1)}, bf...) custom-call(s32[2]{0:T(128)S(1)} %copy-done.3, ...), custom_call_target="tpu_custom_call" | custom-call | flops 10000000000 | bytes 41943040 | tf_op jit(solution)/shard_map/forward/pallas_call | solution.py:237
  48.9 0.0 copy-start.6
  48.9 0.7 fusion.22
  49.6 0.5 fusion.35
  50.1 0.2 fusion.34
  50.3 0.2 multiply_reduce_fusion.2
  50.5 0.0 slice-start
  50.6 0.2 add_convert_fusion.1
  50.8 1.3 copy-done.15
  52.1 3.0 %fusion.36 = f32[256,3072]{1,0:T(8,128)} fusion(bf16[256,768]{1,0:T(8,128)(2,1)S(1)} %bitcast.97, bf16[768,3072]{1,0:T(8,128)(2,1)S(1)} %copy-done.15), kind=kOutput, calls=%fused_computation.96 | convolution fusion | flops 1207959552 | bytes 8257536 | tf_op jit(solution)/shard_map/dot_general | solution.py:40
  55.1 0.0 slice-done.1
  55.1 0.0 slice-start.3
  55.1 3.1 %fusion.37 = f32[256,3072]{1,0:T(8,128)} fusion(bf16[256,768]{1,0:T(8,128)(2,1)S(1)} %bitcast.98, bf16[768,3072]{1,0:T(8,128)(2,1)S(1)} %bitcast.102), kind=kOutput, calls=%fused_computation.97 | convolution fusion | flops 1207959552 | bytes 8257536 | tf_op jit(solution)/shard_map/dot_general | solution.py:40
  58.2 0.0 copy-done.8
  58.2 0.1 fusion.6
  58.2 0.0 slice-done.2
  58.3 0.0 slice-done.3
  58.3 4.5 %multiply_convert_fusion = (bf16[256,3072]{1,0:T(8,128)(2,1)S(1)}, bf16[256,3072]{1,0:T(8,128)(2,1)S(1)}, bf16[256,3072]{1,0:T(8,128)(2,1)S(1)}) fusion(f32[256,3072]{1,0:T(8,128)} %fusion.36, f32[256,3072]{1,0:T(8,128)} %fusion.37, bf16[256,768]{1,0:T(8,128)(2,1)S(1)} %bitcast.108, bf16[3072,768]{1,0:T(8,128)(2,1)S(1)} %bitcast.125), kind=kOutput, calls=%fused_computation.3 | convolution fusion | flops 1219756032 | bytes 16121856 | tf_op jit(solution)/shard_map/dot_general | solution.py:44
  62.8 1.4 fusion.39
  64.2 1.5 fusion.10
  65.7 0.4 fusion.11
  66.1 1.4 fusion.38
  67.5 1.4 multiply_reduce_fusion
  68.9 3.5 %convolution_convert_fusion.2 = bf16[768,3072]{1,0:T(8,128)(2,1)} fusion(bf16[256,768]{1,0:T(8,128)(2,1)S(1)} %bitcast.99, bf16[256,3072]{1,0:T(8,128)(2,1)S(1)} %get-tuple-element.55), kind=kOutput, calls=%fused_computation.2 | convolution fusion | flops 1210318848 | bytes 6684672 | tf_op jit(solution)/shard_map/dot_general | solution.py:48
  72.4 3.6 %convolution_convert_fusion.1 = bf16[768,3072]{1,0:T(8,128)(2,1)} fusion(bf16[256,768]{1,0:T(8,128)(2,1)S(1)} %bitcast.100, bf16[256,3072]{1,0:T(8,128)(2,1)S(1)} %get-tuple-element.54), kind=kOutput, calls=%fused_computation.1 | convolution fusion | flops 1210318848 | bytes 6684672 | tf_op jit(solution)/shard_map/dot_general | solution.py:48
  76.0 3.7 %convolution_convert_fusion = bf16[3072,768]{1,0:T(8,128)(2,1)} fusion(bf16[256,3072]{1,0:T(8,128)(2,1)S(1)} %get-tuple-element.56, bf16[256,768]{1,0:T(8,128)(2,1)S(1)} %bitcast.109), kind=kOutput, calls=%fused_computation | convolution fusion | flops 1210318848 | bytes 6684672 | tf_op jit(solution)/shard_map/dot_general | solution.py:48
  79.7 0.1 multiply_convert_fusion.3
  79.8 1.5 convolution_convert_fusion.3
  81.3 1.3 convolution_convert_fusion.4.refs_7_
  82.6 0.1 iota_compare_fusion.4
  82.7 1.3 concatenate.14.refs_14_
  83.9 106.8 %backward.1 = (f32[24,3072]{1,0:T(8,128)}, f32[24,3072]{1,0:T(8,128)}, f32[96,768]{1,0:T(8,128)}, f32[24,768]{1,0:T(8,128)}, f32[24,768]{1,0:T(8,128)}, /*index=...) custom-call(bf16[2,2,2,96,3072]{4,3,2,1,0:T(8,128)(2,1)} %bitcast.94, ...), custom_call_target="tpu_custom_call" | custom-call | flops 10000000000 | bytes 209715200 | tf_op jit(solution)/shard_map/backward/pallas_call | solution.py:782
  190.7 1.0 slice.39
  191.7 0.2 reshape.146
  192.0 0.0 copy-start.13
  192.0 0.1 copy.33
  192.1 0.1 copy.35
  192.4 0.2 dynamic-slice_reduce_fusion
  192.5 2.6 %fusion.4 = f32[96]{0:T(128)} fusion(f32[16,4608]{1,0:T(8,128)S(1)} %bitcast.106, bf16[768,4608]{1,0:T(8,128)(2,1)} %ada_hbm.1, s32[]{:T(128)S(6)} %select_n.29, f32[16,768]{1,0:T(8,128)S(1)} %add_divide_fusion.1, f32[16,768]{1,0:T(8,128)S(1)} %reshape_squeeze.6, f32[16]{0:T(128)S(1)} %dynamic-slice_reduce_fusion), kind=kOutput, calls=%fused_computation.22 | convolution fusion | flops 84945312 | bytes 1193408 | tf_op jit(solution)/shard_map/dot_general | solution.py:944
  195.1 0.6 fusion.18
  195.7 0.8 reshape.148
  196.5 0.9 pad_maximum_fusion
  197.4 0.7 reshape.149
  198.1 1.5 reshape.150
  199.6 0.9 slice_reduce_fusion
  200.5 1.0 convolution_bitcast_fusion
  201.5 0.1 copy.36
  201.6 0.6 dynamic_slice.26
  202.2 0.1 convolution_bitcast_fusion.1
  202.3 0.1 copy.32
  202.4 0.1 reshape.152
  202.5 0.6 dynamic_slice.27
  203.1 0.8 copy.37
  203.9 0.8 copy.38
  204.7 0.7 reshape.155
  205.4 0.7 copy.40
  (45 shorter events, 0.3 us)
Async XLA Ops:
  0.6 49.0 %copy-start = (bf16[768,768]{1,0:T(8,128)(2,1)S(1)}, bf16[768,768]{1,0:T(8,128)(2,1)}, u32[]{:S(2)}) copy-start(bf16[768,768]{1,0:T(8,128)(2,1)} %param.24) | copy-start | bytes 3538948
  3.5 1.0 copy-start.1
  4.5 1.0 copy-start.2
  5.6 0.7 copy-start.3
  48.9 1.9 copy-start.4
  48.9 1.9 copy-start.5
  48.9 1.9 copy-start.6
  49.6 2.4 %copy-start.15 = (bf16[768,3072]{1,0:T(8,128)(2,1)S(1)}, bf16[768,3072]{1,0:T(8,128)(2,1)}, u32[]{:S(2)}) copy-start(bf16[768,3072]{1,0:T(8,128)(2,1)} %param.27) | copy-start | bytes 14155780
  50.5 4.5 %slice-start = ((s8[4718592]{0:T(1024)(128)(4,1)}), s8[4194304]{0:T(1024)(128)(4,1)S(1)}, s32[]{:S(2)}) async-start(s8[4718592]{0:T(1024)(128)(4,1)} %bitcast.101), calls=%async_computation | async-start | bytes 8388608
  52.0 3.0 %slice-start.1 = ((s8[4718592]{0:T(1024)(128)(4,1)}), s8[524288]{0:T(1024)(128)(4,1)S(1)}, s32[]{:S(2)}) async-start(s8[4718592]{0:T(1024)(128)(4,1)} %bitcast.101), calls=%async_computation.1 | async-start | bytes 1048576
  52.0 6.2 %slice-start.2 = ((s8[4718592]{0:T(1024)(128)(4,1)}), s8[4194304]{0:T(1024)(128)(4,1)S(1)}, s32[]{:S(2)}) async-start(s8[4718592]{0:T(1024)(128)(4,1)} %bitcast.124), calls=%async_computation.2 | async-start | bytes 8388608
  55.1 3.1 %copy-start.8 = (bf16[2,128,768]{2,1,0:T(8,128)(2,1)S(1)}, bf16[2,128,768]{2,1,0:T(8,128)(2,1)}, u32[]{:S(2)}) copy-start(bf16[2,128,768]{2,1,0:T(8,128)(2,1)} %param.16) | copy-start | bytes 1179652
  55.1 3.2 %slice-start.3 = ((s8[4718592]{0:T(1024)(128)(4,1)}), s8[524288]{0:T(1024)(128)(4,1)S(1)}, s32[]{:S(2)}) async-start(s8[4718592]{0:T(1024)(128)(4,1)} %bitcast.124), calls=%async_computation.3 | async-start | bytes 1048576
  68.9 10.8 %copy-start.7 = (f32[2,128,768]{2,1,0:T(8,128)}, f32[2,128,768]{2,1,0:T(8,128)S(1)}, u32[]{:S(2)}) copy-start(f32[2,128,768]{2,1,0:T(8,128)S(1)} %get-tuple-element.47) | copy-start | bytes 2359300
  79.7 2.9 %copy-start.16 = (s32[2]{0:T(128)S(1)}, s32[2]{0:T(128)}, u32[]{:S(2)}) copy-start(s32[2]{0:T(128)} %param.18) | copy-start | bytes 28
  191.7 4.8 %copy-start.14 = (f32[24,1536]{1,0:T(8,128)S(1)}, f32[24,1536]{1,0:T(8,128)}, u32[]{:S(2)}) copy-start(f32[24,1536]{1,0:T(8,128)} %get-tuple-element.36) | copy-start | bytes 442372
  192.0 10.2 %copy-start.13 = (bf16[128,256]{1,0:T(8,128)(2,1)S(1)}, bf16[128,256]{1,0:T(8,128)(2,1)}, u32[]{:S(2)}) copy-start(bf16[128,256]{1,0:T(8,128)(2,1)} %param.25) | copy-start | bytes 196612
  192.1 11.1 %copy-start.12 = (f32[24,3072]{1,0:T(8,128)S(1)}, f32[24,3072]{1,0:T(8,128)}, u32[]{:S(2)}) copy-start(f32[24,3072]{1,0:T(8,128)} %get-tuple-element.38) | copy-start | bytes 884740
  192.2 11.7 %copy-start.11 = (f32[24,3072]{1,0:T(8,128)S(1)}, f32[24,3072]{1,0:T(8,128)}, u32[]{:S(2)}) copy-start(f32[24,3072]{1,0:T(8,128)} %get-tuple-element.39) | copy-start | bytes 884740
  192.2 12.5 %copy-start.10 = (f32[96,768]{1,0:T(8,128)S(1)}, f32[96,768]{1,0:T(8,128)}, u32[]{:S(2)}) copy-start(f32[96,768]{1,0:T(8,128)} %get-tuple-element.40) | copy-start | bytes 884740
  192.5 12.9 %copy-start.9 = (bf16[256,768]{1,0:T(8,128)(2,1)S(1)}, bf16[256,768]{1,0:T(8,128)(2,1)}, u32[]{:S(2)}) copy-start(bf16[256,768]{1,0:T(8,128)(2,1)} %get-tuple-element.33) | copy-start | bytes 1179652

commit v6 on v5

--- a/solution.py
+++ b/solution.py
@@ -63,7 +63,7 @@
 def forward_kernel(
     sizes,
     facts_ref,
-    tokens_ref,
+    tokens_hbm,
     cond_ref,
     table_ref,
     ada_hbm,
@@ -79,6 +79,7 @@
     ada_ref,
     weight_ref,
     bins_ref,
+    tokens_ref,
     load_sem,
     gathered,
     send_sem,
@@ -92,7 +93,7 @@
     loads = [
         Load(source, target, load_sem.at[at])
         for at, (source, target) in enumerate(
-            [(ada_hbm, ada_ref), (weight_hbm, weight_ref), (bins_hbm, bins_ref)]
+            [(ada_hbm, ada_ref), (weight_hbm, weight_ref), (bins_hbm, bins_ref), (tokens_hbm, tokens_ref)]
         )
     ]
     for load in loads:
@@ -125,7 +126,7 @@
 
                 @pl.when((here + 1 - 2 * way >= 0) & (here + 1 - 2 * way < count))
                 def _(way=way, window=window):
-                    body(copy(way, 0, window, here, tokens_ref.at[window]))
+                    body(copy(way, 0, window, here, tokens_hbm.at[window]))
 
     for_sends(lambda each: each.start())
     loads[0].copy.wait()
@@ -135,6 +136,7 @@
         mod_ref[:, cols] = mod[:8] + mod[8:16] + mod[16:24]
     loads[1].copy.wait()
     loads[2].copy.wait()
+    loads[3].copy.wait()
 
     def project(window, shard, values):
         normed, _ = norm_rows(values.astype(f32))
@@ -233,10 +235,10 @@
     pairs = width // (2 * head_size)
     count = lax.axis_size("seq")
     vmem = pl.BlockSpec(memory_space=pltpu.VMEM)
-    hbm = pl.BlockSpec(memory_space=pl.ANY)
+    hbm = pl.BlockSpec(memory_space=pltpu.HBM)
     return pl.pallas_call(
         functools.partial(forward_kernel, (windows, rows, length, head_size)),
-        in_specs=[pl.BlockSpec(memory_space=pltpu.SMEM), vmem, vmem, vmem, hbm, hbm, hbm],
+        in_specs=[pl.BlockSpec(memory_space=pltpu.SMEM), hbm, vmem, vmem, hbm, hbm, hbm],
         out_specs=[vmem] * 7,
         out_shape=[
             jax.ShapeDtypeStruct((8, ada_weight.shape[1]), f32),
@@ -251,7 +253,8 @@
             pltpu.VMEM(ada_weight.shape, bf16),
             pltpu.VMEM(qkv_weight.shape, bf16),
             pltpu.VMEM(bins.shape, jnp.int32),
-            pltpu.SemaphoreType.DMA((3,)),
+            pltpu.VMEM(tokens.shape, bf16),
+            pltpu.SemaphoreType.DMA((4,)),
             pltpu.VMEM((count, windows, rows, width), bf16),
             pltpu.SemaphoreType.DMA((2, count - 1, windows)),
             pltpu.SemaphoreType.DMA((2, count - 1, windows)),
@@ -519,7 +522,8 @@
 
     grads = take(4)
     sources = take(9)
-    scale_ref, early_ref = take(2)
+    (scale_ref,) = take(1)
+    early_refs = take(6)
     shares = take(6)
     tokens_out, small_out = take(2)
     targets = take(9)
@@ -668,7 +672,7 @@
             second = jnp.mean(dy * normed, axis=-1, keepdims=True)
             back = (dy - first - normed * second) * inv_std
             tokens_out[rows_at, :] = (hidden_ref[rows_at, :] + back).astype(bf16)
-        facts = jnp.concatenate(shift_rows + scale_rows + [early_ref[...]], axis=0)
+        facts = jnp.concatenate(shift_rows + scale_rows + [early[...] for early in early_refs], axis=0)
         small.mine[0, :, :width] = facts
         small.mine[0, :, width:] = table_sum[...]
 
@@ -781,7 +785,7 @@
     ]
     return pl.pallas_call(
         functools.partial(backward_kernel, flows, sizes),
-        in_specs=[pl.BlockSpec(memory_space=pl.ANY)] * (len(grads) + len(loads)) + [vmem] * 2,
+        in_specs=[pl.BlockSpec(memory_space=pl.ANY)] * (len(grads) + len(loads)) + [vmem] * (1 + len(early)),
         out_specs=[vmem] * (len(out_shape) - 1) + [pl.BlockSpec(memory_space=pl.ANY)],
         out_shape=out_shape,
         scratch_shapes=scratch,
@@ -790,7 +794,146 @@
         ),
         cost_estimate=pl.CostEstimate(flops=10**10, bytes_accessed=200 * 2**20, transcendentals=0),
         name="backward",
-    )(*[flow.view(grad) for flow, grad in zip(flows, grads)], *loads, scales, early)
+    )(*[flow.view(grad) for flow, grad in zip(flows, grads)], *loads, scales, *early)
+
+
+def tail_kernel(windows, *refs):
+    gate, up, down, out, q, kv, tokens, small, ada_hbm, pair_table, pair_weight = refs[:11]
+    to_gate, to_up, to_down, to_out, to_qkv, to_tokens, to_class, to_ada, to_table, to_weight = refs[11:21]
+    by_row, cond_t, pre_t, onehot_t, table_flat, weight_rows, padded, ada_rows, cond_grad, ada_sem = refs[21:]
+    width = tokens.shape[1]
+    owner = lax.axis_index("win") * lax.axis_size("seq") + lax.axis_index("seq")
+    share = to_class.shape[1]
+    per_class = width // share
+    column_at = lax.rem(owner, per_class) * share
+    window_at = pl.multiple_of(jnp.minimum(column_at // 16 * 16, width - ada_rows.shape[0]), 16)
+    load_ada = pltpu.make_async_copy(ada_hbm.at[pl.ds(window_at, ada_rows.shape[0]), :], ada_rows, ada_sem)
+    load_ada.start()
+
+    def flatten(target, values, columns, first):
+        rows = values.shape[0]
+        for at in range(values.shape[1] // 128):
+            spot = pl.ds(first // 128 + at, rows, stride=columns // 128)
+            target[spot, :] = values[:, at * 128 : (at + 1) * 128]
+
+    for target, source in ((to_gate, gate), (to_up, up), (to_down, down), (to_out, out)):
+        flatten(target, source, source.shape[1], 0)
+    flatten(to_qkv, q, 3 * width, 0)
+    flatten(to_qkv, kv, 3 * width, width)
+    to_tokens[...] = tokens[...]
+
+    groups = small.shape[0]
+
+    def sort_rows(group, carry):
+        for which in range(8):
+            for window in range(windows):
+                row = small[group, pl.ds(which * windows + window, 1), :width]
+                by_row[pl.ds(window * groups + group, 1), which * width : (which + 1) * width] = row
+        return carry
+
+    lax.fori_loop(0, groups, sort_rows, 0)
+
+    def rows_of(which):
+        return by_row[:, which * width : (which + 1) * width]
+
+    mods = [rows_of(part) for part in range(6)]
+    pre = rows_of(6)
+    cond_t[...] = (pre * jax.nn.sigmoid(pre)).T
+    pre_t[...] = pre.T
+    onehot_t[...] = rows_of(7).T
+    ada_share = width // (lax.axis_size("win") * lax.axis_size("seq"))
+    cond_rows = cond_t[pl.ds(owner * ada_share, ada_share), :]
+    grad_cond = jnp.zeros((ada_rows.shape[0], pre.shape[0]), f32)
+    load_ada.wait()
+    for part, mod in enumerate(mods):
+        product = jnp.dot(cond_rows, mod, precision=highest, preferred_element_type=f32)
+        flatten(to_ada, product, 6 * width, part * width)
+        grad_cond = grad_cond + lax.dot_general(
+            ada_rows[:, part * width : (part + 1) * width].astype(f32),
+            mod,
+            (((1,), (1,)), ((), ())),
+            precision=highest,
+            preferred_element_type=f32,
+        )
+    cond_grad[...] = grad_cond
+    grad_cond = cond_grad[pl.ds(column_at - window_at, share), :]
+    pre_cols = pre_t[pl.ds(column_at, share), :]
+    sig_cols = jax.nn.sigmoid(pre_cols)
+    grad_pre = grad_cond * sig_cols * (1.0 + pre_cols * (1.0 - sig_cols))
+    mine = jnp.broadcast_to(onehot_t[pl.ds(owner // per_class, 1), :], (8, pre.shape[0]))
+    of_class = lax.dot_general(
+        mine, grad_pre, (((1,), (1,)), ((), ())), precision=highest, preferred_element_type=f32
+    )
+    to_class[...] = of_class[:1]
+
+    table = jnp.sum(small[:, :, width:], axis=0)
+    heads = pair_weight.shape[1]
+    padded[...] = jnp.zeros_like(padded)
+    padded[:, :heads] = pair_weight[...].astype(f32)
+    grad_table = lax.dot_general(
+        table.T, padded[...], (((1,), (1,)), ((), ())), precision=highest, preferred_element_type=f32
+    )
+    flatten(table_flat, grad_table, grad_table.shape[1], 0)
+    count = to_table.shape[0]
+    to_table[...] = table_flat[pl.ds(owner * count, count), :]
+    grad_weight = jnp.dot(
+        table, pair_table[...].astype(f32), precision=highest, preferred_element_type=f32
+    )
+    weight_rows[...] = grad_weight.T
+    count = to_weight.shape[1] // heads
+    mine = weight_rows[pl.ds(owner * count, count), :]
+    head = lax.broadcasted_iota(jnp.int32, (16, 128), 0)
+    lane = lax.broadcasted_iota(jnp.int32, (16, 128), 1)
+    spread = jnp.dot(
+        mine,
+        jnp.where(lax.rem(lane, heads) == head, 1.0, 0.0),
+        precision=highest,
+        preferred_element_type=f32,
+    )
+    row = lax.broadcasted_iota(jnp.int32, spread.shape, 0)
+    lane = lax.broadcasted_iota(jnp.int32, spread.shape, 1)
+    spread = jnp.sum(jnp.where(lane // heads == row, spread, 0.0), axis=0, keepdims=True)
+    to_weight[...] = spread[:, : to_weight.shape[1]]
+
+
+def tail(shares, tokens, small, ada_weight, pair_table, pair_weight, windows, class_share):
+    width = tokens.shape[1]
+    devices = lax.axis_size("win") * lax.axis_size("seq")
+    features = pair_table.shape[1]
+    span = class_share if class_share % 16 == 0 else -(-(class_share + 15) // 16) * 16
+    sizes = [share.size for share in shares[:4]] + [shares[4].size + shares[5].size]
+    table_size = pair_table.size // devices
+    ada_size = ada_weight.size // devices
+    every = windows * small.shape[0]
+    vmem = pl.BlockSpec(memory_space=pltpu.VMEM)
+
+    def flat(size):
+        return jax.ShapeDtypeStruct((size // 128, 128), f32)
+
+    return pl.pallas_call(
+        functools.partial(tail_kernel, windows),
+        in_specs=[vmem] * 8 + [pl.BlockSpec(memory_space=pl.ANY)] + [vmem] * 2,
+        out_specs=[vmem] * 10,
+        out_shape=[flat(size) for size in sizes]
+        + [
+            jax.ShapeDtypeStruct(tokens.shape, bf16),
+            jax.ShapeDtypeStruct((1, class_share), f32),
+            flat(ada_size),
+            flat(table_size),
+            jax.ShapeDtypeStruct((1, pair_weight.size // devices), f32),
+        ],
+        scratch_shapes=[pltpu.VMEM((every, 8 * width), f32)]
+        + [pltpu.VMEM((width, every), f32)] * 3
+        + [
+            pltpu.VMEM((pair_table.size // 128, 128), f32),
+            pltpu.VMEM((features, 16), f32),
+            pltpu.VMEM((features, 16), f32),
+            pltpu.VMEM((span, ada_weight.shape[1]), bf16),
+            pltpu.VMEM((span, every), f32),
+            pltpu.SemaphoreType.DMA,
+        ],
+        name="tail",
+    )(*shares, tokens, small, ada_weight, pair_table, pair_weight)
 
 
 def three_parts(values):
@@ -830,7 +973,6 @@
     win_count = lax.axis_size("win")
     seq_count = lax.axis_size("seq")
     devices = win_count * seq_count
-    owner = lax.axis_index("win") * seq_count + lax.axis_index("seq")
     class_onehot = (cath_ids[:, None] == jnp.arange(classes, dtype=jnp.int32)[None, :]).astype(f32)
     pre_cond = jnp.dot(
         class_onehot, class_table.astype(f32), precision=highest
@@ -893,17 +1035,14 @@
     grad_out = dot_tn(attn_mixed, grad_attn_out).astype(bf16)
     grad_mixed = dot_nt(grad_attn_out, out_weight).astype(bf16)
 
-    early = jnp.concatenate(
-        [
-            grad_gate_attn,
-            grad_shift_ffn,
-            grad_scale_ffn,
-            grad_gate_ffn,
-            pre_cond / seq_count,
-            jnp.pad(class_onehot, ((0, 0), (0, width - classes))) / seq_count,
-        ],
-        axis=0,
-    )
+    early = [
+        grad_gate_attn,
+        grad_shift_ffn,
+        grad_scale_ffn,
+        grad_gate_ffn,
+        pre_cond / seq_count,
+        jnp.pad(class_onehot, ((0, 0), (0, width - classes))) / seq_count,
+    ]
     owned_gate, owned_up, owned_down, owned_out, owned_q, owned_kv, grad_tokens, small = backward(
         [grad_gate, grad_up, grad_down, grad_out],
         [
@@ -923,46 +1062,29 @@
         6,
         [False, True, False, True, True, True],
     )
-    grad_tokens = grad_tokens.reshape(windows, row_count, width)
-    rows_all = small[:, :, :width].reshape(win_count, 8, windows, width)
-    mod_all = jnp.swapaxes(rows_all[:, :6], 1, 2).reshape(win_count * windows, 6 * width)
-    table_all = jnp.sum(small[:, :head_count, width : width + table_rows], axis=0).T
-    pre_all = rows_all[:, 6].reshape(win_count * windows, width)
-    onehot_all = rows_all[:, 7].reshape(win_count * windows, width)
-    ada_rows = width // devices
-    sig_all = jax.nn.sigmoid(pre_all)
-    condition_rows = lax.dynamic_slice_in_dim(pre_all * sig_all, owner * ada_rows, ada_rows, 1)
-    owned_ada = lax.dot_general(
-        condition_rows, mod_all, (((0,), (0,)), ((), ())), precision=highest
-    )
     class_share = classes * width // devices
-    per_class = width // class_share
-    column_at = (owner % per_class) * class_share
-    pre_cols = lax.dynamic_slice_in_dim(pre_all, column_at, class_share, 1)
-    sig_cols = lax.dynamic_slice_in_dim(sig_all, column_at, class_share, 1)
-    ada_cols = lax.dynamic_slice_in_dim(ada_weight, column_at, class_share, 0).astype(f32)
-    grad_cond = lax.dot_general(mod_all, ada_cols, (((1,), (1,)), ((), ())), precision=highest)
-    grad_pre = grad_cond * sig_cols * (1.0 + pre_cols * (1.0 - sig_cols))
-    onehot_mine = lax.dynamic_slice_in_dim(onehot_all, owner // per_class, 1, 1)
-    owned_class = jnp.sum(grad_pre * onehot_mine, axis=0)
-    grad_pair_table = jnp.dot(table_all, pair_weight.astype(f32).T, precision=highest).reshape(-1)
-    grad_pair_weight = jnp.dot(pair_table.astype(f32).T, table_all, precision=highest).reshape(-1)
-    table_size = grad_pair_table.shape[0] // devices
-    weight_size = grad_pair_weight.shape[0] // devices
-    owned_pair_table = lax.dynamic_slice_in_dim(grad_pair_table, owner * table_size, table_size)
-    owned_pair_weight = lax.dynamic_slice_in_dim(grad_pair_weight, owner * weight_size, weight_size)
+    flat_gate, flat_up, flat_down, flat_out, flat_qkv, grad_tokens, of_class, flat_ada, of_table, of_weight = tail(
+        [owned_gate, owned_up, owned_down, owned_out, owned_q, owned_kv],
+        grad_tokens,
+        small,
+        ada_weight,
+        pair_table,
+        pair_weight,
+        windows,
+        class_share,
+    )
     return (
         layer_out,
-        grad_tokens,
-        owned_class,
-        owned_ada.reshape(-1),
-        jnp.concatenate([owned_q, owned_kv], axis=-1).reshape(-1),
-        owned_out.reshape(-1),
-        owned_pair_table,
-        owned_pair_weight,
-        owned_gate.reshape(-1),
-        owned_up.reshape(-1),
-        owned_down.reshape(-1),
+        grad_tokens.reshape(windows, row_count, width),
+        of_class.reshape(-1),
+        flat_ada.reshape(-1),
+        flat_qkv.reshape(-1),
+        flat_out.reshape(-1),
+        of_table.reshape(-1),
+        of_weight.reshape(-1),
+        flat_gate.reshape(-1),
+        flat_up.reshape(-1),
+        flat_down.reshape(-1),
     )
 
 

time: 207 us -> 200 us (0.966)
  local copies, waits for them, and re-layouts: 14.6 us -> 4.78 us
  Pallas kernels: 149 us -> 156 us
  matrix products: 35.2 us -> 31.7 us
    pallas_call x0 -> x1, Pallas kernels: none -> 6.34 us  [tail(): pl.pallas_call(functools.partial(tail_kernel, windows), in_specs=[vmem] *...]
    dot_general x4 -> x0, matrix products: 4.26 us -> none  [the longest x1 2.55 us: per_device(): lax.dot_general(mod_all, ada_cols, (((1,), (1,)), ((), ())), precision=hi...]
    reshape x6 -> x0, local copies, waits for them, and re-layouts: 4.09 us -> none  [the longest x1 1.52 us: per_device(): owned_out.reshape(-1)]
    unnamed x49 -> x33, local copies, waits for them, and re-layouts: 6.56 us -> 4.77 us
where the time goes in v6:
time: 200 us; the launch traced here: 199 us
  Pallas kernels  156 us (78%)
  matrix products  31.7 us (16%)
  other arithmetic  6 us (3%)
  local copies, waits for them, and re-layouts  4.78 us (2%)
    pallas_call x1, Pallas kernels, backward(): pl.pallas_call(functools.partial(backward_kernel, flows, sizes), in_specs...  107 us
    pallas_call x1, Pallas kernels, forward(): pl.pallas_call(functools.partial(forward_kernel, (windows, rows, length,...  42.8 us
    dot_general x4, matrix products, dot_tn(): lax.dot_general(a, b, (((0,), (0,)), ((), ())), preferred_element_type=f32)  12.4 us
    dot_general x5, matrix products, dot(): return jnp.dot(a, b, preferred_element_type=f32)  9.08 us
    dot_general x4, matrix products, dot_nt(): lax.dot_general(a, b, (((1,), (1,)), ((), ())), preferred_element_type=f32)  8.69 us
    pallas_call x1, Pallas kernels, tail(): pl.pallas_call(functools.partial(tail_kernel, windows), in_specs=[vmem] *...  6.34 us
    unnamed x33, local copies, waits for them, and re-layouts  4.77 us

profile of v6, /device:TPU:0, one launch (start us, length us, event | category | flops | bytes accessed | tf_op | source)
XLA Modules:
  0.0 199.5 jit_solution(8608574579926464535)
XLA Ops:
  0.6 0.0 copy-start
  0.7 0.8 broadcast_multiply_fusion.3
  1.4 0.1 multiply_sine_fusion
  1.6 1.5 reduce-precision_convert_fusion.1
  3.1 1.0 fusion.1.table_ref
  4.1 0.0 copy-start.1
  4.1 1.0 copy-done.1
  5.1 0.0 copy-start.2
  5.1 1.0 copy-done.2
  6.1 0.0 copy-start.3
  6.1 0.7 copy-done.3
  6.8 42.8 %forward.1 = (f32[8,4608]{1,0:T(8,128)S(1)}, bf16[256,768]{1,0:T(8,128)(2,1)S(1)}, bf16[1024,1536]{1,0:T(8,128)(2,1)}, bf16[1024,768]{1,0:T(8,128)(2,1)S(1)}, bf...) custom-call(s32[2]{0:T(128)S(1)} %copy-done.3, ...), custom_call_target="tpu_custom_call" | custom-call | flops 10000000000 | bytes 41943040 | tf_op jit(solution)/shard_map/forward/pallas_call | solution.py:239
  49.6 0.0 copy-start.4
  49.6 0.0 copy-start.5
  49.6 0.0 copy-start.6
  49.7 0.7 fusion.16
  50.4 0.0 copy-done
  50.4 0.0 copy-start.10
  50.4 0.5 fusion.27
  50.9 0.2 fusion.26
  51.1 0.2 multiply_reduce_fusion.2
  51.3 0.0 slice-start
  51.3 0.2 add_convert_fusion.1
  51.5 0.0 copy-done.4
  51.5 0.0 copy-done.5
  51.6 0.0 copy-done.6
  51.6 1.2 copy-done.10
  52.8 0.0 slice-start.1
  52.8 0.0 slice-start.2
  52.8 3.1 %fusion.28 = f32[256,3072]{1,0:T(8,128)} fusion(bf16[256,768]{1,0:T(8,128)(2,1)S(1)} %bitcast.83, bf16[768,3072]{1,0:T(8,128)(2,1)S(1)} %copy-done.10), kind=kOutput, calls=%fused_computation.79 | convolution fusion | flops 1207959552 | bytes 8257536 | tf_op jit(solution)/shard_map/dot_general | solution.py:40
  55.9 0.0 slice-done
  55.9 0.0 slice-done.1
  55.9 0.0 copy-start.8
  55.9 0.0 slice-start.3
  55.9 3.1 %fusion.29 = f32[256,3072]{1,0:T(8,128)} fusion(bf16[256,768]{1,0:T(8,128)(2,1)S(1)} %bitcast.84, bf16[768,3072]{1,0:T(8,128)(2,1)S(1)} %bitcast.88), kind=kOutput, calls=%fused_computation.80 | convolution fusion | flops 1207959552 | bytes 8257536 | tf_op jit(solution)/shard_map/dot_general | solution.py:40
  59.1 0.0 copy-done.8
  59.1 0.1 fusion.2
  59.2 0.0 slice-done.2
  59.2 0.0 slice-done.3
  59.2 4.5 %multiply_convert_fusion = (bf16[256,3072]{1,0:T(8,128)(2,1)S(1)}, bf16[256,3072]{1,0:T(8,128)(2,1)S(1)}, bf16[256,3072]{1,0:T(8,128)(2,1)S(1)}) fusion(f32[256,3072]{1,0:T(8,128)} %fusion.28, f32[256,3072]{1,0:T(8,128)} %fusion.29, bf16[256,768]{1,0:T(8,128)(2,1)S(1)} %bitcast.92, bf16[3072,768]{1,0:T(8,128)(2,1)S(1)} %bitcast.102), kind=kOutput, calls=%fused_computation.3 | convolution fusion | flops 1219756032 | bytes 16121856 | tf_op jit(solution)/shard_map/dot_general | solution.py:44
  63.7 1.4 fusion.31
  65.1 1.5 fusion.6
  66.6 0.9 fusion.7
  67.6 1.4 fusion.30
  69.0 2.0 %multiply_reduce_fusion = (f32[2,768]{1,0:T(2,128)}, f32[2,128,768]{2,1,0:T(8,128)S(1)}, bf16[2,128,768]{2,1,0:T(8,128)(2,1)}, f32[2,768]{1,0:T(2,128)}) fusion(f32[2,768]{1,0:T(2,128)S(1)} %get-tuple-element.84, f32[2,768]{1,0:T(2,128)S(1)} %bitcast.97, f32[256,768]{1,0:T(8,128)S(1)} %fusion.27, f32[2,128]{1,0:T(2,128)S(1)} %broadcast_multiply_fusion.1, ...), kind=kLoop, calls=%fused_computation.25 | loop fusion | flops 3929088 | bytes 4765696 | tf_op jit(solution)/shard_map/reduce_sum | solution.py:1034
  71.0 0.0 copy-start.7
  71.0 3.6 %convolution_convert_fusion.2 = bf16[768,3072]{1,0:T(8,128)(2,1)} fusion(bf16[256,768]{1,0:T(8,128)(2,1)S(1)} %bitcast.85, bf16[256,3072]{1,0:T(8,128)(2,1)S(1)} %get-tuple-element.75), kind=kOutput, calls=%fused_computation.2 | convolution fusion | flops 1210318848 | bytes 6684672 | tf_op jit(solution)/shard_map/dot_general | solution.py:48
  74.5 3.6 %convolution_convert_fusion.1 = bf16[768,3072]{1,0:T(8,128)(2,1)} fusion(bf16[256,768]{1,0:T(8,128)(2,1)S(1)} %bitcast.86, bf16[256,3072]{1,0:T(8,128)(2,1)S(1)} %get-tuple-element.74), kind=kOutput, calls=%fused_computation.1 | convolution fusion | flops 1210318848 | bytes 6684672 | tf_op jit(solution)/shard_map/dot_general | solution.py:48
  78.2 3.7 %convolution_convert_fusion = bf16[3072,768]{1,0:T(8,128)(2,1)} fusion(bf16[256,3072]{1,0:T(8,128)(2,1)S(1)} %get-tuple-element.76, bf16[256,768]{1,0:T(8,128)(2,1)S(1)} %bitcast.93), kind=kOutput, calls=%fused_computation | convolution fusion | flops 1210318848 | bytes 6684672 | tf_op jit(solution)/shard_map/dot_general | solution.py:48
  81.8 0.0 copy-start.11
  81.8 0.0 copy-done.7
  81.8 0.1 multiply_convert_fusion.3
  81.9 1.6 convolution_convert_fusion.3
  83.5 1.3 convolution_convert_fusion.4.refs_7_
  84.7 0.0 copy-done.11
  84.7 0.1 iota_compare_fusion.4
  84.8 0.6 pad_select_fusion.refs_19_
  85.4 0.0 copy-start.9
  85.4 106.8 %backward.1 = (f32[24,3072]{1,0:T(8,128)}, f32[24,3072]{1,0:T(8,128)}, f32[96,768]{1,0:T(8,128)}, f32[24,768]{1,0:T(8,128)}, f32[24,768]{1,0:T(8,128)}, /*index=...) custom-call(bf16[2,2,2,96,3072]{4,3,2,1,0:T(8,128)(2,1)} %bitcast.80, ...), custom_call_target="tpu_custom_call" | custom-call | flops 10000000000 | bytes 209715200 | tf_op jit(solution)/shard_map/backward/pallas_call | solution.py:786
  192.2 0.0 copy-done.9
  192.2 0.8 copy.26.refs_10_
  193.0 6.3 %tail.1 = (f32[576,128]{1,0:T(8,128)}, f32[576,128]{1,0:T(8,128)}, f32[576,128]{1,0:T(8,128)}, f32[144,128]{1,0:T(8,128)}, f32[432,128]{1,0:T(8,128)}, /*index=5...) custom-call(f32[24,3072]{1,0:T(8,128)} %get-tuple-element.43.refs_0_, ...), custom_call_target="tpu_custom_call" | custom-call | tf_op jit(solution)/shard_map/tail/pallas_call | solution.py:913
  (10 shorter events, 0.1 us)
Async XLA Ops:
  0.6 49.7 %copy-start = (bf16[768,768]{1,0:T(8,128)(2,1)S(1)}, bf16[768,768]{1,0:T(8,128)(2,1)}, u32[]{:S(2)}) copy-start(bf16[768,768]{1,0:T(8,128)(2,1)} %param.24) | copy-start | bytes 3538948
  4.1 1.0 copy-start.1
  5.1 1.0 copy-start.2
  6.1 0.7 copy-start.3
  49.6 1.9 copy-start.4
  49.6 1.9 copy-start.5
  49.6 1.9 copy-start.6
  50.4 2.4 %copy-start.10 = (bf16[768,3072]{1,0:T(8,128)(2,1)S(1)}, bf16[768,3072]{1,0:T(8,128)(2,1)}, u32[]{:S(2)}) copy-start(bf16[768,3072]{1,0:T(8,128)(2,1)} %param.27) | copy-start | bytes 14155780
  51.3 4.6 %slice-start = ((s8[4718592]{0:T(1024)(128)(4,1)}), s8[4194304]{0:T(1024)(128)(4,1)S(1)}, s32[]{:S(2)}) async-start(s8[4718592]{0:T(1024)(128)(4,1)} %bitcast.87), calls=%async_computation | async-start | bytes 8388608
  52.8 3.1 %slice-start.1 = ((s8[4718592]{0:T(1024)(128)(4,1)}), s8[524288]{0:T(1024)(128)(4,1)S(1)}, s32[]{:S(2)}) async-start(s8[4718592]{0:T(1024)(128)(4,1)} %bitcast.87), calls=%async_computation.1 | async-start | bytes 1048576
  52.8 6.3 %slice-start.2 = ((s8[4718592]{0:T(1024)(128)(4,1)}), s8[4194304]{0:T(1024)(128)(4,1)S(1)}, s32[]{:S(2)}) async-start(s8[4718592]{0:T(1024)(128)(4,1)} %bitcast.101), calls=%async_computation.2 | async-start | bytes 8388608
  55.9 3.2 %copy-start.8 = (bf16[2,128,768]{2,1,0:T(8,128)(2,1)S(1)}, bf16[2,128,768]{2,1,0:T(8,128)(2,1)}, u32[]{:S(2)}) copy-start(bf16[2,128,768]{2,1,0:T(8,128)(2,1)} %param.16) | copy-start | bytes 1179652
  55.9 3.2 %slice-start.3 = ((s8[4718592]{0:T(1024)(128)(4,1)}), s8[524288]{0:T(1024)(128)(4,1)S(1)}, s32[]{:S(2)}) async-start(s8[4718592]{0:T(1024)(128)(4,1)} %bitcast.101), calls=%async_computation.3 | async-start | bytes 1048576
  71.0 10.9 %copy-start.7 = (f32[2,128,768]{2,1,0:T(8,128)}, f32[2,128,768]{2,1,0:T(8,128)S(1)}, u32[]{:S(2)}) copy-start(f32[2,128,768]{2,1,0:T(8,128)S(1)} %get-tuple-element.67) | copy-start | bytes 2359300
  81.8 2.9 %copy-start.11 = (s32[2]{0:T(128)S(1)}, s32[2]{0:T(128)}, u32[]{:S(2)}) copy-start(s32[2]{0:T(128)} %param.18) | copy-start | bytes 28
  85.4 106.8 %copy-start.9 = (bf16[256,12]{0,1:T(8,128)(2,1)S(1)}, bf16[256,12]{0,1:T(8,128)(2,1)}, u32[]{:S(2)}) copy-start(bf16[256,12]{0,1:T(8,128)(2,1)} %param.26) | copy-start | bytes 18436

commit v7 on v6

--- a/solution.py
+++ b/solution.py
@@ -12,13 +12,6 @@
 norm_eps = 1e-06
 f32 = jnp.float32
 bf16 = jnp.bfloat16
-
-
-def layer_norm_parts(values):
-    centered = values - jnp.mean(values, axis=-1, keepdims=True)
-    variance = jnp.mean(centered * centered, axis=-1, keepdims=True)
-    inv_std = lax.rsqrt(variance + norm_eps)
-    return (centered * inv_std, inv_std)
 
 
 def norm_back(grad_normed, normed, inv_std):
@@ -260,7 +253,7 @@
             pltpu.SemaphoreType.DMA((2, count - 1, windows)),
         ],
         compiler_params=pltpu.CompilerParams(
-            collective_id=0, has_side_effects=True, vmem_limit_bytes=48 * 2**20
+            collective_id=0, has_side_effects=True, vmem_limit_bytes=63 * 2**20
         ),
         cost_estimate=pl.CostEstimate(flops=10**10, bytes_accessed=40 * 2**20, transcendentals=0),
         name="forward",
@@ -523,7 +516,7 @@
     grads = take(4)
     sources = take(9)
     (scale_ref,) = take(1)
-    early_refs = take(6)
+    early_refs = take(3)
     shares = take(6)
     tokens_out, small_out = take(2)
     targets = take(9)
@@ -936,6 +929,121 @@
     )(*shares, tokens, small, ada_weight, pair_table, pair_weight)
 
 
+def feed_forward_kernel(windows, *refs):
+    mod, tokens, cotangent, mixed, out_weight, gate, up, down = refs[:8]
+    layer_out, grad_hidden_out, grad_mixed, grad_out, sums, grad_gate, grad_up, grad_down = refs[8:16]
+    attn_out, hidden_state, ffn_in, ffn_in_t, grad_ffn, ffn_out, grad_in = refs[16:]
+    total_rows, width = tokens.shape
+    rows = total_rows // windows
+
+    def part(which):
+        cols = slice(which * width, (which + 1) * width)
+        return jnp.concatenate(
+            [jnp.broadcast_to(mod[w : w + 1, cols], (rows, width)) for w in range(windows)], axis=0
+        )
+
+    @pl.when(pl.program_id(0) == 0)
+    def _():
+        projected = dot(mixed[...], out_weight[...])
+        attn_out[...] = projected
+        state = tokens[...].astype(f32) + jax.nn.sigmoid(part(2)) * projected
+        hidden_state[...] = state
+        normed, _ = norm_rows(state)
+        block = (normed * (1.0 + part(4)) + part(3)).astype(bf16)
+        ffn_in[...] = block
+        ffn_in_t[...] = block.T
+        grad_ffn[...] = (jax.nn.sigmoid(part(5)) * cotangent[...].astype(f32)).astype(bf16)
+        ffn_out[...] = jnp.zeros_like(ffn_out)
+        grad_in[...] = jnp.zeros_like(grad_in)
+
+    gate_val = dot(ffn_in[...], gate[...])
+    up_val = dot(ffn_in[...], up[...])
+    gate_sig = jax.nn.sigmoid(gate_val)
+    silu_gate = gate_val * gate_sig
+    ffn_hidden = (silu_gate * up_val).astype(bf16)
+    ffn_out[...] += dot(ffn_hidden, down[...])
+    grad_down[...] = dot(ffn_hidden.T, grad_ffn[...]).astype(bf16)
+    grad_hidden_ffn = dot_nt(grad_ffn[...], down[...])
+    grad_up_val = (grad_hidden_ffn * silu_gate).astype(bf16)
+    grad_gate_val = (
+        grad_hidden_ffn * up_val * gate_sig * (1.0 + gate_val * (1.0 - gate_sig))
+    ).astype(bf16)
+    grad_gate[...] = dot(ffn_in_t[...], grad_gate_val).astype(bf16)
+    grad_up[...] = dot(ffn_in_t[...], grad_up_val).astype(bf16)
+    grad_in[...] += dot_nt(grad_gate_val, gate[...]) + dot_nt(grad_up_val, up[...])
+
+    @pl.when(pl.program_id(0) == pl.num_programs(0) - 1)
+    def _():
+        def window_sums(at, values):
+            for w in range(windows):
+                total = jnp.sum(values[w * rows : (w + 1) * rows], axis=0, keepdims=True)
+                sums[pl.ds(at * windows + w, 1), :] = total
+
+        state = hidden_state[...]
+        sig_f = jax.nn.sigmoid(part(5))
+        grad_layer = cotangent[...].astype(f32)
+        layer_out[...] = (state + sig_f * ffn_out[...]).astype(bf16)
+        window_sums(3, grad_layer * ffn_out[...] * sig_f * (1.0 - sig_f))
+        normed, inv_std = norm_rows(state)
+        window_sums(1, grad_in[...])
+        window_sums(2, grad_in[...] * normed)
+        back = norm_back(grad_in[...] * (1.0 + part(4)), normed, inv_std)
+        grad_hidden = grad_layer + back
+        grad_hidden_out[...] = grad_hidden
+        sig_a = jax.nn.sigmoid(part(2))
+        window_sums(0, grad_hidden * attn_out[...] * sig_a * (1.0 - sig_a))
+        grad_attn_out = (sig_a * grad_hidden).astype(bf16)
+        grad_out[...] = dot(mixed[...].T, grad_attn_out).astype(bf16)
+        grad_mixed[...] = dot_nt(grad_attn_out, out_weight[...]).astype(bf16)
+
+
+def feed_forward(modulation, tokens, cotangent, mixed, out_weight, gate, up, down, windows):
+    total_rows, width = tokens.shape
+    hidden = gate.shape[1]
+    blocks = 6
+    size = hidden // blocks
+
+    def whole(shape):
+        return pl.BlockSpec(shape, lambda j: (0, 0))
+
+    columns = pl.BlockSpec((width, size), lambda j: (0, j))
+    lines = pl.BlockSpec((size, width), lambda j: (j, 0))
+    row = (total_rows, width)
+    return pl.pallas_call(
+        functools.partial(feed_forward_kernel, windows),
+        grid=(blocks,),
+        in_specs=[whole(modulation.shape)]
+        + [whole(row)] * 3
+        + [whole(out_weight.shape), columns, columns, lines],
+        out_specs=[whole(row)] * 3
+        + [whole(out_weight.shape), whole((4 * windows, width)), columns, columns, lines],
+        out_shape=[
+            jax.ShapeDtypeStruct(row, bf16),
+            jax.ShapeDtypeStruct(row, f32),
+            jax.ShapeDtypeStruct(row, bf16),
+            jax.ShapeDtypeStruct(out_weight.shape, bf16),
+            jax.ShapeDtypeStruct((4 * windows, width), f32),
+            jax.ShapeDtypeStruct(gate.shape, bf16),
+            jax.ShapeDtypeStruct(up.shape, bf16),
+            jax.ShapeDtypeStruct(down.shape, bf16),
+        ],
+        scratch_shapes=[
+            pltpu.VMEM(row, f32),
+            pltpu.VMEM(row, f32),
+            pltpu.VMEM(row, bf16),
+            pltpu.VMEM((width, total_rows), bf16),
+            pltpu.VMEM(row, bf16),
+            pltpu.VMEM(row, f32),
+            pltpu.VMEM(row, f32),
+        ],
+        compiler_params=pltpu.CompilerParams(vmem_limit_bytes=63 * 2**20),
+        cost_estimate=pl.CostEstimate(
+            flops=18 * total_rows * width * hidden, bytes_accessed=40 * 2**20, transcendentals=0
+        ),
+        name="ffn",
+    )(modulation, tokens, cotangent, mixed, out_weight, gate, up, down)
+
+
 def three_parts(values):
     parts = []
     for _ in range(3):
@@ -993,53 +1101,21 @@
         distance_bins,
         head_size,
     )
-    modulation = modulation[:windows].reshape(windows, 6, width)
-    shift_attn = modulation[:, 0][:, None, :]
-    scale_attn = modulation[:, 1][:, None, :]
-    gate_attn = modulation[:, 2][:, None, :]
-    shift_ffn = modulation[:, 3][:, None, :]
-    scale_ffn = modulation[:, 4][:, None, :]
-    gate_ffn = modulation[:, 5][:, None, :]
-    tokens_float = tokens.astype(f32)
-    attn_out = dot(attn_mixed, out_weight).reshape(windows, row_count, width)
-    gate_attn_sig = jax.nn.sigmoid(gate_attn)
-    hidden_state = tokens_float + gate_attn_sig * attn_out
-    normed_h, inv_h = layer_norm_parts(hidden_state)
-    ffn_in = (normed_h * (1.0 + scale_ffn) + shift_ffn).astype(bf16).reshape(total_rows, width)
-    gate_val = dot(ffn_in, gate_weight)
-    up_val = dot(ffn_in, up_weight)
-    gate_sig = jax.nn.sigmoid(gate_val)
-    silu_gate = gate_val * gate_sig
-    ffn_hidden = (silu_gate * up_val).astype(bf16)
-    gate_ffn_sig = jax.nn.sigmoid(gate_ffn)
-    grad_layer = cotangent.astype(f32)
-    grad_ffn = (gate_ffn_sig * grad_layer).astype(bf16).reshape(total_rows, width)
-    grad_down = dot_tn(ffn_hidden, grad_ffn).astype(bf16)
-    ffn_out = dot(ffn_hidden, down_weight).reshape(windows, row_count, width)
-    layer_out = (hidden_state + gate_ffn_sig * ffn_out).astype(bf16)
-    grad_gate_ffn = jnp.sum(grad_layer * ffn_out * gate_ffn_sig * (1.0 - gate_ffn_sig), axis=1)
-    grad_hidden_ffn = dot_nt(grad_ffn, down_weight)
-    grad_up_val = (grad_hidden_ffn * silu_gate).astype(bf16)
-    grad_gate_val = (
-        grad_hidden_ffn * up_val * gate_sig * (1.0 + gate_val * (1.0 - gate_sig))
-    ).astype(bf16)
-    grad_gate = dot_tn(ffn_in, grad_gate_val).astype(bf16)
-    grad_up = dot_tn(ffn_in, grad_up_val).astype(bf16)
-    grad_ffn_in = dot_nt(grad_gate_val, gate_weight) + dot_nt(grad_up_val, up_weight)
-    grad_ffn_in = grad_ffn_in.reshape(windows, row_count, width)
-    grad_scale_ffn = jnp.sum(grad_ffn_in * normed_h, axis=1)
-    grad_shift_ffn = jnp.sum(grad_ffn_in, axis=1)
-    grad_hidden = grad_layer + norm_back(grad_ffn_in * (1.0 + scale_ffn), normed_h, inv_h)
-    grad_attn_out = (gate_attn_sig * grad_hidden).astype(bf16).reshape(total_rows, width)
-    grad_gate_attn = jnp.sum(grad_hidden * attn_out * gate_attn_sig * (1.0 - gate_attn_sig), axis=1)
-    grad_out = dot_tn(attn_mixed, grad_attn_out).astype(bf16)
-    grad_mixed = dot_nt(grad_attn_out, out_weight).astype(bf16)
-
+    flat_tokens = tokens.reshape(total_rows, width)
+    layer_out, grad_hidden, grad_mixed, grad_out, sums, grad_gate, grad_up, grad_down = feed_forward(
+        modulation,
+        flat_tokens,
+        cotangent.reshape(total_rows, width),
+        attn_mixed,
+        out_weight,
+        gate_weight,
+        up_weight,
+        down_weight,
+        windows,
+    )
+    scale_attn = modulation[:windows, width : 2 * width]
     early = [
-        grad_gate_attn,
-        grad_shift_ffn,
-        grad_scale_ffn,
-        grad_gate_ffn,
+        sums,
         pre_cond / seq_count,
         jnp.pad(class_onehot, ((0, 0), (0, width - classes))) / seq_count,
     ]
@@ -1053,10 +1129,10 @@
             attn_in_all,
             qkv_weight,
             pair_index,
-            tokens.reshape(total_rows, width),
-            grad_hidden.reshape(total_rows, width),
+            flat_tokens,
+            grad_hidden,
         ],
-        1.0 + scale_attn.reshape(windows, width),
+        1.0 + scale_attn,
         early,
         (windows, row_count, length, head_size),
         6,
@@ -1074,7 +1150,7 @@
         class_share,
     )
     return (
-        layer_out,
+        layer_out.reshape(windows, row_count, width),
         grad_tokens.reshape(windows, row_count, width),
         of_class.reshape(-1),
         flat_ada.reshape(-1),

time: 200 us -> 187 us (0.935)
  matrix products: 31.7 us -> 3.04 us
  Pallas kernels: 156 us -> 179 us
  local copies, waits for them, and re-layouts: 4.78 us -> 0.76 us
  other arithmetic: 6 us -> 2.84 us
    pallas_call x0 -> x1, Pallas kernels: none -> 21.9 us  [feed_forward(): pl.pallas_call(functools.partial(feed_forward_kernel, windows), grid=(blo...]
    dot_general x8 -> x0, matrix products: 21.1 us -> none  [the longest x4 12.4 us: dot_tn(): lax.dot_general(a, b, (((0,), (0,)), ((), ())), preferred_element_type=f32)]
    dot_general x5 -> x1, matrix products: 9.08 us -> 1.6 us  [dot(): return jnp.dot(a, b, preferred_element_type=f32)]
    unnamed x33 -> x7, local copies, waits for them, and re-layouts: 4.77 us -> 0.76 us
    reduce_sum x4 -> x0, other arithmetic: 3.37 us -> none  [the longest x1 2.01 us: per_device(): jnp.sum(grad_hidden * attn_out * gate_attn_sig * (1.0 - gate_attn_sig), a...]
where the time goes in v7:
time: 187 us; the launch traced here: 186 us
  Pallas kernels  179 us (96%)
  matrix products  3.04 us (2%)
  other arithmetic  2.84 us (2%)
    pallas_call x1, Pallas kernels, backward(): pl.pallas_call(functools.partial(backward_kernel, flows, sizes), in_specs...  107 us
    pallas_call x1, Pallas kernels, forward(): pl.pallas_call(functools.partial(forward_kernel, (windows, rows, length,...  44 us
    pallas_call x1, Pallas kernels, feed_forward(): pl.pallas_call(functools.partial(feed_forward_kernel, windows), grid=(blo...  21.9 us
    pallas_call x1, Pallas kernels, tail(): pl.pallas_call(functools.partial(tail_kernel, windows), in_specs=[vmem] *...  6.34 us

profile of v7, /device:TPU:0, one launch (start us, length us, event | category | flops | bytes accessed | tf_op | source)
XLA Modules:
  0.0 186.4 jit_solution(10978504314321088847)
XLA Ops:
  0.6 0.0 copy-start
  0.7 0.7 broadcast_multiply_fusion.1
  1.3 0.1 multiply_sine_fusion
  1.5 0.0 copy-done
  1.5 1.4 reduce-precision_convert_fusion.1
  2.9 0.6 fusion.6.cond_ref
  3.6 1.6 fusion.table_ref
  5.2 44.0 %forward.1 = (f32[8,4608]{1,0:T(8,128)}, bf16[256,768]{1,0:T(8,128)(2,1)}, bf16[1024,1536]{1,0:T(8,128)(2,1)}, bf16[1024,768]{1,0:T(8,128)(2,1)}, bf16[256,768]{...) custom-call(s32[2]{0:T(128)} %facts_ref.1, bf16[2,128,768]{2,1,0:T(8,128)(2,1)} %tokens_hbm.1, ...), custom_call_target="tpu_custom_call" | custom-call | flops 10000000000 | bytes 41943040 | tf_op jit(solution)/shard_map/forward/pallas_call | solution.py:232
  49.2 0.0 copy-start.2
  49.2 21.9 %ffn.1 = (bf16[256,768]{1,0:T(8,128)(2,1)}, f32[256,768]{1,0:T(8,128)}, bf16[256,768]{1,0:T(8,128)(2,1)}, bf16[768,768]{1,0:T(8,128)(2,1)}, f32[8,768]{1,0:T(8,1...) custom-call(f32[8,4608]{1,0:T(8,128)} %get-tuple-element.44.refs_0_, ...), custom_call_target="tpu_custom_call" | custom-call | flops 10871635968 | bytes 41943040 | tf_op jit(solution)/shard_map/ffn/pallas_call | solution.py:1012
  71.1 0.0 copy-done.2
  71.1 0.1 iota_compare_fusion.4
  71.2 1.3 pad_select_fusion
  72.5 0.0 copy-start.1
  72.5 106.7 %backward.1 = (f32[24,3072]{1,0:T(8,128)}, f32[24,3072]{1,0:T(8,128)}, f32[96,768]{1,0:T(8,128)}, f32[24,768]{1,0:T(8,128)}, f32[24,768]{1,0:T(8,128)}, /*index=...) custom-call(bf16[2,2,2,96,3072]{4,3,2,1,0:T(8,128)(2,1)} %bitcast.33, ...), custom_call_target="tpu_custom_call" | custom-call | flops 10000000000 | bytes 209715200 | tf_op jit(solution)/shard_map/backward/pallas_call | solution.py:779
  179.2 0.0 copy-done.1
  179.2 0.7 copy.26.refs_10_
  179.9 6.3 %tail.1 = (f32[576,128]{1,0:T(8,128)}, f32[576,128]{1,0:T(8,128)}, f32[576,128]{1,0:T(8,128)}, f32[144,128]{1,0:T(8,128)}, f32[432,128]{1,0:T(8,128)}, /*index=5...) custom-call(f32[24,3072]{1,0:T(8,128)} %get-tuple-element.59.refs_0_, ...), custom_call_target="tpu_custom_call" | custom-call | tf_op jit(solution)/shard_map/tail/pallas_call | solution.py:906
  (2 shorter events, 0.0 us)
Async XLA Ops:
  0.6 0.8 copy-start
  49.2 21.9 %copy-start.2 = (s32[2]{0:T(128)S(1)}, s32[2]{0:T(128)}, u32[]{:S(2)}) copy-start(s32[2]{0:T(128)} %param.18) | copy-start | bytes 28
  72.5 106.7 %copy-start.1 = (bf16[256,12]{0,1:T(8,128)(2,1)S(1)}, bf16[256,12]{0,1:T(8,128)(2,1)}, u32[]{:S(2)}) copy-start(bf16[256,12]{0,1:T(8,128)(2,1)} %param.26) | copy-start | bytes 18436

commit v8 on v7

--- a/solution.py
+++ b/solution.py
@@ -58,7 +58,8 @@
     facts_ref,
     tokens_hbm,
     cond_ref,
-    table_ref,
+    pair_table,
+    pair_weight,
     ada_hbm,
     weight_hbm,
     bins_hbm,
@@ -73,6 +74,7 @@
     weight_ref,
     bins_ref,
     tokens_ref,
+    table_ref,
     load_sem,
     gathered,
     send_sem,
@@ -122,6 +124,7 @@
                     body(copy(way, 0, window, here, tokens_hbm.at[window]))
 
     for_sends(lambda each: each.start())
+    table_ref[...] = dot_nt(pair_weight[...], pair_table[...]).astype(bf16).astype(f32)
     loads[0].copy.wait()
     for part in range(mod_ref.shape[1] // width):
         cols = slice(part * width, (part + 1) * width)
@@ -222,7 +225,7 @@
     lax.fori_loop(0, (count - 2) * windows * 2, sent, 0)
 
 
-def forward(facts, tokens, cond_parts, table, ada_weight, qkv_weight, bins, head_size):
+def forward(facts, tokens, cond_parts, pair_table, pair_weight, ada_weight, qkv_weight, bins, head_size):
     windows, rows, length = bins.shape
     width = tokens.shape[-1]
     pairs = width // (2 * head_size)
@@ -231,7 +234,7 @@
     hbm = pl.BlockSpec(memory_space=pltpu.HBM)
     return pl.pallas_call(
         functools.partial(forward_kernel, (windows, rows, length, head_size)),
-        in_specs=[pl.BlockSpec(memory_space=pltpu.SMEM), hbm, vmem, vmem, hbm, hbm, hbm],
+        in_specs=[pl.BlockSpec(memory_space=pltpu.SMEM), hbm, vmem, vmem, vmem, hbm, hbm, hbm],
         out_specs=[vmem] * 7,
         out_shape=[
             jax.ShapeDtypeStruct((8, ada_weight.shape[1]), f32),
@@ -247,6 +250,7 @@
             pltpu.VMEM(qkv_weight.shape, bf16),
             pltpu.VMEM(bins.shape, jnp.int32),
             pltpu.VMEM(tokens.shape, bf16),
+            pltpu.VMEM((pair_weight.shape[0], pair_table.shape[0]), f32),
             pltpu.SemaphoreType.DMA((4,)),
             pltpu.VMEM((count, windows, rows, width), bf16),
             pltpu.SemaphoreType.DMA((2, count - 1, windows)),
@@ -257,7 +261,7 @@
         ),
         cost_estimate=pl.CostEstimate(flops=10**10, bytes_accessed=40 * 2**20, transcendentals=0),
         name="forward",
-    )(facts, tokens, cond_parts, table, ada_weight, qkv_weight, bins)
+    )(facts, tokens, cond_parts, pair_table, pair_weight, ada_weight, qkv_weight, bins)
 
 
 def bit_steps():
@@ -860,12 +864,10 @@
     to_class[...] = of_class[:1]
 
     table = jnp.sum(small[:, :, width:], axis=0)
-    heads = pair_weight.shape[1]
+    heads = pair_weight.shape[0]
     padded[...] = jnp.zeros_like(padded)
-    padded[:, :heads] = pair_weight[...].astype(f32)
-    grad_table = lax.dot_general(
-        table.T, padded[...], (((1,), (1,)), ((), ())), precision=highest, preferred_element_type=f32
-    )
+    padded[:heads, :] = pair_weight[...].astype(f32)
+    grad_table = jnp.dot(table.T, padded[...], precision=highest, preferred_element_type=f32)
     flatten(table_flat, grad_table, grad_table.shape[1], 0)
     count = to_table.shape[0]
     to_table[...] = table_flat[pl.ds(owner * count, count), :]
@@ -920,7 +922,7 @@
         + [
             pltpu.VMEM((pair_table.size // 128, 128), f32),
             pltpu.VMEM((features, 16), f32),
-            pltpu.VMEM((features, 16), f32),
+            pltpu.VMEM((16, features), f32),
             pltpu.VMEM((span, ada_weight.shape[1]), bf16),
             pltpu.VMEM((span, every), f32),
             pltpu.SemaphoreType.DMA,
@@ -1000,7 +1002,7 @@
 def feed_forward(modulation, tokens, cotangent, mixed, out_weight, gate, up, down, windows):
     total_rows, width = tokens.shape
     hidden = gate.shape[1]
-    blocks = 6
+    blocks = 3
     size = hidden // blocks
 
     def whole(shape):
@@ -1090,12 +1092,12 @@
     cond_parts = jnp.concatenate(
         [jnp.pad(part, ((0, 8 - windows), (0, 0))) for part in three_parts(condition)], axis=0
     )
-    table_bias = dot(pair_table, pair_weight).astype(bf16)
     modulation, queries, keys_values, attn_in_all, attn_mixed, probs, pair_index = forward(
         chain_start,
         tokens,
         cond_parts,
-        table_bias.astype(f32).T,
+        pair_table,
+        pair_weight.T,
         ada_weight,
         qkv_weight,
         distance_bins,
@@ -1145,7 +1147,7 @@
         small,
         ada_weight,
         pair_table,
-        pair_weight,
+        pair_weight.T,
         windows,
         class_share,
     )

time: 187 us -> 185 us (0.989)
  no operation moved by 1% of the time
where the time goes in v8:
time: 185 us; the launch traced here: 184 us
  Pallas kernels  179 us (97%)
  other arithmetic  3.5 us (2%)
    pallas_call x1, Pallas kernels, backward(): pl.pallas_call(functools.partial(backward_kernel, flows, sizes), in_specs...  107 us
    pallas_call x1, Pallas kernels, forward(): pl.pallas_call(functools.partial(forward_kernel, (windows, rows, length,...  44.1 us
    pallas_call x1, Pallas kernels, feed_forward(): pl.pallas_call(functools.partial(feed_forward_kernel, windows), grid=(blo...  21.5 us
    pallas_call x1, Pallas kernels, tail(): pl.pallas_call(functools.partial(tail_kernel, windows), in_specs=[vmem] *...  6.35 us

profile of v8, /device:TPU:0, one launch (start us, length us, event | category | flops | bytes accessed | tf_op | source)
XLA Modules:
  0.0 184.4 jit_solution(2448764918363437362)
XLA Ops:
  0.6 0.0 copy-start
  0.7 0.7 broadcast_multiply_fusion.1
  1.3 0.7 iota_compare_fusion.4
  2.1 0.1 multiply_sine_fusion
  2.2 0.0 copy-done
  2.2 1.4 reduce-precision_convert_fusion.1
  3.7 0.6 fusion.5.cond_ref
  4.3 44.1 %forward.1 = (f32[8,4608]{1,0:T(8,128)}, bf16[256,768]{1,0:T(8,128)(2,1)}, bf16[1024,1536]{1,0:T(8,128)(2,1)}, bf16[1024,768]{1,0:T(8,128)(2,1)}, bf16[256,768]{...) custom-call(s32[2]{0:T(128)} %facts_ref.1, bf16[2,128,768]{2,1,0:T(8,128)(2,1)} %tokens_hbm.1, ...), custom_call_target="tpu_custom_call" | custom-call | flops 10000000000 | bytes 41943040 | tf_op jit(solution)/shard_map/forward/pallas_call | solution.py:235
  48.4 1.3 pad_select_fusion
  49.7 21.5 %ffn.1 = (bf16[256,768]{1,0:T(8,128)(2,1)}, f32[256,768]{1,0:T(8,128)}, bf16[256,768]{1,0:T(8,128)(2,1)}, bf16[768,768]{1,0:T(8,128)(2,1)}, f32[8,768]{1,0:T(8,1...) custom-call(f32[8,4608]{1,0:T(8,128)} %get-tuple-element.44.refs_0_, ...), custom_call_target="tpu_custom_call" | custom-call | flops 10871635968 | bytes 41943040 | tf_op jit(solution)/shard_map/ffn/pallas_call | solution.py:1014
  71.2 106.7 %backward.1 = (f32[24,3072]{1,0:T(8,128)}, f32[24,3072]{1,0:T(8,128)}, f32[96,768]{1,0:T(8,128)}, f32[24,768]{1,0:T(8,128)}, f32[24,768]{1,0:T(8,128)}, /*index=...) custom-call(bf16[2,2,2,96,3072]{4,3,2,1,0:T(8,128)(2,1)} %bitcast.34, ...), custom_call_target="tpu_custom_call" | custom-call | flops 10000000000 | bytes 209715200 | tf_op jit(solution)/shard_map/backward/pallas_call | solution.py:783
  177.9 6.4 %tail.1 = (f32[576,128]{1,0:T(8,128)}, f32[576,128]{1,0:T(8,128)}, f32[576,128]{1,0:T(8,128)}, f32[144,128]{1,0:T(8,128)}, f32[432,128]{1,0:T(8,128)}, /*index=5...) custom-call(f32[24,3072]{1,0:T(8,128)} %get-tuple-element.59.refs_0_, ...), custom_call_target="tpu_custom_call" | custom-call | tf_op jit(solution)/shard_map/tail/pallas_call | solution.py:908
  (2 shorter events, 0.0 us)
Async XLA Ops:
  0.6 1.6 copy-start

commit v9 on v8

--- a/solution.py
+++ b/solution.py
@@ -692,13 +692,15 @@
     chunks = flows[0].chunks
     stages = flows[0].stages()
     order = [1, 0] + list(range(2, stages))
-    total = max(max(flow.offset for flow in flows) + chunks + stages - 1, max(jobs) + 1)
+    near = len(flows[0].near)
+    lags = list(range(stages - near)) + [stages - near + 1 + 2 * at for at in range(near)]
+    total = max(max(flow.offset for flow in flows) + chunks + lags[-1], max(jobs) + 1)
     table_sum[...] = jnp.zeros_like(table_sum)
 
     def step(at, carry):
         for stage in order:
             for offset in sorted({flow.offset for flow in flows}):
-                chunk = at - stage - offset
+                chunk = at - lags[stage] - offset
 
                 @pl.when((chunk >= 0) & (chunk < chunks))
                 def _(stage=stage, chunk=chunk, offset=offset):

time: 185 us -> 184 us (level)
  no operation moved by 1% of the time
where the time goes in v9:
time: 184 us; the launch traced here: 183 us
  Pallas kernels  178 us (97%)
  other arithmetic  3.5 us (2%)
    pallas_call x1, Pallas kernels, backward(): pl.pallas_call(functools.partial(backward_kernel, flows, sizes), in_specs...  106 us
    pallas_call x1, Pallas kernels, forward(): pl.pallas_call(functools.partial(forward_kernel, (windows, rows, length,...  44.1 us
    pallas_call x1, Pallas kernels, feed_forward(): pl.pallas_call(functools.partial(feed_forward_kernel, windows), grid=(blo...  21.5 us
    pallas_call x1, Pallas kernels, tail(): pl.pallas_call(functools.partial(tail_kernel, windows), in_specs=[vmem] *...  6.35 us

profile of v9, /device:TPU:0, one launch (start us, length us, event | category | flops | bytes accessed | tf_op | source)
XLA Modules:
  0.0 183.3 jit_solution(485758419406606137)
XLA Ops:
  0.6 0.0 copy-start
  0.7 0.7 broadcast_multiply_fusion.1
  1.3 0.7 iota_compare_fusion.4
  2.1 0.1 multiply_sine_fusion
  2.2 0.0 copy-done
  2.2 1.4 reduce-precision_convert_fusion.1
  3.7 0.6 fusion.5.cond_ref
  4.3 44.1 %forward.1 = (f32[8,4608]{1,0:T(8,128)}, bf16[256,768]{1,0:T(8,128)(2,1)}, bf16[1024,1536]{1,0:T(8,128)(2,1)}, bf16[1024,768]{1,0:T(8,128)(2,1)}, bf16[256,768]{...) custom-call(s32[2]{0:T(128)} %facts_ref.1, bf16[2,128,768]{2,1,0:T(8,128)(2,1)} %tokens_hbm.1, ...), custom_call_target="tpu_custom_call" | custom-call | flops 10000000000 | bytes 41943040 | tf_op jit(solution)/shard_map/forward/pallas_call | solution.py:235
  48.4 1.3 pad_select_fusion
  49.7 21.5 %ffn.1 = (bf16[256,768]{1,0:T(8,128)(2,1)}, f32[256,768]{1,0:T(8,128)}, bf16[256,768]{1,0:T(8,128)(2,1)}, bf16[768,768]{1,0:T(8,128)(2,1)}, f32[8,768]{1,0:T(8,1...) custom-call(f32[8,4608]{1,0:T(8,128)} %get-tuple-element.44.refs_0_, ...), custom_call_target="tpu_custom_call" | custom-call | flops 10871635968 | bytes 41943040 | tf_op jit(solution)/shard_map/ffn/pallas_call | solution.py:1016
  71.2 105.6 %backward.1 = (f32[24,3072]{1,0:T(8,128)}, f32[24,3072]{1,0:T(8,128)}, f32[96,768]{1,0:T(8,128)}, f32[24,768]{1,0:T(8,128)}, f32[24,768]{1,0:T(8,128)}, /*index=...) custom-call(bf16[2,2,2,96,3072]{4,3,2,1,0:T(8,128)(2,1)} %bitcast.34, ...), custom_call_target="tpu_custom_call" | custom-call | flops 10000000000 | bytes 209715200 | tf_op jit(solution)/shard_map/backward/pallas_call | solution.py:785
  176.8 6.4 %tail.1 = (f32[576,128]{1,0:T(8,128)}, f32[576,128]{1,0:T(8,128)}, f32[576,128]{1,0:T(8,128)}, f32[144,128]{1,0:T(8,128)}, f32[432,128]{1,0:T(8,128)}, /*index=5...) custom-call(f32[24,3072]{1,0:T(8,128)} %get-tuple-element.59.refs_0_, ...), custom_call_target="tpu_custom_call" | custom-call | tf_op jit(solution)/shard_map/tail/pallas_call | solution.py:910
  (2 shorter events, 0.0 us)
Async XLA Ops:
  0.6 1.6 copy-start
